TPU v7x, 32 devices: a whole 2x2x4 slice. The times are simulated.
32 devices in a mesh: req: 2 (over y), tm: 4 (over z), rows: 2 (over x), sub: 2 (over core).
Axes of the slice: x: 2, y: 2, z: 4, core: 2. Of those that a mesh axis runs over, the one named last changes fastest.
Arguments:
- latents: bfloat16 [32, 256, 640], P('tm', ('req', 'rows')), parts along dimension 1, may hold values from -6 to 6
- cotangent: bfloat16 [32, 256, 640], P('tm', ('req', 'rows')), parts along dimension 1, may hold values from -6 to 6
- w_qkv: bfloat16 [640, 3, 640], P(None, None, 'sub'), may hold values from -0.25 to 0.25
- w_out: bfloat16 [640, 640], P('sub'), may hold values from -0.25 to 0.25
- time_bias: float32 [8, 63], replicated, may hold values from -4 to 310
Outputs:
- grad_latents: bfloat16 [32, 256, 640], P('tm', ('req', 'rows'), 'sub'), parts along dimension 1
- grad_w_qkv: float32 [1280, 3, 640], P(('req', 'tm', 'rows'), None, 'sub'), parts along dimension 0
- grad_w_out_t: float32 [1280, 640], P(('req', 'tm', 'rows'), 'sub'), parts along dimension 0
There are 2 independent parts, one for each index of `req`. A program takes and returns all parts, laid end to end along the dimension named above; an argument that names none is the same for every part. Nothing has to cross between parts.
All inputs are finite; a program needn't handle non-finite values.
Results may differ from a plain program's by a relative error of at most 0.012.
Values may be sent and summed in bfloat16 or wider, within the bound.
No kernel may reach another device: no remote copies, remote signals or barrier semaphores. Data moves between devices by JAX's collectives and lax.ppermute only.
A program may use at most 128 MiB of HBM per device.

v0:
```python
import math

import jax
import jax.numpy as jnp
from jax import lax
from jax.sharding import PartitionSpec as P

H = 8


def positional(frame_pos, channels):
    half = channels // 2
    frequency = jnp.exp(-math.log(10000.0) * jnp.arange(half, dtype=jnp.float32) * 2.0 / channels)
    angles = frame_pos.astype(jnp.float32)[:, None] * frequency[None, :]
    return jnp.concatenate((jnp.sin(angles), jnp.cos(angles)), axis=1)


def bias_table(bias_rows, frames):
    offsets = (
        jnp.arange(frames, dtype=jnp.int32)[:, None]
        - jnp.arange(frames, dtype=jnp.int32)[None, :]
        + frames
        - 1
    )
    return bias_rows[:, offsets]


def embed(latents, frame_pos):
    return (
        latents.astype(jnp.float32) + positional(frame_pos, latents.shape[2])[:, None, :]
    ).astype(jnp.bfloat16)


def project(hidden, w_qkv, cotangent, w_out):
    qkv = jnp.einsum("fsc,ctd->fstd", hidden, w_qkv, preferred_element_type=jnp.float32).astype(
        jnp.bfloat16
    )
    grad_attn = jnp.einsum(
        "fse,de->fsd", cotangent, w_out, preferred_element_type=jnp.float32
    ).astype(jnp.bfloat16)
    return (qkv[:, :, 0], qkv[:, :, 1], qkv[:, :, 2], grad_attn)


def attend(query_rows, key_rows, value_rows, grad_rows, bias_rows, head_count):
    frames, positions, local_width = query_rows.shape
    head_size = local_width // head_count
    inv_root = 1.0 / math.sqrt(head_size)
    shape4 = (frames, positions, head_count, head_size)
    query_heads = query_rows.reshape(shape4)
    key_heads = key_rows.reshape(shape4)
    value_heads = value_rows.reshape(shape4)
    grad_heads = grad_rows.reshape(shape4)
    scores = (
        jnp.einsum("iphd,jphd->phij", query_heads, key_heads, preferred_element_type=jnp.float32)
        * inv_root
        + bias_rows[None]
    )
    row_max = jnp.max(scores, axis=-1, keepdims=True)
    raw_weights = jnp.exp(scores - row_max)
    probs = raw_weights / jnp.sum(raw_weights, axis=-1, keepdims=True)
    probs_low = probs.astype(jnp.bfloat16)
    attn_out = jnp.einsum(
        "phij,jphd->iphd", probs_low, value_heads, preferred_element_type=jnp.float32
    ).astype(jnp.bfloat16)
    grad_probs = jnp.einsum(
        "iphd,jphd->phij", grad_heads, value_heads, preferred_element_type=jnp.float32
    )
    row_dot = jnp.sum(probs * grad_probs, axis=-1, keepdims=True)
    grad_scores = (probs * (grad_probs - row_dot) * inv_root).astype(jnp.bfloat16)
    grad_query = jnp.einsum(
        "phij,jphd->iphd", grad_scores, key_heads, preferred_element_type=jnp.float32
    ).astype(jnp.bfloat16)
    grad_key = jnp.einsum(
        "phij,iphd->jphd", grad_scores, query_heads, preferred_element_type=jnp.float32
    ).astype(jnp.bfloat16)
    grad_value = jnp.einsum(
        "phij,iphd->jphd", probs_low, grad_heads, preferred_element_type=jnp.float32
    ).astype(jnp.bfloat16)
    flat = (frames, positions, local_width)
    return (
        attn_out.reshape(flat),
        grad_query.reshape(flat),
        grad_key.reshape(flat),
        grad_value.reshape(flat),
    )


def latent_grad(grad_qkv, w_qkv, cotangent, head_group):
    local_width = w_qkv.shape[2]
    back_term = jnp.einsum("fstd,ctd->fsc", grad_qkv, w_qkv, preferred_element_type=jnp.float32)
    summed_back = lax.psum_scatter(
        back_term.astype(jnp.bfloat16), "sub", scatter_dimension=2, tiled=True
    ).astype(jnp.float32)
    own_cotangent = lax.dynamic_slice_in_dim(cotangent, head_group * local_width, local_width, 2)
    return (own_cotangent.astype(jnp.float32) + summed_back).astype(jnp.bfloat16)


def per_device(latents, cotangent, w_qkv, w_out, time_bias):
    channels = latents.shape[2]
    local_width = w_qkv.shape[2]
    head_count = H // lax.axis_size("sub")
    head_group = lax.axis_index("sub")
    all_frames = latents.shape[0] * lax.axis_size("tm")
    bias_rows = bias_table(
        lax.dynamic_slice_in_dim(time_bias, head_group * head_count, head_count, 0), all_frames
    )
    frame_pos = lax.axis_index("tm") * latents.shape[0] + jnp.arange(
        latents.shape[0], dtype=jnp.int32
    )
    hidden = embed(latents, frame_pos)
    query_rows, key_rows, value_rows, grad_attn = project(hidden, w_qkv, cotangent, w_out)
    query_rows, key_rows, value_rows, grad_attn = (
        lax.all_to_all(query_rows, "tm", split_axis=1, concat_axis=0, tiled=True),
        lax.all_to_all(key_rows, "tm", split_axis=1, concat_axis=0, tiled=True),
        lax.all_to_all(value_rows, "tm", split_axis=1, concat_axis=0, tiled=True),
        lax.all_to_all(grad_attn, "tm", split_axis=1, concat_axis=0, tiled=True),
    )
    attn_out, grad_query, grad_key, grad_value = attend(
        query_rows, key_rows, value_rows, grad_attn, bias_rows, head_count
    )
    attn_out, grad_query, grad_key, grad_value = (
        lax.all_to_all(attn_out, "tm", split_axis=0, concat_axis=1, tiled=True),
        lax.all_to_all(grad_query, "tm", split_axis=0, concat_axis=1, tiled=True),
        lax.all_to_all(grad_key, "tm", split_axis=0, concat_axis=1, tiled=True),
        lax.all_to_all(grad_value, "tm", split_axis=0, concat_axis=1, tiled=True),
    )
    grad_qkv = jnp.stack((grad_query, grad_key, grad_value), axis=2)
    grad_latents = latent_grad(grad_qkv, w_qkv, cotangent, head_group)
    flat_hidden = hidden.reshape(-1, channels)
    flat_cotangent = cotangent.reshape(-1, channels)
    flat_grads = grad_qkv.reshape(-1, 3 * local_width)
    flat_out = attn_out.reshape(-1, local_width)
    qkv_part = lax.dot_general(
        flat_hidden, flat_grads, (((0,), (0,)), ((), ())), preferred_element_type=jnp.float32
    )
    out_part = lax.dot_general(
        flat_cotangent, flat_out, (((0,), (0,)), ((), ())), preferred_element_type=jnp.float32
    )
    summed_grads = lax.psum_scatter(
        jnp.concatenate((qkv_part, out_part), axis=1),
        ("tm", "rows"),
        scatter_dimension=0,
        tiled=True,
    )
    grad_w_qkv = summed_grads[:, : 3 * local_width].reshape(-1, 3, local_width)
    grad_w_out_t = summed_grads[:, 3 * local_width :]
    return (grad_latents, grad_w_qkv, grad_w_out_t)


def solution(mesh):
    return jax.shard_map(
        per_device,
        mesh=mesh,
        in_specs=(
            P("tm", ("req", "rows"), None),
            P("tm", ("req", "rows"), None),
            P(None, None, "sub"),
            P("sub", None),
            P(),
        ),
        out_specs=(
            P("tm", ("req", "rows"), "sub"),
            P(("req", "tm", "rows"), None, "sub"),
            P(("req", "tm", "rows"), "sub"),
        ),
        check_vma=False,
    )
```

profile of v0, /device:TPU:0, one launch (start us, length us, event | category | flops | bytes accessed | tf_op | source)
XLA Modules:
  0.0 233.2 jit_solution(9928908016868254245)
XLA Ops:
  7.2 1.9 convolution_convert_fusion.5
  10.0 6.3 %all-to-all-start.2 = ((bf16[8,64,320]{2,0,1:T(8,128)(2,1)}), bf16[8,64,320]{2,0,1:T(8,128)(2,1)S(1)}, u32[]{:S(2)}, u32[]{:S(2)}) async-start(bf16[8,64,320]{2,0,1:T(8,128)(2,1)} %copy.49), calls=%async_computation.2 | async-start | bytes 786432 | tf_op jit(solution)/shard_map/all_to_all | solution.py:116
  19.0 9.0 %all-to-all-done.2 = bf16[8,64,320]{2,0,1:T(8,128)(2,1)S(1)} async-done(((bf16[8,64,320]{2,0,1:T(8,128)(2,1)}), bf16[8,64,320]{2,0,1:T(8,128)(2,1)S(1)}, u32[]{:S(2)}, u32[]{:S(2)}) %all-to-all-start.2) | async-done | bytes 327712 | tf_op jit(solution)/shard_map/all_to_all | solution.py:116
  28.1 3.5 %all-to-all-start.3 = ((bf16[8,64,320]{2,0,1:T(8,128)(2,1)}), bf16[8,64,320]{2,0,1:T(8,128)(2,1)S(1)}, u32[]{:S(2)}, u32[]{:S(2)}) async-start(bf16[8,64,320]{2,0,1:T(8,128)(2,1)} %copy.51), calls=%async_computation.3 | async-start | bytes 786432 | tf_op jit(solution)/shard_map/all_to_all | solution.py:115
  32.5 9.9 %all-to-all-done.3 = bf16[8,64,320]{2,0,1:T(8,128)(2,1)S(1)} async-done(((bf16[8,64,320]{2,0,1:T(8,128)(2,1)}), bf16[8,64,320]{2,0,1:T(8,128)(2,1)S(1)}, u32[]{:S(2)}, u32[]{:S(2)}) %all-to-all-start.3) | async-done | bytes 327712 | tf_op jit(solution)/shard_map/all_to_all | solution.py:115
  42.4 3.5 %all-to-all-start.1 = ((bf16[8,64,320]{2,0,1:T(8,128)(2,1)}), bf16[8,64,320]{2,0,1:T(8,128)(2,1)S(1)}, u32[]{:S(2)}, u32[]{:S(2)}) async-start(bf16[8,64,320]{2,0,1:T(8,128)(2,1)} %copy.43), calls=%async_computation.1 | async-start | bytes 786432 | tf_op jit(solution)/shard_map/all_to_all | solution.py:113
  46.8 8.8 %all-to-all-done.1 = bf16[8,64,320]{2,0,1:T(8,128)(2,1)S(1)} async-done(((bf16[8,64,320]{2,0,1:T(8,128)(2,1)}), bf16[8,64,320]{2,0,1:T(8,128)(2,1)S(1)}, u32[]{:S(2)}, u32[]{:S(2)}) %all-to-all-start.1) | async-done | bytes 327712 | tf_op jit(solution)/shard_map/all_to_all | solution.py:113
  55.7 3.5 %all-to-all-start = ((bf16[8,64,320]{2,0,1:T(8,128)(2,1)}), bf16[8,64,320]{2,0,1:T(8,128)(2,1)S(1)}, u32[]{:S(2)}, u32[]{:S(2)}) async-start(bf16[8,64,320]{2,0,1:T(8,128)(2,1)} %copy.41), calls=%async_computation | async-start | bytes 786432 | tf_op jit(solution)/shard_map/all_to_all | solution.py:114
  59.4 4.0 %gather_fusion = f32[1024,4]{1,0:T(8,128)} fusion(f32[4,63]{0,1:T(8,128)S(1)} %copy.80, s32[1024]{0:T(1024)S(1)} %broadcast_clamp_fusion), kind=kCustom, calls=%fused_computation | custom fusion | bytes 36864 | tf_op jit(solution)/shard_map/gather | solution.py:25
  65.5 2.1 reshape.98
  70.4 2.1 fusion.7
  73.8 2.5 %fusion.13 = bf16[32,16,4,80]{3,0,2,1:T(8,128)(2,1)} fusion(bf16[32,16,4,80]{3,2,1,0:T(4,128)(2,1)} %reshape.98, f32[16,4,32]{2,1,0:T(4,128)S(1)} %get-tuple-element.17, f32[16,4,32,32]{2,3,1,0:T(8,128)S(1)} %fusion.7), kind=kOutput, calls=%fused_computation.25 | convolution fusion | flops 10848287 | bytes 925696 | tf_op jit(solution)/shard_map/phij,iphd->jphd/dot_general | solution.py:76
  78.7 5.0 %all-to-all-start.6 = ((bf16[32,16,320]{2,1,0:T(8,128)(2,1)}), bf16[32,16,320]{2,1,0:T(8,128)(2,1)}, u32[]{:S(2)}, u32[]{:S(2)}) async-start(bf16[32,16,320]{2,1,0:T(8,128)(2,1)} %reshape.102), calls=%async_computation.6 | async-start | bytes 786432 | tf_op jit(solution)/shard_map/all_to_all | solution.py:125
  83.7 3.0 %fusion.27 = f32[16,4,32,32]{2,3,1,0:T(8,128)} fusion(bf16[32,16,4,80]{3,2,1,0:T(4,128)(2,1)} %reshape.99, bf16[32,16,4,80]{3,2,1,0:T(4,128)(2,1)} %reshape.98), kind=kOutput, calls=%fused_computation.39 | convolution fusion | flops 10485760 | bytes 917504 | tf_op jit(solution)/shard_map/iphd,jphd->phij/dot_general | solution.py:65
  86.7 3.7 %fusion.12 = bf16[32,16,4,80]{3,0,2,1:T(8,128)(2,1)} fusion(f32[16,4,32,32]{2,3,1,0:T(8,128)} %fusion.27, bf16[32,16,4,80]{3,2,1,0:T(4,128)(2,1)S(1)} %copy-done.3, f32[16,4,32,32]{2,3,1,0:T(8,128)} %get-tuple-element.18, f32[16,4,32]{2,1,0:T(4,128)S(1)} %get-tuple-element.17), kind=kOutput, calls=%fused_computation.24 | convolution fusion | flops 11110431 | bytes 1187840 | tf_op jit(solution)/shard_map/phij,iphd->jphd/dot_general | solution.py:73
  93.0 5.0 %all-to-all-start.5 = ((bf16[32,16,320]{2,1,0:T(8,128)(2,1)}), bf16[32,16,320]{2,1,0:T(8,128)(2,1)}, u32[]{:S(2)}, u32[]{:S(2)}) async-start(bf16[32,16,320]{2,1,0:T(8,128)(2,1)} %reshape.101), calls=%async_computation.5 | async-start | bytes 786432 | tf_op jit(solution)/shard_map/all_to_all | solution.py:124
  98.0 3.9 %fusion.10 = bf16[32,16,4,80]{3,0,2,1:T(8,128)(2,1)} fusion(f32[16,4,32,32]{2,3,1,0:T(8,128)} %fusion.27, bf16[32,16,4,80]{3,2,1,0:T(4,128)(2,1)} %copy-done.2, f32[16,4,32,32]{2,3,1,0:T(8,128)} %get-tuple-element.18, f32[16,4,32]{2,1,0:T(4,128)S(1)} %get-tuple-element.17), kind=kOutput, calls=%fused_computation.22 | convolution fusion | flops 11110431 | bytes 1187840 | tf_op jit(solution)/shard_map/phij,jphd->iphd/dot_general | solution.py:70
  104.3 2.7 %all-to-all-done.5 = bf16[32,16,320]{2,1,0:T(8,128)(2,1)} async-done(((bf16[32,16,320]{2,1,0:T(8,128)(2,1)}), bf16[32,16,320]{2,1,0:T(8,128)(2,1)}, u32[]{:S(2)}, u32[]{:S(2)}) %all-to-all-start.5) | async-done | bytes 327712 | tf_op jit(solution)/shard_map/all_to_all | solution.py:124
  107.0 3.6 %all-to-all-start.4 = ((bf16[32,16,320]{2,1,0:T(8,128)(2,1)}), bf16[32,16,320]{2,1,0:T(8,128)(2,1)S(1)}, u32[]{:S(2)}, u32[]{:S(2)}) async-start(bf16[32,16,320]{2,1,0:T(8,128)(2,1)} %reshape.100), calls=%async_computation.4 | async-start | bytes 786432 | tf_op jit(solution)/shard_map/all_to_all | solution.py:123
  110.7 2.5 %fusion.11 = bf16[32,16,4,80]{3,0,2,1:T(8,128)(2,1)} fusion(bf16[32,16,4,80]{3,2,1,0:T(4,128)(2,1)} %reshape.99, f32[16,4,32]{2,1,0:T(4,128)S(1)} %get-tuple-element.17, f32[16,4,32,32]{2,3,1,0:T(8,128)S(1)} %fusion.7), kind=kOutput, calls=%fused_computation.23 | convolution fusion | flops 10848287 | bytes 925696 | tf_op jit(solution)/shard_map/phij,jphd->iphd/dot_general | solution.py:62
  119.3 4.1 %all-to-all-start.7 = ((bf16[32,16,320]{2,1,0:T(8,128)(2,1)}), bf16[32,16,320]{2,1,0:T(8,128)(2,1)}, u32[]{:S(2)}, u32[]{:S(2)}) async-start(bf16[32,16,320]{2,1,0:T(8,128)(2,1)} %reshape.105), calls=%async_computation.7 | async-start | bytes 786432 | tf_op jit(solution)/shard_map/all_to_all | solution.py:122
  124.3 1.9 fusion.8
  126.2 2.2 copy.76
  128.4 1.6 reshape.122
  130.2 2.2 all-to-all-done.7
  132.4 1.8 copy.69
  135.5 2.3 reshape.104
  137.8 1.7 convolution_bitcast_fusion.1
  140.5 1.9 pad_maximum_fusion
  142.4 4.6 %copy.78 = f32[640,1280]{1,0:T(8,128)} copy(f32[640,1280]{0,1:T(8,128)} %pad_maximum_fusion) | data formatting | bytes 6553600
  149.9 72.6 %reduce-scatter.9.cloned.1.call-done = f32[80,1280]{1,0:T(8,128)} async-done(((f32[640,1280]{1,0:T(8,128)}), f32[80,1280]{1,0:T(8,128)}) %reduce-scatter.9.cloned.1.call-update) | async-done | bytes 409616
  224.7 1.6 slice.26
  (79 shorter events, 33.6 us)
Async XLA Ops:
  7.2 9.6 %copy-start = (bf16[640,3,320]{0,2,1:T(8,128)(2,1)S(1)}, bf16[640,3,320]{0,2,1:T(8,128)(2,1)}, u32[]{:S(2)}) copy-start(bf16[640,3,320]{0,2,1:T(8,128)(2,1)} %param.7) | copy-start | bytes 3686404
  7.2 9.4 %copy-start.11 = (bf16[8,64,640]{2,1,0:T(8,128)(2,1)S(1)}, bf16[8,64,640]{2,1,0:T(8,128)(2,1)}, u32[]{:S(2)}) copy-start(bf16[8,64,640]{2,1,0:T(8,128)(2,1)} %param.5) | copy-start | bytes 1966084
  10.0 18.0 %all-to-all-start.2 = ((bf16[8,64,320]{2,0,1:T(8,128)(2,1)}), bf16[8,64,320]{2,0,1:T(8,128)(2,1)S(1)}, u32[]{:S(2)}, u32[]{:S(2)}) async-start(bf16[8,64,320]{2,0,1:T(8,128)(2,1)} %copy.49), calls=%async_computation.2 | async-start | bytes 786432 | tf_op jit(solution)/shard_map/all_to_all | solution.py:116
  28.1 14.3 %all-to-all-start.3 = ((bf16[8,64,320]{2,0,1:T(8,128)(2,1)}), bf16[8,64,320]{2,0,1:T(8,128)(2,1)S(1)}, u32[]{:S(2)}, u32[]{:S(2)}) async-start(bf16[8,64,320]{2,0,1:T(8,128)(2,1)} %copy.51), calls=%async_computation.3 | async-start | bytes 786432 | tf_op jit(solution)/shard_map/all_to_all | solution.py:115
  32.5 26.7 %copy-start.12 = (f32[8,63]{1,0:T(8,128)S(1)}, f32[8,63]{1,0:T(8,128)}, u32[]{:S(2)}) copy-start(f32[8,63]{1,0:T(8,128)} %param.9) | copy-start | bytes 6052
  42.4 13.3 %all-to-all-start.1 = ((bf16[8,64,320]{2,0,1:T(8,128)(2,1)}), bf16[8,64,320]{2,0,1:T(8,128)(2,1)S(1)}, u32[]{:S(2)}, u32[]{:S(2)}) async-start(bf16[8,64,320]{2,0,1:T(8,128)(2,1)} %copy.43), calls=%async_computation.1 | async-start | bytes 786432 | tf_op jit(solution)/shard_map/all_to_all | solution.py:113
  55.7 14.3 %all-to-all-start = ((bf16[8,64,320]{2,0,1:T(8,128)(2,1)}), bf16[8,64,320]{2,0,1:T(8,128)(2,1)S(1)}, u32[]{:S(2)}, u32[]{:S(2)}) async-start(bf16[8,64,320]{2,0,1:T(8,128)(2,1)} %copy.41), calls=%async_computation | async-start | bytes 786432 | tf_op jit(solution)/shard_map/all_to_all | solution.py:114
  70.4 3.4 %copy-start.2 = (bf16[32,16,4,80]{3,2,1,0:T(4,128)(2,1)}, bf16[32,16,4,80]{3,2,1,0:T(4,128)(2,1)S(1)}, u32[]{:S(2)}) copy-start(bf16[32,16,4,80]{3,2,1,0:T(4,128)(2,1)S(1)} %reshape.96) | copy-start | bytes 983044
  78.7 14.4 %all-to-all-start.6 = ((bf16[32,16,320]{2,1,0:T(8,128)(2,1)}), bf16[32,16,320]{2,1,0:T(8,128)(2,1)}, u32[]{:S(2)}, u32[]{:S(2)}) async-start(bf16[32,16,320]{2,1,0:T(8,128)(2,1)} %reshape.102), calls=%async_computation.6 | async-start | bytes 786432 | tf_op jit(solution)/shard_map/all_to_all | solution.py:125
  83.7 3.0 %copy-start.3 = (bf16[32,16,4,80]{3,2,1,0:T(4,128)(2,1)S(1)}, bf16[32,16,4,80]{3,2,1,0:T(4,128)(2,1)}, u32[]{:S(2)}) copy-start(bf16[32,16,4,80]{3,2,1,0:T(4,128)(2,1)} %reshape.97) | copy-start | bytes 983044
  93.0 14.0 %all-to-all-start.5 = ((bf16[32,16,320]{2,1,0:T(8,128)(2,1)}), bf16[32,16,320]{2,1,0:T(8,128)(2,1)}, u32[]{:S(2)}, u32[]{:S(2)}) async-start(bf16[32,16,320]{2,1,0:T(8,128)(2,1)} %reshape.101), calls=%async_computation.5 | async-start | bytes 786432 | tf_op jit(solution)/shard_map/all_to_all | solution.py:124
  107.0 12.3 %all-to-all-start.4 = ((bf16[32,16,320]{2,1,0:T(8,128)(2,1)}), bf16[32,16,320]{2,1,0:T(8,128)(2,1)S(1)}, u32[]{:S(2)}, u32[]{:S(2)}) async-start(bf16[32,16,320]{2,1,0:T(8,128)(2,1)} %reshape.100), calls=%async_computation.4 | async-start | bytes 786432 | tf_op jit(solution)/shard_map/all_to_all | solution.py:123
  116.6 6.9 %copy-start.5 = (bf16[8,4,16,320]{3,2,1,0:T(8,128)(2,1)}, bf16[8,4,16,320]{3,2,1,0:T(8,128)(2,1)S(1)}, u32[]{:S(2)}) copy-start(bf16[8,4,16,320]{3,2,1,0:T(8,128)(2,1)S(1)} %copy.64) | copy-start | bytes 983044
  117.8 5.7 %copy-start.7 = (bf16[8,4,16,320]{3,2,1,0:T(8,128)(2,1)}, bf16[8,4,16,320]{3,2,1,0:T(8,128)(2,1)S(1)}, u32[]{:S(2)}) copy-start(bf16[8,4,16,320]{3,2,1,0:T(8,128)(2,1)S(1)} %copy.61) | copy-start | bytes 983044
  119.3 13.1 %all-to-all-start.7 = ((bf16[32,16,320]{2,1,0:T(8,128)(2,1)}), bf16[32,16,320]{2,1,0:T(8,128)(2,1)}, u32[]{:S(2)}, u32[]{:S(2)}) async-start(bf16[32,16,320]{2,1,0:T(8,128)(2,1)} %reshape.105), calls=%async_computation.7 | async-start | bytes 786432 | tf_op jit(solution)/shard_map/all_to_all | solution.py:122
  123.5 23.6 %reduce-scatter.7.cloned.1.call-start = ((), (), s32[]{:S(2)}) async-start(), calls=%async_computation.10 | async-start | bytes 983040
  123.6 0.8 copy-start.9
  130.1 4.1 %copy-start.6 = (bf16[8,4,16,320]{3,2,1,0:T(8,128)(2,1)S(1)}, bf16[8,4,16,320]{3,2,1,0:T(8,128)(2,1)}, u32[]{:S(2)}) copy-start(bf16[8,4,16,320]{3,2,1,0:T(8,128)(2,1)} %copy-done.5) | copy-start | bytes 983044
  130.1 4.1 %copy-start.8 = (bf16[8,4,16,320]{3,2,1,0:T(8,128)(2,1)S(1)}, bf16[8,4,16,320]{3,2,1,0:T(8,128)(2,1)}, u32[]{:S(2)}) copy-start(bf16[8,4,16,320]{3,2,1,0:T(8,128)(2,1)} %copy-done.7) | copy-start | bytes 983044
  130.1 4.1 %copy-start.10 = (bf16[8,4,16,320]{3,2,1,0:T(8,128)(2,1)S(1)}, bf16[8,4,16,320]{3,2,1,0:T(8,128)(2,1)}, u32[]{:S(2)}) copy-start(bf16[8,4,16,320]{3,2,1,0:T(8,128)(2,1)} %copy-done.9) | copy-start | bytes 983044
  130.1 92.4 %reduce-scatter.9.cloned.1.call-start = ((), (), s32[]{:S(2)}) async-start(), calls=%async_computation.11 | async-start | bytes 3686400
  137.8 1.8 copy-start.1
  147.0 1.9 copy-start.4
Sparse Core Ops, SparseCore 0:
  130.2 9.4 reduce-scatter.6
  147.2 75.3 reduce-scatter.8
where the time goes:
time: 235 us; the launch traced here: 233 us
  waiting for transfers between devices  107 us (46%)
  local copies, waits for them, and re-layouts  47.2 us (20%)
  starting transfers between devices  34.6 us (15%)
  matrix products  25.4 us (11%)
  between operations  14.4 us (6%)
  other arithmetic  4.71 us (2%)
    unnamed x4, waiting for transfers between devices  72.7 us
    unnamed x34, local copies, waits for them, and re-layouts  12.3 us
    all_to_all x1, waiting for transfers between devices, per_device(): lax.all_to_all(value_rows, 'tm', split_axis=1, concat_axis=0, tiled=True)  9.88 us
    all_to_all x1, waiting for transfers between devices, per_device(): lax.all_to_all(grad_attn, 'tm', split_axis=1, concat_axis=0, tiled=True)  9.01 us
    all_to_all x1, waiting for transfers between devices, per_device(): lax.all_to_all(query_rows, 'tm', split_axis=1, concat_axis=0, tiled=True)  8.82 us
    all_to_all x1, starting transfers between devices, per_device(): lax.all_to_all(grad_attn, 'tm', split_axis=1, concat_axis=0, tiled=True)  6.32 us
    gather x2, local copies, waits for them, and re-layouts, bias_table(): return bias_rows[:, offsets]  5.38 us
    all_to_all x1, starting transfers between devices, per_device(): lax.all_to_all(grad_value, 'tm', split_axis=0, concat_axis=1, tiled=True)  5.05 us
  transfers between devices with their start and end apart: 10, of which 8 were waited for; matrix products, arithmetic and copies ran while one was open for 26% of the time, Pallas kernels for 0%

commit v1 on v0

v1 whole, which is shorter than its diff:
```python
import functools
import math

import jax
import jax.numpy as jnp
from jax import lax
from jax.experimental import pallas as pl
from jax.experimental.pallas import tpu as pltpu
from jax.sharding import PartitionSpec as P

H = 8
VMEM = pl.BlockSpec(memory_space=pltpu.VMEM)
ANY = pl.BlockSpec(memory_space=pl.ANY)
BF16 = jnp.bfloat16
F32 = jnp.float32


def params():
    return pltpu.CompilerParams(vmem_limit_bytes=48 << 20)


def shift_send(array, axis, step):
    size = lax.axis_size(axis)
    return lax.ppermute(array, axis, [(i, (i + step) % size) for i in range(size)])


def dot_nn(a, b):
    return lax.dot_general(a, b, (((1,), (0,)), ((), ())), preferred_element_type=F32)


def dot_nt(a, b):
    return lax.dot_general(a, b, (((1,), (1,)), ((), ())), preferred_element_type=F32)


def dot_tn(a, b):
    return lax.dot_general(a, b, (((0,), (0,)), ((), ())), preferred_element_type=F32)


def positional(frames, channels):
    half = channels // 2
    frequency = jnp.exp(-math.log(10000.0) * jnp.arange(half, dtype=F32) * 2.0 / channels)
    angles = jnp.arange(frames, dtype=jnp.int32).astype(F32)[:, None] * frequency[None, :]
    return jnp.concatenate((jnp.sin(angles), jnp.cos(angles)), axis=1)


def split_kernel(count, width, lat_ref, cot_ref, own_lat, own_cot, *rest):
    sends, sems = rest[: count - 1], rest[count - 1]
    me = lax.axis_index("tm")
    core = lax.axis_index("sub")

    def block(ref, step):
        start = pl.multiple_of(lax.rem(me + step, count) * width, width)
        return ref.at[:, pl.ds(start, width), :]

    def move(ref):
        copies = [
            pltpu.make_async_copy(block(ref, step), sends[step - 1], sems.at[step + 1])
            for step in range(1, count)
        ]
        for copy in copies:
            copy.start()
        for copy in copies:
            copy.wait()

    own = [
        pltpu.make_async_copy(block(lat_ref, 0), own_lat, sems.at[0]),
        pltpu.make_async_copy(block(cot_ref, 0), own_cot, sems.at[1]),
    ]

    @pl.when(core == 0)
    def _():
        move(lat_ref)

    @pl.when(core != 0)
    def _():
        move(cot_ref)

    for copy in own:
        copy.start()
    for copy in own:
        copy.wait()


def split_rows(latents, cotangent, count):
    frames, positions, channels = latents.shape
    width = positions // count
    if width % 16 == 0:
        shape = jax.ShapeDtypeStruct((frames, width, channels), BF16)
        blocks = pl.pallas_call(
            functools.partial(split_kernel, count, width),
            out_shape=[shape] * (count + 1),
            in_specs=[ANY] * 2,
            out_specs=[ANY] * (count + 1),
            scratch_shapes=[pltpu.SemaphoreType.DMA((count + 1,))],
            compiler_params=params(),
            name="split_rows",
        )(latents, cotangent)
    else:
        me = lax.axis_index("tm")
        sent = jnp.where(lax.axis_index("sub") == 0, latents, cotangent)

        def cut(array, step):
            start = lax.rem(me + step, count) * width
            return lax.dynamic_slice_in_dim(array, start, width, 1)

        blocks = [cut(latents, 0), cut(cotangent, 0)] + [cut(sent, k) for k in range(1, count)]
    blocks = [b.reshape(frames * width, channels) for b in blocks]
    return blocks[0], blocks[1], blocks[2:]


def table_kernel(frames, owners, width, bias_ref, table_ref, order_ref):
    heads = bias_ref.shape[0]
    group = table_ref.shape[0]
    lanes = bias_ref.shape[1]
    row = lax.broadcasted_iota(jnp.int32, (group, group), 0)
    col = lax.broadcasted_iota(jnp.int32, (group, group), 1)
    same = lax.div(row, frames) == lax.div(col, frames)
    for h in range(heads):
        spread = jnp.broadcast_to(bias_ref[h : h + 1, :], (group, lanes))
        skewed = pltpu.roll(spread, (1 - frames) % lanes, 1, stride=1, stride_axis=0)
        table_ref[:, h * group : (h + 1) * group] = jnp.where(same, skewed[:, :group], -1e30)
    rows = order_ref.shape[1]
    span = frames // owners

    def source(index):
        place, frame = lax.div(index, frames), lax.rem(index, frames)
        return lax.div(frame, span) * (span * width) + lax.rem(frame, span) * width + place

    here = lax.broadcasted_iota(jnp.int32, (rows, rows), 1)
    there = source(lax.broadcasted_iota(jnp.int32, (rows, 1), 0))
    order_ref[0] = jnp.where(here == there, 1.0, 0.0).astype(BF16)
    here = lax.broadcasted_iota(jnp.int32, (rows, rows), 0)
    there = source(lax.broadcasted_iota(jnp.int32, (1, rows), 1))
    order_ref[1] = jnp.where(here == there, 1.0, 0.0).astype(BF16)


def tables(time_bias, heads, frames, owners, width, group):
    first = lax.axis_index("sub") * heads
    own = jnp.flip(lax.dynamic_slice_in_dim(time_bias, first, heads, 0), 1)
    lanes = -(-max(2 * frames - 1, group) // 128) * 128
    own = jnp.pad(own, ((0, 0), (0, lanes - own.shape[1])))
    rows = frames * width
    return pl.pallas_call(
        functools.partial(table_kernel, frames, owners, width),
        out_shape=[
            jax.ShapeDtypeStruct((group, heads * group), F32),
            jax.ShapeDtypeStruct((2, rows, rows), BF16),
        ],
        in_specs=[VMEM],
        out_specs=[VMEM] * 2,
        compiler_params=params(),
        name="tables",
    )(own)


def main_kernel(frames, owners, sides, block, heads, *refs):
    parts = 2 * owners
    inputs, refs = refs[:parts], refs[parts:]
    pe_ref, table_ref, order_ref, w_qkv_ref, w_out_ref = refs[:5]
    refs = refs[5:]
    split = block % 16 == 0
    weight_outs = 2 * sides if split else 2
    weight_refs, refs = refs[:weight_outs], refs[weight_outs:]
    back_keep, back_send, refs = refs[0], refs[1], refs[2:]
    rows_ref, hidden_ref, cot_ref, q_ref, k_ref, v_ref, g_ref, dqk_ref, dvo_ref, sems = refs

    me = lax.axis_index("tm")
    core = lax.axis_index("sub")
    side = lax.axis_index("rows")
    rows, channels = hidden_ref.shape
    width = q_ref.shape[1]
    size = width // heads
    group = table_ref.shape[0]
    inv_root = 1.0 / math.sqrt(size)

    copies = []
    for step in range(owners):
        owner = lax.rem(me - step + owners, owners)
        for which in range(2):
            kind = which if step == 0 else (core if which == 0 else 1 - core)
            copies.append(
                pltpu.make_async_copy(
                    inputs[2 * step + which], rows_ref.at[kind, owner], sems.at[2 * step + which]
                )
            )
    for copy in copies:
        copy.start()
    for copy in copies:
        copy.wait()

    order = order_ref[0]
    moved = dot_nn(order, rows_ref[0].reshape(rows, channels))
    pe = pe_ref[...]
    for start in range(0, rows, frames):
        hidden_ref[start : start + frames, :] = (moved[start : start + frames, :] + pe).astype(BF16)
    cot_ref[...] = dot_nn(order, rows_ref[1].reshape(rows, channels)).astype(BF16)

    hidden = hidden_ref[...]
    for t, ref in enumerate((q_ref, k_ref, v_ref)):
        ref[...] = dot_nt(hidden, w_qkv_ref[t]).astype(BF16)
    g_ref[...] = dot_nt(cot_ref[...], w_out_ref[...]).astype(BF16)

    lane = lax.broadcasted_iota(jnp.int32, (group, width), 1)
    masks = [(lane >= h * size) & (lane < (h + 1) * size) for h in range(heads)]
    zero = jnp.zeros((group, width), BF16)

    def stack(value):
        return jnp.concatenate([jnp.where(mask, value, zero) for mask in masks], axis=0)

    def flip(value):
        return jnp.concatenate(
            [value[:, h * group : (h + 1) * group].T for h in range(heads)], axis=1
        )

    for start in range(0, rows, group):
        span = slice(start, start + group)
        query, key, value, grad = q_ref[span, :], k_ref[span, :], v_ref[span, :], g_ref[span, :]
        keys, values = stack(key), stack(value)
        scores = dot_nt(query, keys) * inv_root + table_ref[...]
        grad_probs = dot_nt(grad, values)
        low, grad_scores = [], []
        for h in range(heads):
            part = slice(h * group, (h + 1) * group)
            own = scores[:, part]
            raw = jnp.exp(own - jnp.max(own, axis=1, keepdims=True))
            probs = raw / jnp.sum(raw, axis=1, keepdims=True)
            up = grad_probs[:, part]
            row_dot = jnp.sum(probs * up, axis=1, keepdims=True)
            low.append(probs.astype(BF16))
            grad_scores.append((probs * (up - row_dot) * inv_root).astype(BF16))
        low = jnp.concatenate(low, axis=1)
        grad_scores = jnp.concatenate(grad_scores, axis=1)
        attn_out = dot_nn(low, values)
        grad_query = dot_nn(grad_scores, keys)
        grad_key = dot_nn(flip(grad_scores), stack(query))
        grad_value = dot_nn(flip(low), stack(grad))
        dqk_ref[span, :] = jnp.concatenate([grad_query, grad_key], axis=1).astype(BF16)
        dvo_ref[span, :] = jnp.concatenate([grad_value, attn_out], axis=1).astype(BF16)

    def store(full, refs):
        if not split:
            refs[0][...] = full
            return
        for z in range(owners):
            slot = lax.rem(z - me + owners, owners)
            for x in range(sides):
                first = (z * sides + x) * block
                piece = full[first : first + block, :]
                turn = lax.rem(x - side + sides, sides)
                for j in range(sides):

                    @pl.when(turn == j)
                    def _(piece=piece, j=j, slot=slot):
                        refs[j][slot] = piece if j == 0 else piece.astype(BF16)

    half = len(weight_refs) // 2
    grad_vo = dvo_ref[...]
    grad_v, attn_out = grad_vo[:, :width], grad_vo[:, width:]
    store(
        jnp.concatenate([dot_tn(hidden, grad_v), dot_tn(cot_ref[...], attn_out)], axis=1),
        weight_refs[:half],
    )
    grad_qk = dqk_ref[...]
    store(dot_tn(hidden, grad_qk), weight_refs[half:])

    back = (
        dot_nn(grad_qk[:, :width], w_qkv_ref[0])
        + dot_nn(grad_qk[:, width:], w_qkv_ref[1])
        + dot_nn(grad_v, w_qkv_ref[2])
    ).astype(BF16)
    back = dot_nn(order_ref[1], back)
    chunk = rows // owners
    lower, upper = back[:, :width], back[:, width:]
    cot = rows_ref[1].reshape(rows, channels).astype(F32)

    def store_back(own, other, base):
        for z in range(owners):
            slot = lax.rem(z - me + owners, owners)
            span = slice(z * chunk, (z + 1) * chunk)
            back_keep[slot] = own[span, :] + base[span, :]
            back_send[slot] = other[span, :].astype(BF16)

    @pl.when(core == 0)
    def _():
        store_back(lower, upper, cot[:, :width])

    @pl.when(core != 0)
    def _():
        store_back(upper, lower, cot[:, width:])


def attend(inputs, pe, table, order, w_qkv, w_out, frames, owners, sides, heads):
    chunk, channels = inputs[0].shape
    rows = chunk * owners
    width = w_qkv.shape[1]
    block = channels // (owners * sides)
    if block % 16 == 0:
        keep = jax.ShapeDtypeStruct((owners, block, 2 * width), F32)
        send = jax.ShapeDtypeStruct((owners, block, 2 * width), BF16)
        weight_outs = ([keep] + [send] * (sides - 1)) * 2
    else:
        weight_outs = [jax.ShapeDtypeStruct((channels, 2 * width), F32)] * 2
    outs = weight_outs + [
        jax.ShapeDtypeStruct((owners, chunk, width), F32),
        jax.ShapeDtypeStruct((owners, chunk, width), BF16),
    ]
    result = pl.pallas_call(
        functools.partial(main_kernel, frames, owners, sides, block, heads),
        out_shape=outs,
        in_specs=[ANY] * len(inputs) + [VMEM] * 5,
        out_specs=[VMEM] * len(outs),
        scratch_shapes=[
            pltpu.VMEM((2, owners, chunk, channels), BF16),
            pltpu.VMEM((rows, channels), BF16),
            pltpu.VMEM((rows, channels), BF16),
            pltpu.VMEM((rows, width), BF16),
            pltpu.VMEM((rows, width), BF16),
            pltpu.VMEM((rows, width), BF16),
            pltpu.VMEM((rows, width), BF16),
            pltpu.VMEM((rows, 2 * width), BF16),
            pltpu.VMEM((rows, 2 * width), BF16),
            pltpu.SemaphoreType.DMA((2 * owners,)),
        ],
        compiler_params=params(),
        name="attend",
    )(*inputs, pe, table, order, w_qkv, w_out)
    back_keep, back_send = result[-2:]
    weights = []
    for at in range(2):
        if block % 16 == 0:
            part = result[at * sides : (at + 1) * sides]
            weights.append((part[0], list(part[1:])))
        else:
            full = result[at].reshape(owners, sides, block, 2 * width)
            full = jnp.roll(full, (-lax.axis_index("tm"), -lax.axis_index("rows")), (0, 1))
            weights.append((full[:, 0], [full[:, j].astype(BF16) for j in range(1, sides)]))
    return weights, back_keep, back_send


def combine_kernel(keep_ref, *refs):
    owners = keep_ref.shape[0]
    arrived, outs = refs[: len(refs) - owners], refs[len(refs) - owners :]
    for slot in range(owners):
        total = keep_ref[slot]
        for ref in arrived:
            total = total + ref[slot].astype(F32)
        outs[slot][...] = total.astype(outs[slot].dtype)


def combine(keep, arrived, own_dtype):
    owners = keep.shape[0]
    outs = [jax.ShapeDtypeStruct(keep.shape[1:], own_dtype)]
    outs += [jax.ShapeDtypeStruct(keep.shape[1:], BF16)] * (owners - 1)
    result = pl.pallas_call(
        combine_kernel,
        out_shape=outs,
        in_specs=[VMEM] * (1 + len(arrived)),
        out_specs=[VMEM] * owners,
        compiler_params=params(),
        name="combine",
    )(keep, *arrived)
    return result[0], result[1:]


def finish_kernel(count, *refs):
    ins, (w_qkv_ref, w_out_ref) = refs[:-2], refs[-2:]

    def total(parts):
        value = parts[0][...]
        for ref in parts[1:]:
            value = value + ref[...].astype(F32)
        return value

    width = w_out_ref.shape[1]
    value_out, query_key = total(ins[:count]), total(ins[count:])
    w_qkv_ref[0] = query_key[:, :width]
    w_qkv_ref[1] = query_key[:, width:]
    w_qkv_ref[2] = value_out[:, :width]
    w_out_ref[...] = value_out[:, width:]


def finish(value_out, query_key):
    block, width = value_out[0].shape[0], value_out[0].shape[1] // 2
    count = len(value_out)
    w_qkv, w_out = pl.pallas_call(
        functools.partial(finish_kernel, count),
        out_shape=[
            jax.ShapeDtypeStruct((3, block, width), F32),
            jax.ShapeDtypeStruct((block, width), F32),
        ],
        in_specs=[VMEM] * (2 * count),
        out_specs=[VMEM] * 2,
        compiler_params=params(),
        name="finish",
    )(*value_out, *query_key)
    return jnp.transpose(w_qkv, (1, 0, 2)), w_out


def place_kernel(*refs):
    blocks, out_ref, sems = refs[:-2], refs[-2], refs[-1]
    count, width = len(blocks), blocks[0].shape[1]
    me = lax.axis_index("tm")
    copies = []
    for step, ref in enumerate(blocks):
        start = pl.multiple_of(lax.rem(me - step + count, count) * width, width)
        copies.append(
            pltpu.make_async_copy(ref, out_ref.at[:, pl.ds(start, width), :], sems.at[step])
        )
    for copy in copies:
        copy.start()
    for copy in copies:
        copy.wait()


def place(blocks, frames):
    count = len(blocks)
    chunk, channels = blocks[0].shape
    width = chunk // frames
    blocks = [b.reshape(frames, width, channels) for b in blocks]
    if width % 16 == 0:
        return pl.pallas_call(
            place_kernel,
            out_shape=jax.ShapeDtypeStruct((frames, count * width, channels), BF16),
            in_specs=[ANY] * count,
            out_specs=ANY,
            scratch_shapes=[pltpu.SemaphoreType.DMA((count,))],
            compiler_params=params(),
            name="place",
        )(*blocks)
    me = lax.axis_index("tm")
    ordered = jnp.roll(jnp.stack(blocks[::-1]), me + 1, 0)
    return jnp.transpose(ordered, (1, 0, 2, 3)).reshape(frames, count * width, channels)


def per_device(latents, cotangent, w_qkv, w_out, time_bias):
    own_frames, positions, channels = latents.shape
    owners, sides = lax.axis_size("tm"), lax.axis_size("rows")
    frames = own_frames * owners
    heads = H // lax.axis_size("sub")
    width = positions // owners
    group = max(frames, 128)

    own_lat, own_cot, sends = split_rows(latents, cotangent, owners)
    table, order = tables(time_bias, heads, frames, owners, width, group)
    pe = positional(frames, channels)
    inputs = [own_lat, own_cot]
    for step, block in enumerate(sends):
        mine = shift_send(block, "tm", step + 1)
        inputs += [mine, shift_send(mine, "sub", 1)]
    weights, back_keep, back_send = attend(
        inputs,
        pe,
        table,
        order,
        jnp.transpose(w_qkv, (1, 2, 0)),
        w_out,
        frames,
        owners,
        sides,
        heads,
    )

    own_back, back_blocks = combine(back_keep, [shift_send(back_send, "sub", 1)], BF16)
    back_blocks = [own_back] + [
        shift_send(block, "tm", step + 1) for step, block in enumerate(back_blocks)
    ]
    sums = []
    for keep, side_blocks in weights:
        arrived = [shift_send(b, "rows", j + 1) for j, b in enumerate(side_blocks)]
        own, blocks = combine(keep, arrived, F32)
        sums.append([own] + [shift_send(b, "tm", step + 1) for step, b in enumerate(blocks)])
    grad_w_qkv, grad_w_out_t = finish(*sums)
    return (place(back_blocks, own_frames), grad_w_qkv, grad_w_out_t)


def solution(mesh):
    return jax.shard_map(
        per_device,
        mesh=mesh,
        in_specs=(
            P("tm", ("req", "rows"), None),
            P("tm", ("req", "rows"), None),
            P(None, None, "sub"),
            P("sub", None),
            P(),
        ),
        out_specs=(
            P("tm", ("req", "rows"), "sub"),
            P(("req", "tm", "rows"), None, "sub"),
            P(("req", "tm", "rows"), "sub"),
        ),
        check_vma=False,
    )
```

time: 235 us -> 79.5 us (0.34)
  waiting for transfers between devices: 107 us -> 24.7 us
  local copies, waits for them, and re-layouts: 47.2 us -> 3.28 us
  matrix products: 25.4 us -> 0 us
  Pallas kernels: 0 us -> 16.6 us
  between operations: 14.4 us -> 0.77 us
  other arithmetic: 4.71 us -> 0.34 us
    unnamed x4 -> x0, waiting for transfers between devices: 72.7 us -> none
    all_to_all x8 -> x0, starting transfers between devices: 34.5 us -> none  [the longest x1 6.32 us: per_device(): lax.all_to_all(grad_attn, 'tm', split_axis=1, concat_axis=0, tiled=True)]
    all_to_all x8 -> x0, waiting for transfers between devices: 34.3 us -> none  [the longest x1 9.88 us: per_device(): lax.all_to_all(value_rows, 'tm', split_axis=1, concat_axis=0, tiled=True)]
    ppermute x0 -> x18, starting transfers between devices: none -> 33.5 us  [shift_send(): lax.ppermute(array, axis, [(i, (i + step) % size) for i in range(size)])]
    dot_general x11 -> x0, matrix products: 25.4 us -> none  [the longest x1 3.86 us: attend(): jnp.einsum('phij,jphd->iphd', grad_scores, key_heads, preferred_element_t...]
    ppermute x0 -> x18, waiting for transfers between devices: none -> 24.7 us  [shift_send(): lax.ppermute(array, axis, [(i, (i + step) % size) for i in range(size)])]
    pallas_call x0 -> x8, Pallas kernels: none -> 16.6 us  [the longest x1 14.1 us: attend(): pl.pallas_call(functools.partial(main_kernel, frames, owners, sides, bloc...]
    reshape x9 -> x0, local copies, waits for them, and re-layouts: 11.5 us -> none  [the longest x1 2.31 us: per_device(): flat_grads = grad_qkv.reshape(-1, 3 * local_width)]
  transfers between devices with their start and end apart: 10 -> 18, of which waited for: 8 -> 7; matrix products, arithmetic and copies ran while one was open for 26% -> 1% of each run, Pallas kernels for 0% -> 2%
where the time goes in v1:
time: 79.5 us; the launch traced here: 79.2 us
  starting transfers between devices  33.5 us (42%)
  waiting for transfers between devices  24.7 us (31%)
  Pallas kernels  16.6 us (21%)
  local copies, waits for them, and re-layouts  3.28 us (4%)
    ppermute x18, starting transfers between devices, shift_send(): lax.ppermute(array, axis, [(i, (i + step) % size) for i in range(size)])  33.5 us
    ppermute x18, waiting for transfers between devices, shift_send(): lax.ppermute(array, axis, [(i, (i + step) % size) for i in range(size)])  24.7 us
    pallas_call x1, Pallas kernels, attend(): pl.pallas_call(functools.partial(main_kernel, frames, owners, sides, bloc...  14.1 us
    unnamed x10, local copies, waits for them, and re-layouts  3.17 us
  transfers between devices with their start and end apart: 18, of which 7 were waited for; matrix products, arithmetic and copies ran while one was open for 1% of the time, Pallas kernels for 2%

profile of v1, /device:TPU:0, one launch (start us, length us, event | category | flops | bytes accessed | tf_op | source)
XLA Modules:
  0.0 79.2 jit_solution(7804790323072509876)
XLA Ops:
  0.7 1.1 %copy-done.2 = bf16[8,64,640]{2,1,0:T(8,128)(2,1)S(1)} copy-done((bf16[8,64,640]{2,1,0:T(8,128)(2,1)S(1)}, bf16[8,64,640]{2,1,0:T(8,128)(2,1)}, u32[]{:S(2)}) %copy-start.2) | copy-done | bytes 655384
  1.7 1.1 %copy-done.3 = bf16[8,64,640]{2,1,0:T(8,128)(2,1)S(1)} copy-done((bf16[8,64,640]{2,1,0:T(8,128)(2,1)S(1)}, bf16[8,64,640]{2,1,0:T(8,128)(2,1)}, u32[]{:S(2)}) %copy-start.3) | copy-done | bytes 655384
  2.8 0.2 split_rows.1
  3.0 3.1 %collective-permute-start = (bf16[128,640]{1,0:T(8,128)(2,1)S(1)}, bf16[128,640]{1,0:T(8,128)(2,1)S(1)}, u32[]{:S(2)}, u32[]{:S(2)}) collective-permute-start(bf16[128,640]{1,0:T(8,128)(2,1)S(1)} %bitcast.19), channel_id=1, source_target_pairs={{0,4},{4,8},{8,12},{12,0},{1,5},{5,9},{9,13},{13,1},{2,6},{6,10},{... | collective-permute-start | bytes 491528 | tf_op jit(solution)/shard_map/ppermute | solution.py:24
  6.1 2.6 %collective-permute-start.2 = (bf16[128,640]{1,0:T(8,128)(2,1)S(1)}, bf16[128,640]{1,0:T(8,128)(2,1)S(1)}, u32[]{:S(2)}, u32[]{:S(2)}) collective-permute-start(bf16[128,640]{1,0:T(8,128)(2,1)S(1)} %bitcast.18), channel_id=1, source_target_pairs={{0,8},{4,12},{8,0},{12,4},{1,9},{5,13},{9,1},{13,5},{2,10},{6,14},... | collective-permute-start | bytes 491528 | tf_op jit(solution)/shard_map/ppermute | solution.py:24
  8.7 1.3 %collective-permute-start.4 = (bf16[128,640]{1,0:T(8,128)(2,1)S(1)}, bf16[128,640]{1,0:T(8,128)(2,1)S(1)}, u32[]{:S(2)}, u32[]{:S(2)}) collective-permute-start(bf16[128,640]{1,0:T(8,128)(2,1)S(1)} %bitcast.17), channel_id=1, source_target_pairs={{0,12},{4,0},{8,4},{12,8},{1,13},{5,1},{9,5},{13,9},{2,14},{6,2},{... | collective-permute-start | bytes 491528 | tf_op jit(solution)/shard_map/ppermute | solution.py:24
  10.1 0.3 multiply_sine_fusion
  10.3 2.9 %collective-permute-done.refs_2_ = bf16[128,640]{1,0:T(8,128)(2,1)S(1)} collective-permute-done((bf16[128,640]{1,0:T(8,128)(2,1)S(1)}, bf16[128,640]{1,0:T(8,128)(2,1)S(1)}, u32[]{:S(2)}, u32[]{:S(2)}) %collective-permute-start) | collective-permute-done | bytes 163872 | tf_op jit(solution)/shard_map/ppermute | solution.py:24
  13.3 6.2 %collective-permute-done.2.refs_4_ = bf16[128,640]{1,0:T(8,128)(2,1)S(1)} collective-permute-done((bf16[128,640]{1,0:T(8,128)(2,1)S(1)}, bf16[128,640]{1,0:T(8,128)(2,1)S(1)}, u32[]{:S(2)}, u32[]{:S(2)}) %collective-permute-start.2) | collective-permute-done | bytes 163872 | tf_op jit(solution)/shard_map/ppermute | solution.py:24
  19.4 0.5 collective-permute-start.5
  20.0 0.1 rev.4
  20.1 0.5 tables.1
  20.6 1.0 %copy-done.1 = bf16[2,512,512]{2,1,0:T(8,128)(2,1)} copy-done((bf16[2,512,512]{2,1,0:T(8,128)(2,1)}, bf16[2,512,512]{2,1,0:T(8,128)(2,1)S(1)}, u32[]{:S(2)}) %copy-start.1) | copy-done | bytes 1048600
  21.5 0.1 pad_maximum_fusion.refs_8_
  21.7 14.1 %attend.1 = (f32[4,80,640]{2,1,0:T(8,128)S(1)}, bf16[4,80,640]{2,1,0:T(8,128)(2,1)S(1)}, f32[4,80,640]{2,1,0:T(8,128)S(1)}, bf16[4,80,640]{2,1,0:T(8,128)(2,1)S(...) custom-call(bf16[128,640]{1,0:T(8,128)(2,1)S(1)} %bitcast.11, bf16[128,640]{1,0:T(8,128)(2,1)S(1)} %bitcast.12, ...), custom_call_target="tpu_custom_call" | custom-call | tf_op jit(solution)/shard_map/attend/pallas_call | solution.py:307
  35.7 1.6 %collective-permute-start.10 = (bf16[4,80,640]{2,1,0:T(8,128)(2,1)S(1)}, bf16[4,80,640]{2,1,0:T(8,128)(2,1)S(1)}, u32[]{:S(2)}, u32[]{:S(2)}) collective-permute-start(bf16[4,80,640]{2,1,0:T(8,128)(2,1)S(1)} %get-tuple-element.44), channel_id=1, source_target_pairs={{0,2},{2,0},{1,3},{3,1},{4,6},{6,4},{5,7},{7,5},{8,10},{10,8},{9,1... | collective-permute-start | bytes 1228808 | tf_op jit(solution)/shard_map/ppermute | solution.py:24
  37.3 0.5 collective-permute-start.14
  37.8 10.3 %collective-permute-done.10.refs_0_ = bf16[4,80,640]{2,1,0:T(8,128)(2,1)S(1)} collective-permute-done((bf16[4,80,640]{2,1,0:T(8,128)(2,1)S(1)}, bf16[4,80,640]{2,1,0:T(8,128)(2,1)S(1)}, u32[]{:S(2)}, u32[]{:S(2)}) %collective-permute-start.10) | collective-permute-done | bytes 409632 | tf_op jit(solution)/shard_map/ppermute | solution.py:24
  48.2 3.5 %collective-permute-start.11 = (bf16[80,640]{1,0:T(8,128)(2,1)S(1)}, bf16[80,640]{1,0:T(8,128)(2,1)S(1)}, u32[]{:S(2)}, u32[]{:S(2)}) collective-permute-start(bf16[80,640]{1,0:T(8,128)(2,1)S(1)} %get-tuple-element.46), channel_id=1, source_target_pairs={{0,4},{4,8},{8,12},{12,0},{1,5},{5,9},{9,13},{13,1},{2,6},{6,10},{... | collective-permute-start | bytes 307208 | tf_op jit(solution)/shard_map/ppermute | solution.py:24
  51.7 0.1 collective-permute-start.7
  51.8 2.2 %collective-permute-start.8 = (bf16[128,320]{1,0:T(8,128)(2,1)S(1)}, bf16[128,320]{1,0:T(8,128)(2,1)S(1)}, u32[]{:S(2)}, u32[]{:S(2)}) collective-permute-start(bf16[128,320]{1,0:T(8,128)(2,1)S(1)} %get-tuple-element.41), channel_id=1, source_target_pairs={{0,8},{4,12},{8,0},{12,4},{1,9},{5,13},{9,1},{13,5},{2,10},{6,14},... | collective-permute-start | bytes 245768 | tf_op jit(solution)/shard_map/ppermute | solution.py:24
  54.1 2.8 %collective-permute-start.9 = (bf16[128,320]{1,0:T(8,128)(2,1)S(1)}, bf16[128,320]{1,0:T(8,128)(2,1)S(1)}, u32[]{:S(2)}, u32[]{:S(2)}) collective-permute-start(bf16[128,320]{1,0:T(8,128)(2,1)S(1)} %get-tuple-element.42), channel_id=1, source_target_pairs={{0,12},{4,0},{8,4},{12,8},{1,13},{5,1},{9,5},{13,9},{2,14},{6,2},{... | collective-permute-start | bytes 245768 | tf_op jit(solution)/shard_map/ppermute | solution.py:24
  56.9 2.1 %collective-permute-start.12 = (bf16[80,640]{1,0:T(8,128)(2,1)S(1)}, bf16[80,640]{1,0:T(8,128)(2,1)S(1)}, u32[]{:S(2)}, u32[]{:S(2)}) collective-permute-start(bf16[80,640]{1,0:T(8,128)(2,1)S(1)} %get-tuple-element.47), channel_id=1, source_target_pairs={{0,8},{4,12},{8,0},{12,4},{1,9},{5,13},{9,1},{13,5},{2,10},{6,14},... | collective-permute-start | bytes 307208 | tf_op jit(solution)/shard_map/ppermute | solution.py:24
  59.0 0.3 collective-permute-done.7
  59.4 3.1 %collective-permute-start.13 = (bf16[80,640]{1,0:T(8,128)(2,1)S(1)}, bf16[80,640]{1,0:T(8,128)(2,1)S(1)}, u32[]{:S(2)}, u32[]{:S(2)}) collective-permute-start(bf16[80,640]{1,0:T(8,128)(2,1)S(1)} %get-tuple-element.48), channel_id=1, source_target_pairs={{0,12},{4,0},{8,4},{12,8},{1,13},{5,1},{9,5},{13,9},{2,14},{6,2},{... | collective-permute-start | bytes 307208 | tf_op jit(solution)/shard_map/ppermute | solution.py:24
  62.5 6.7 %collective-permute-start.15 = (bf16[80,640]{1,0:T(8,128)(2,1)S(1)}, bf16[80,640]{1,0:T(8,128)(2,1)S(1)}, u32[]{:S(2)}, u32[]{:S(2)}) collective-permute-start(bf16[80,640]{1,0:T(8,128)(2,1)S(1)} %get-tuple-element.52), channel_id=1, source_target_pairs={{0,4},{4,8},{8,12},{12,0},{1,5},{5,9},{9,13},{13,1},{2,6},{6,10},{... | collective-permute-start | bytes 307208 | tf_op jit(solution)/shard_map/ppermute | solution.py:24
  69.2 3.4 %collective-permute-start.16 = (bf16[80,640]{1,0:T(8,128)(2,1)S(1)}, bf16[80,640]{1,0:T(8,128)(2,1)S(1)}, u32[]{:S(2)}, u32[]{:S(2)}) collective-permute-start(bf16[80,640]{1,0:T(8,128)(2,1)S(1)} %get-tuple-element.53), channel_id=1, source_target_pairs={{0,8},{4,12},{8,0},{12,4},{1,9},{5,13},{9,1},{13,5},{2,10},{6,14},... | collective-permute-start | bytes 307208 | tf_op jit(solution)/shard_map/ppermute | solution.py:24
  72.6 0.8 place.1
  73.4 1.4 %collective-permute-done.15.refs_5_ = bf16[80,640]{1,0:T(8,128)(2,1)S(1)} collective-permute-done((bf16[80,640]{1,0:T(8,128)(2,1)S(1)}, bf16[80,640]{1,0:T(8,128)(2,1)S(1)}, u32[]{:S(2)}, u32[]{:S(2)}) %collective-permute-start.15) | collective-permute-done | bytes 102432 | tf_op jit(solution)/shard_map/ppermute | solution.py:24
  74.8 3.4 %collective-permute-done.16.refs_6_ = bf16[80,640]{1,0:T(8,128)(2,1)S(1)} collective-permute-done((bf16[80,640]{1,0:T(8,128)(2,1)S(1)}, bf16[80,640]{1,0:T(8,128)(2,1)S(1)}, u32[]{:S(2)}, u32[]{:S(2)}) %collective-permute-start.16) | collective-permute-done | bytes 102432 | tf_op jit(solution)/shard_map/ppermute | solution.py:24
  78.1 0.2 collective-permute-done.17.refs_7_
  78.3 0.9 %finish.1 = (f32[3,80,320]{2,1,0:T(8,128)}, f32[80,320]{1,0:T(8,128)}) custom-call(f32[80,640]{1,0:T(8,128)S(1)} %get-tuple-element.45.refs_0_, bf16[80,640]{1,0:T(8,128)(2,1)S(1)} %collective-permute-done.11.refs_1_, bf16[80,640]{1,0:T(8,128)(2,1)S(1)} %collective-permute-done.12.refs_2_, bf16[80,640]{1,0:T(8,128)(2,1)S(1)} %collective-permute-done.13.refs_3_, ...), custom_call_target="tpu_custom_call" | custom-call | tf_op jit(solution)/shard_map/finish/pallas_call | solution.py:385
  (29 shorter events, 0.3 us)
Async XLA Ops:
  0.6 19.3 %copy-start = (f32[8,63]{1,0:T(8,128)S(1)}, f32[8,63]{1,0:T(8,128)}, u32[]{:S(2)}) copy-start(f32[8,63]{1,0:T(8,128)} %param.9) | copy-start | bytes 6052
  0.6 1.1 %copy-start.2 = (bf16[8,64,640]{2,1,0:T(8,128)(2,1)S(1)}, bf16[8,64,640]{2,1,0:T(8,128)(2,1)}, u32[]{:S(2)}) copy-start(bf16[8,64,640]{2,1,0:T(8,128)(2,1)} %lat_ref.1) | copy-start | bytes 1966084
  1.7 1.1 %copy-start.3 = (bf16[8,64,640]{2,1,0:T(8,128)(2,1)S(1)}, bf16[8,64,640]{2,1,0:T(8,128)(2,1)}, u32[]{:S(2)}) copy-start(bf16[8,64,640]{2,1,0:T(8,128)(2,1)} %cot_ref.1) | copy-start | bytes 1966084
  2.8 18.8 %copy-start.4 = (bf16[320,640]{1,0:T(8,128)(2,1)S(1)}, bf16[320,640]{1,0:T(8,128)(2,1)}, u32[]{:S(2)}) copy-start(bf16[320,640]{1,0:T(8,128)(2,1)} %refs_12_.1) | copy-start | bytes 1228804
  3.0 10.2 %collective-permute-start = (bf16[128,640]{1,0:T(8,128)(2,1)S(1)}, bf16[128,640]{1,0:T(8,128)(2,1)S(1)}, u32[]{:S(2)}, u32[]{:S(2)}) collective-permute-start(bf16[128,640]{1,0:T(8,128)(2,1)S(1)} %bitcast.19), channel_id=1, source_target_pairs={{0,4},{4,8},{8,12},{12,0},{1,5},{5,9},{9,13},{13,1},{2,6},{6,10},{... | collective-permute-start | bytes 491528 | tf_op jit(solution)/shard_map/ppermute | solution.py:24
  6.1 13.3 %collective-permute-start.2 = (bf16[128,640]{1,0:T(8,128)(2,1)S(1)}, bf16[128,640]{1,0:T(8,128)(2,1)S(1)}, u32[]{:S(2)}, u32[]{:S(2)}) collective-permute-start(bf16[128,640]{1,0:T(8,128)(2,1)S(1)} %bitcast.18), channel_id=1, source_target_pairs={{0,8},{4,12},{8,0},{12,4},{1,9},{5,13},{9,1},{13,5},{2,10},{6,14},... | collective-permute-start | bytes 491528 | tf_op jit(solution)/shard_map/ppermute | solution.py:24
  8.7 10.8 %collective-permute-start.4 = (bf16[128,640]{1,0:T(8,128)(2,1)S(1)}, bf16[128,640]{1,0:T(8,128)(2,1)S(1)}, u32[]{:S(2)}, u32[]{:S(2)}) collective-permute-start(bf16[128,640]{1,0:T(8,128)(2,1)S(1)} %bitcast.17), channel_id=1, source_target_pairs={{0,12},{4,0},{8,4},{12,8},{1,13},{5,1},{9,5},{13,9},{2,14},{6,2},{... | collective-permute-start | bytes 491528 | tf_op jit(solution)/shard_map/ppermute | solution.py:24
  13.3 8.4 %collective-permute-start.1 = (bf16[128,640]{1,0:T(8,128)(2,1)S(1)}, bf16[128,640]{1,0:T(8,128)(2,1)S(1)}, u32[]{:S(2)}, u32[]{:S(2)}) collective-permute-start(bf16[128,640]{1,0:T(8,128)(2,1)S(1)} %collective-permute-done.refs_2_), channel_id=1, source_target_pairs={{0,1},{1,0},{2,3},{3,2},{4,5},{5,4},{6,7},{7,6},{8,9},{9,8},{10,11... | collective-permute-start | bytes 491528 | tf_op jit(solution)/shard_map/ppermute | solution.py:24
  19.4 2.2 %collective-permute-start.3 = (bf16[128,640]{1,0:T(8,128)(2,1)S(1)}, bf16[128,640]{1,0:T(8,128)(2,1)S(1)}, u32[]{:S(2)}, u32[]{:S(2)}) collective-permute-start(bf16[128,640]{1,0:T(8,128)(2,1)S(1)} %collective-permute-done.2.refs_4_), channel_id=1, source_target_pairs={{0,1},{1,0},{2,3},{3,2},{4,5},{5,4},{6,7},{7,6},{8,9},{9,8},{10,11... | collective-permute-start | bytes 491528 | tf_op jit(solution)/shard_map/ppermute | solution.py:24
  19.4 2.2 %collective-permute-start.5 = (bf16[128,640]{1,0:T(8,128)(2,1)S(1)}, bf16[128,640]{1,0:T(8,128)(2,1)S(1)}, u32[]{:S(2)}, u32[]{:S(2)}) collective-permute-start(bf16[128,640]{1,0:T(8,128)(2,1)S(1)} %collective-permute-done.4.refs_6_), channel_id=1, source_target_pairs={{0,1},{1,0},{2,3},{3,2},{4,5},{5,4},{6,7},{7,6},{8,9},{9,8},{10,11... | collective-permute-start | bytes 491528 | tf_op jit(solution)/shard_map/ppermute | solution.py:24
  20.6 1.0 %copy-start.1 = (bf16[2,512,512]{2,1,0:T(8,128)(2,1)}, bf16[2,512,512]{2,1,0:T(8,128)(2,1)S(1)}, u32[]{:S(2)}) copy-start(bf16[2,512,512]{2,1,0:T(8,128)(2,1)S(1)} %get-tuple-element.36.refs_10_) | copy-start | bytes 3145732
  35.7 12.4 %collective-permute-start.10 = (bf16[4,80,640]{2,1,0:T(8,128)(2,1)S(1)}, bf16[4,80,640]{2,1,0:T(8,128)(2,1)S(1)}, u32[]{:S(2)}, u32[]{:S(2)}) collective-permute-start(bf16[4,80,640]{2,1,0:T(8,128)(2,1)S(1)} %get-tuple-element.44), channel_id=1, source_target_pairs={{0,2},{2,0},{1,3},{3,1},{4,6},{6,4},{5,7},{7,5},{8,10},{10,8},{9,1... | collective-permute-start | bytes 1228808 | tf_op jit(solution)/shard_map/ppermute | solution.py:24
  37.3 19.6 %collective-permute-start.14 = (bf16[4,80,640]{2,1,0:T(8,128)(2,1)S(1)}, bf16[4,80,640]{2,1,0:T(8,128)(2,1)S(1)}, u32[]{:S(2)}, u32[]{:S(2)}) collective-permute-start(bf16[4,80,640]{2,1,0:T(8,128)(2,1)S(1)} %get-tuple-element.50), channel_id=1, source_target_pairs={{0,2},{2,0},{1,3},{3,1},{4,6},{6,4},{5,7},{7,5},{8,10},{10,8},{9,1... | collective-permute-start | bytes 1228808 | tf_op jit(solution)/shard_map/ppermute | solution.py:24
  37.8 13.8 %collective-permute-start.6 = (bf16[4,128,320]{2,1,0:T(8,128)(2,1)S(1)}, bf16[4,128,320]{2,1,0:T(8,128)(2,1)S(1)}, u32[]{:S(2)}, u32[]{:S(2)}) collective-permute-start(bf16[4,128,320]{2,1,0:T(8,128)(2,1)S(1)} %get-tuple-element.38), channel_id=1, source_target_pairs={{0,1},{1,0},{2,3},{3,2},{4,5},{5,4},{6,7},{7,6},{8,9},{9,8},{10,11... | collective-permute-start | bytes 983048 | tf_op jit(solution)/shard_map/ppermute | solution.py:24
  48.2 24.4 %collective-permute-start.11 = (bf16[80,640]{1,0:T(8,128)(2,1)S(1)}, bf16[80,640]{1,0:T(8,128)(2,1)S(1)}, u32[]{:S(2)}, u32[]{:S(2)}) collective-permute-start(bf16[80,640]{1,0:T(8,128)(2,1)S(1)} %get-tuple-element.46), channel_id=1, source_target_pairs={{0,4},{4,8},{8,12},{12,0},{1,5},{5,9},{9,13},{13,1},{2,6},{6,10},{... | collective-permute-start | bytes 307208 | tf_op jit(solution)/shard_map/ppermute | solution.py:24
  51.7 7.6 %collective-permute-start.7 = (bf16[128,320]{1,0:T(8,128)(2,1)S(1)}, bf16[128,320]{1,0:T(8,128)(2,1)S(1)}, u32[]{:S(2)}, u32[]{:S(2)}) collective-permute-start(bf16[128,320]{1,0:T(8,128)(2,1)S(1)} %get-tuple-element.40), channel_id=1, source_target_pairs={{0,4},{4,8},{8,12},{12,0},{1,5},{5,9},{9,13},{13,1},{2,6},{6,10},{... | collective-permute-start | bytes 245768 | tf_op jit(solution)/shard_map/ppermute | solution.py:24
  51.8 10.7 %collective-permute-start.8 = (bf16[128,320]{1,0:T(8,128)(2,1)S(1)}, bf16[128,320]{1,0:T(8,128)(2,1)S(1)}, u32[]{:S(2)}, u32[]{:S(2)}) collective-permute-start(bf16[128,320]{1,0:T(8,128)(2,1)S(1)} %get-tuple-element.41), channel_id=1, source_target_pairs={{0,8},{4,12},{8,0},{12,4},{1,9},{5,13},{9,1},{13,5},{2,10},{6,14},... | collective-permute-start | bytes 245768 | tf_op jit(solution)/shard_map/ppermute | solution.py:24
  54.1 15.2 %collective-permute-start.9 = (bf16[128,320]{1,0:T(8,128)(2,1)S(1)}, bf16[128,320]{1,0:T(8,128)(2,1)S(1)}, u32[]{:S(2)}, u32[]{:S(2)}) collective-permute-start(bf16[128,320]{1,0:T(8,128)(2,1)S(1)} %get-tuple-element.42), channel_id=1, source_target_pairs={{0,12},{4,0},{8,4},{12,8},{1,13},{5,1},{9,5},{13,9},{2,14},{6,2},{... | collective-permute-start | bytes 245768 | tf_op jit(solution)/shard_map/ppermute | solution.py:24
  56.9 16.5 %collective-permute-start.12 = (bf16[80,640]{1,0:T(8,128)(2,1)S(1)}, bf16[80,640]{1,0:T(8,128)(2,1)S(1)}, u32[]{:S(2)}, u32[]{:S(2)}) collective-permute-start(bf16[80,640]{1,0:T(8,128)(2,1)S(1)} %get-tuple-element.47), channel_id=1, source_target_pairs={{0,8},{4,12},{8,0},{12,4},{1,9},{5,13},{9,1},{13,5},{2,10},{6,14},... | collective-permute-start | bytes 307208 | tf_op jit(solution)/shard_map/ppermute | solution.py:24
  59.4 14.0 %collective-permute-start.13 = (bf16[80,640]{1,0:T(8,128)(2,1)S(1)}, bf16[80,640]{1,0:T(8,128)(2,1)S(1)}, u32[]{:S(2)}, u32[]{:S(2)}) collective-permute-start(bf16[80,640]{1,0:T(8,128)(2,1)S(1)} %get-tuple-element.48), channel_id=1, source_target_pairs={{0,12},{4,0},{8,4},{12,8},{1,13},{5,1},{9,5},{13,9},{2,14},{6,2},{... | collective-permute-start | bytes 307208 | tf_op jit(solution)/shard_map/ppermute | solution.py:24
  62.5 12.3 %collective-permute-start.15 = (bf16[80,640]{1,0:T(8,128)(2,1)S(1)}, bf16[80,640]{1,0:T(8,128)(2,1)S(1)}, u32[]{:S(2)}, u32[]{:S(2)}) collective-permute-start(bf16[80,640]{1,0:T(8,128)(2,1)S(1)} %get-tuple-element.52), channel_id=1, source_target_pairs={{0,4},{4,8},{8,12},{12,0},{1,5},{5,9},{9,13},{13,1},{2,6},{6,10},{... | collective-permute-start | bytes 307208 | tf_op jit(solution)/shard_map/ppermute | solution.py:24
  69.2 8.9 %collective-permute-start.16 = (bf16[80,640]{1,0:T(8,128)(2,1)S(1)}, bf16[80,640]{1,0:T(8,128)(2,1)S(1)}, u32[]{:S(2)}, u32[]{:S(2)}) collective-permute-start(bf16[80,640]{1,0:T(8,128)(2,1)S(1)} %get-tuple-element.53), channel_id=1, source_target_pairs={{0,8},{4,12},{8,0},{12,4},{1,9},{5,13},{9,1},{13,5},{2,10},{6,14},... | collective-permute-start | bytes 307208 | tf_op jit(solution)/shard_map/ppermute | solution.py:24
  72.6 5.7 %collective-permute-start.17 = (bf16[80,640]{1,0:T(8,128)(2,1)S(1)}, bf16[80,640]{1,0:T(8,128)(2,1)S(1)}, u32[]{:S(2)}, u32[]{:S(2)}) collective-permute-start(bf16[80,640]{1,0:T(8,128)(2,1)S(1)} %get-tuple-element.54), channel_id=1, source_target_pairs={{0,12},{4,0},{8,4},{12,8},{1,13},{5,1},{9,5},{13,9},{2,14},{6,2},{... | collective-permute-start | bytes 307208 | tf_op jit(solution)/shard_map/ppermute | solution.py:24

commit v2 on v1

v2 whole, which is shorter than its diff:
```python
import functools
import math

import jax
import jax.numpy as jnp
from jax import lax
from jax.experimental import pallas as pl
from jax.experimental.pallas import tpu as pltpu
from jax.sharding import PartitionSpec as P

H = 8
VMEM = pl.BlockSpec(memory_space=pltpu.VMEM)
HBM = pl.BlockSpec(memory_space=pltpu.HBM)
BF16 = jnp.bfloat16
F32 = jnp.float32


def params(limit=48 << 20):
    return pltpu.CompilerParams(vmem_limit_bytes=limit)


def shift_send(array, axis, step):
    size = lax.axis_size(axis)
    return lax.ppermute(array, axis, [(i, (i + step) % size) for i in range(size)])


def dot_nn(a, b):
    return lax.dot_general(a, b, (((1,), (0,)), ((), ())), preferred_element_type=F32)


def dot_nt(a, b):
    return lax.dot_general(a, b, (((1,), (1,)), ((), ())), preferred_element_type=F32)


def dot_tn(a, b):
    return lax.dot_general(a, b, (((0,), (0,)), ((), ())), preferred_element_type=F32)


def positional(frame_pos, channels):
    half = channels // 2
    frequency = jnp.exp(-math.log(10000.0) * jnp.arange(half, dtype=F32) * 2.0 / channels)
    angles = frame_pos.astype(F32)[:, None] * frequency[None, :]
    return jnp.concatenate((jnp.sin(angles), jnp.cos(angles)), axis=1)


def by_position(frames, width, back=False):
    rows = frames * width
    inner = width if back else frames
    outer = rows // inner
    row = lax.broadcasted_iota(jnp.int32, (rows, 1), 0)
    col = lax.broadcasted_iota(jnp.int32, (rows, rows), 1)
    source = lax.rem(row, inner) * outer + lax.div(row, inner)
    return jnp.where(col == source, 1.0, 0.0).astype(BF16)


def fetch(ref, owner, width, into, sem):
    start = pl.multiple_of(owner * width, width)
    return [
        pltpu.make_async_copy(ref.at[f, pl.ds(start, width), :], into.at[f], sem)
        for f in range(into.shape[0])
    ]


def block_of(ref, owner, width):
    return ref.at[:, pl.ds(pl.multiple_of(owner * width, width), width), :]


def turned(order, rows):
    frames, width, channels = rows.shape
    return dot_nn(order, rows.reshape(frames * width, channels)).astype(BF16)


def send_kernel(count, width, lat_ref, cot_ref, *refs):
    sends, rows_ref, sems = refs[: count - 1], refs[count - 1], refs[count]
    me = lax.axis_index("tm")
    core = lax.axis_index("sub")

    def copies(ref):
        return [
            pltpu.make_async_copy(
                block_of(ref, lax.rem(me + step, count), width),
                rows_ref.at[step - 1],
                sems.at[step - 1],
            )
            for step in range(1, count)
        ]

    def move(ref):
        moves = copies(ref)
        for copy in moves:
            copy.start()
        order = by_position(rows_ref.shape[1], width)
        for step, copy in enumerate(moves):
            copy.wait()
            sends[step][...] = turned(order, rows_ref[step])

    @pl.when(core == 0)
    def _():
        move(lat_ref)

    @pl.when(core != 0)
    def _():
        move(cot_ref)


def table_kernel(frames, owners, bias_ref, lat_ref, cot_ref, table_ref, own_lat, own_cot, *scratch):
    heads, lanes = bias_ref.shape
    group = table_ref.shape[0]
    span = frames // owners
    me = lax.axis_index("tm")
    copies = []
    if scratch:
        rows_ref, sems = scratch
        width = rows_ref.shape[2]
        for at, ref in enumerate((lat_ref, cot_ref)):
            copies.append(
                pltpu.make_async_copy(block_of(ref, me, width), rows_ref.at[at], sems.at[at])
            )
            copies[-1].start()

    def place_of(index):
        return lax.rem(lax.div(index, span), group // frames)

    def frame_of(index):
        owner = lax.rem(me - lax.div(index, group // owners) + owners, owners)
        return owner * span + lax.rem(index, span)

    row = lax.broadcasted_iota(jnp.int32, (group, 1), 0)
    col = lax.broadcasted_iota(jnp.int32, (1, group), 1)
    same = place_of(row) == place_of(col)
    left = jnp.where(frame_of(row) == col, 1.0, 0.0)
    right = jnp.where(row == frame_of(col), 1.0, 0.0)

    def exact(a, b):
        return lax.dot_general(
            a, b, (((1,), (0,)), ((), ())), precision=lax.Precision.HIGHEST,
            preferred_element_type=F32,
        )

    for h in range(heads):
        spread = jnp.broadcast_to(bias_ref[h : h + 1, :], (group, lanes))
        skewed = pltpu.roll(spread, (1 - frames) % lanes, 1, stride=1, stride_axis=0)
        turned_bias = exact(left, exact(skewed[:, :group], right))
        table_ref[:, h * group : (h + 1) * group] = jnp.where(same, turned_bias, -1e30)
    if scratch:
        order = by_position(span, width)
        for at, ref in enumerate((own_lat, own_cot)):
            copies[at].wait()
            ref[...] = turned(order, rows_ref[at])
    else:
        own_lat[...] = lat_ref[...]
        own_cot[...] = cot_ref[...]


def send_blocks(latents, cotangent, count):
    frames, positions, channels = latents.shape
    width = positions // count
    if width % 16 == 0:
        shape = jax.ShapeDtypeStruct((frames * width, channels), BF16)
        return pl.pallas_call(
            functools.partial(send_kernel, count, width),
            out_shape=[shape] * (count - 1),
            in_specs=[HBM] * 2,
            out_specs=[VMEM] * (count - 1),
            scratch_shapes=[
                pltpu.VMEM((count - 1, frames, width, channels), BF16),
                pltpu.SemaphoreType.DMA((count - 1,)),
            ],
            compiler_params=params(60 << 20),
            name="send_blocks",
        )(latents, cotangent)
    me = lax.axis_index("tm")
    sent = jnp.where(lax.axis_index("sub") == 0, latents, cotangent)
    return [cut(sent, lax.rem(me + step, count), width) for step in range(1, count)]


def cut(array, owner, width):
    block = lax.dynamic_slice_in_dim(array, owner * width, width, 1)
    return jnp.swapaxes(block, 0, 1).reshape(-1, array.shape[2])


def tables(time_bias, latents, cotangent, heads, owners, group):
    span, positions, channels = latents.shape
    frames, width = span * owners, positions // owners
    first = lax.axis_index("sub") * heads
    own = jnp.flip(lax.dynamic_slice_in_dim(time_bias, first, heads, 0), 1)
    lanes = -(-max(2 * frames - 1, group) // 128) * 128
    own = jnp.pad(own, ((0, 0), (0, lanes - own.shape[1])))
    scratch, specs = [], [VMEM] * 3
    if width % 16 == 0:
        scratch = [pltpu.VMEM((2, span, width, channels), BF16), pltpu.SemaphoreType.DMA((2,))]
        specs = [VMEM, HBM, HBM]
    else:
        me = lax.axis_index("tm")
        latents, cotangent = cut(latents, me, width), cut(cotangent, me, width)
    rows = jax.ShapeDtypeStruct((span * width, channels), BF16)
    return pl.pallas_call(
        functools.partial(table_kernel, frames, owners),
        out_shape=[jax.ShapeDtypeStruct((group, heads * group), F32), rows, rows],
        in_specs=specs,
        out_specs=[VMEM] * 3,
        scratch_shapes=scratch,
        compiler_params=params(),
        name="tables",
    )(own, latents, cotangent)


def attend_kernel(owners, heads, *refs):
    parts = 2 * owners
    inputs, refs = refs[:parts], refs[parts:]
    pe_ref, table_ref, w_qkv_ref, w_out_ref = refs[:4]
    hidden_ref, cot_ref, dqk_ref, dvo_ref, back_keep, back_send = refs[4:10]
    q_ref, k_ref, v_ref, g_ref = refs[10:]

    core = lax.axis_index("sub")
    rows, channels = hidden_ref.shape
    width = q_ref.shape[1]
    size = width // heads
    group = table_ref.shape[0]
    span = pe_ref.shape[0] // owners
    chunk = rows // owners
    piece = group // owners
    inv_root = 1.0 / math.sqrt(size)

    for step in range(owners):
        at = slice(step * chunk, (step + 1) * chunk)
        first, second = inputs[2 * step][...], inputs[2 * step + 1][...]
        if step == 0:
            lat, cot = first, second
        else:
            lat = jnp.where(core == 0, first, second)
            cot = jnp.where(core == 0, second, first)
        pe = pe_ref[step * span : (step + 1) * span, :]
        lat = lat.astype(F32).reshape(chunk // span, span, channels) + pe[None]
        hidden_ref[at, :] = lat.reshape(chunk, channels).astype(BF16)
        cot_ref[at, :] = cot

    hidden = hidden_ref[...]
    for t, ref in enumerate((q_ref, k_ref, v_ref)):
        ref[...] = dot_nt(hidden, w_qkv_ref[t]).astype(BF16)
    g_ref[...] = dot_nt(cot_ref[...], w_out_ref[...]).astype(BF16)

    lane = lax.broadcasted_iota(jnp.int32, (group, width), 1)
    masks = [(lane >= h * size) & (lane < (h + 1) * size) for h in range(heads)]
    zero = jnp.zeros((group, width), BF16)

    def stack(value):
        return jnp.concatenate([jnp.where(mask, value, zero) for mask in masks], axis=0)

    def flip(value):
        return jnp.concatenate(
            [value[:, h * group : (h + 1) * group].T for h in range(heads)], axis=1
        )

    for start in range(0, chunk, piece):
        spans = [slice(k * chunk + start, k * chunk + start + piece) for k in range(owners)]

        def rows_of(ref, spans=spans):
            return jnp.concatenate([ref[at, :] for at in spans], axis=0)

        def put(ref, value, spans=spans):
            for k, at in enumerate(spans):
                ref[at, :] = value[k * piece : (k + 1) * piece, :]

        query, key, value, grad = rows_of(q_ref), rows_of(k_ref), rows_of(v_ref), rows_of(g_ref)
        keys, values = stack(key), stack(value)
        scores = dot_nt(query, keys) * inv_root + table_ref[...]
        grad_probs = dot_nt(grad, values)
        low, grad_scores = [], []
        for h in range(heads):
            part = slice(h * group, (h + 1) * group)
            own = scores[:, part]
            raw = jnp.exp(own - jnp.max(own, axis=1, keepdims=True))
            probs = raw / jnp.sum(raw, axis=1, keepdims=True)
            up = grad_probs[:, part]
            row_dot = jnp.sum(probs * up, axis=1, keepdims=True)
            low.append(probs.astype(BF16))
            grad_scores.append((probs * (up - row_dot) * inv_root).astype(BF16))
        low = jnp.concatenate(low, axis=1)
        grad_scores = jnp.concatenate(grad_scores, axis=1)
        attn_out = dot_nn(low, values)
        grad_query = dot_nn(grad_scores, keys)
        grad_key = dot_nn(flip(grad_scores), stack(query))
        grad_value = dot_nn(flip(low), stack(grad))
        put(dqk_ref, jnp.concatenate([grad_query, grad_key], axis=1).astype(BF16))
        put(dvo_ref, jnp.concatenate([grad_value, attn_out], axis=1).astype(BF16))

    grad_v = dvo_ref[:, :width]
    back = dot_nn(dqk_ref[...], w_qkv_ref[0:2].reshape(2 * width, channels))
    back = (back + dot_nn(grad_v, w_qkv_ref[2])).astype(BF16).astype(F32)
    lower, upper = back[:, :width], back[:, width:]
    cot = cot_ref[...].astype(F32)

    def store(own, other, base):
        for k in range(owners):
            slot = (owners - k) % owners
            at = slice(k * chunk, (k + 1) * chunk)
            back_keep[slot] = own[at, :] + base[at, :]
            back_send[slot] = other[at, :].astype(BF16)

    @pl.when(core == 0)
    def _():
        store(lower, upper, cot[:, :width])

    @pl.when(core != 0)
    def _():
        store(upper, lower, cot[:, width:])


def attend(inputs, pe, table, w_qkv, w_out, owners, heads):
    chunk, channels = inputs[0].shape
    rows = chunk * owners
    width = w_qkv.shape[1]
    outs = [
        jax.ShapeDtypeStruct((rows, channels), BF16),
        jax.ShapeDtypeStruct((rows, channels), BF16),
        jax.ShapeDtypeStruct((rows, 2 * width), BF16),
        jax.ShapeDtypeStruct((rows, 2 * width), BF16),
        jax.ShapeDtypeStruct((owners, chunk, width), F32),
        jax.ShapeDtypeStruct((owners, chunk, width), BF16),
    ]
    return pl.pallas_call(
        functools.partial(attend_kernel, owners, heads),
        out_shape=outs,
        in_specs=[VMEM] * (len(inputs) + 4),
        out_specs=[VMEM] * len(outs),
        scratch_shapes=[pltpu.VMEM((rows, width), BF16)] * 4,
        compiler_params=params(),
        name="attend",
    )(*inputs, pe, table, w_qkv, w_out)


def weight_kernel(owners, sides, block, count, *refs):
    lefts, grad_ref, outs = refs[:count], refs[count], refs[count + 1 :]
    me, side = lax.axis_index("tm"), lax.axis_index("rows")
    grads = grad_ref[...]
    full = dot_tn(lefts[0][...], grads)
    if count == 2:
        lane = lax.broadcasted_iota(jnp.int32, full.shape, 1)
        full = jnp.where(lane < full.shape[1] // 2, full, dot_tn(lefts[1][...], grads))
    if block % 16:
        outs[0][...] = full
        return
    for z in range(owners):
        slot = lax.rem(z - me + owners, owners)
        for x in range(sides):
            first = (z * sides + x) * block
            piece = full[first : first + block, :]
            turn = lax.rem(x - side + sides, sides)
            for j in range(sides):

                @pl.when(turn == j)
                def _(piece=piece, j=j, slot=slot):
                    outs[j][slot] = piece if j == 0 else piece.astype(BF16)


def weight_terms(lefts, grads, owners, sides):
    channels, columns = lefts[0].shape[1], grads.shape[1]
    block = channels // (owners * sides)
    if block % 16 == 0:
        keep = jax.ShapeDtypeStruct((owners, block, columns), F32)
        outs = [keep] + [jax.ShapeDtypeStruct((owners, block, columns), BF16)] * (sides - 1)
    else:
        outs = [jax.ShapeDtypeStruct((channels, columns), F32)]
    result = pl.pallas_call(
        functools.partial(weight_kernel, owners, sides, block, len(lefts)),
        out_shape=outs,
        in_specs=[VMEM] * (len(lefts) + 1),
        out_specs=[VMEM] * len(outs),
        compiler_params=params(),
        name="weight_terms",
    )(*lefts, grads)
    if block % 16 == 0:
        return result[0], list(result[1:])
    full = result[0].reshape(owners, sides, block, columns)
    full = jnp.roll(full, (-lax.axis_index("tm"), -lax.axis_index("rows")), (0, 1))
    return full[:, 0], [full[:, j].astype(BF16) for j in range(1, sides)]


def combine_kernel(keep_ref, *refs):
    owners = keep_ref.shape[0]
    arrived, outs = refs[: len(refs) - owners], refs[len(refs) - owners :]
    for slot in range(owners):
        total = keep_ref[slot]
        for ref in arrived:
            total = total + ref[slot].astype(F32)
        outs[slot][...] = total.astype(outs[slot].dtype)


def combine(keep, arrived, own_dtype):
    owners = keep.shape[0]
    outs = [jax.ShapeDtypeStruct(keep.shape[1:], own_dtype)]
    outs += [jax.ShapeDtypeStruct(keep.shape[1:], BF16)] * (owners - 1)
    result = pl.pallas_call(
        combine_kernel,
        out_shape=outs,
        in_specs=[VMEM] * (1 + len(arrived)),
        out_specs=[VMEM] * owners,
        compiler_params=params(),
        name="combine",
    )(keep, *arrived)
    return result[0], result[1:]


def finish_kernel(count, *refs):
    ins, (w_qkv_ref, w_out_ref) = refs[:-2], refs[-2:]

    def total(parts):
        value = parts[0][...]
        for ref in parts[1:]:
            value = value + ref[...].astype(F32)
        return value

    width = w_out_ref.shape[1]
    value_out, query_key = total(ins[:count]), total(ins[count:])
    w_qkv_ref[0] = query_key[:, :width]
    w_qkv_ref[1] = query_key[:, width:]
    w_qkv_ref[2] = value_out[:, :width]
    w_out_ref[...] = value_out[:, width:]


def finish(value_out, query_key):
    block, width = value_out[0].shape[0], value_out[0].shape[1] // 2
    count = len(value_out)
    w_qkv, w_out = pl.pallas_call(
        functools.partial(finish_kernel, count),
        out_shape=[
            jax.ShapeDtypeStruct((3, block, width), F32),
            jax.ShapeDtypeStruct((block, width), F32),
        ],
        in_specs=[VMEM] * (2 * count),
        out_specs=[VMEM] * 2,
        compiler_params=params(),
        name="finish",
    )(*value_out, *query_key)
    return jnp.transpose(w_qkv, (1, 0, 2)), w_out


def place_kernel(*refs):
    blocks, out_ref = refs[:-1], refs[-1]
    count = len(blocks)
    frames, positions, channels = out_ref.shape
    width = positions // count
    me = lax.axis_index("tm")
    order = by_position(frames, width, back=True)
    for step, ref in enumerate(blocks):
        start = pl.multiple_of(lax.rem(me - step + count, count) * width, width)
        rows = dot_nn(order, ref[...]).astype(BF16)
        out_ref[:, pl.ds(start, width), :] = rows.reshape(frames, width, channels)


def place(blocks, frames):
    count = len(blocks)
    chunk, channels = blocks[0].shape
    width = chunk // frames
    if width % 16 == 0:
        return pl.pallas_call(
            place_kernel,
            out_shape=jax.ShapeDtypeStruct((frames, count * width, channels), BF16),
            in_specs=[VMEM] * count,
            out_specs=VMEM,
            compiler_params=params(),
            name="place",
        )(*blocks)
    ordered = jnp.roll(jnp.stack(blocks[::-1]), lax.axis_index("tm") + 1, 0)
    ordered = ordered.reshape(count, width, frames, channels)
    return jnp.transpose(ordered, (2, 0, 1, 3)).reshape(frames, count * width, channels)


def per_device(latents, cotangent, w_qkv, w_out, time_bias):
    span, positions, channels = latents.shape
    owners, sides = lax.axis_size("tm"), lax.axis_size("rows")
    frames = span * owners
    heads = H // lax.axis_size("sub")
    group = max(frames, 128)
    me = lax.axis_index("tm")

    sends = send_blocks(latents, cotangent, owners)
    table, own_lat, own_cot = tables(time_bias, latents, cotangent, heads, owners, group)
    owner = lax.rem(me - jnp.arange(owners, dtype=jnp.int32) + owners, owners)
    frame_pos = owner[:, None] * span + jnp.arange(span, dtype=jnp.int32)[None]
    pe = positional(frame_pos.reshape(-1), channels)
    inputs = [own_lat, own_cot]
    for step, block in enumerate(sends):
        mine = shift_send(block, "tm", step + 1)
        inputs += [mine, shift_send(mine, "sub", 1)]
    hidden, cot, grad_qk, grad_vo, back_keep, back_send = attend(
        inputs, pe, table, jnp.transpose(w_qkv, (1, 2, 0)), w_out, owners, heads
    )

    own_back, back_blocks = combine(back_keep, [shift_send(back_send, "sub", 1)], BF16)
    back_blocks = [own_back] + [
        shift_send(block, "tm", step + 1) for step, block in enumerate(back_blocks)
    ]
    sums = []
    for lefts, grads in (((hidden, cot), grad_vo), ((hidden,), grad_qk)):
        if grads is grad_qk:
            grads, _ = lax.optimization_barrier((grads, own_back))
        keep, side_blocks = weight_terms(lefts, grads, owners, sides)
        arrived = [shift_send(b, "rows", j + 1) for j, b in enumerate(side_blocks)]
        if grads is grad_vo:
            arrived, back_blocks = lax.optimization_barrier((arrived, back_blocks))
        own, blocks = combine(keep, arrived, F32)
        sums.append([own] + [shift_send(b, "tm", step + 1) for step, b in enumerate(blocks)])
    grad_w_qkv, grad_w_out_t = finish(*sums)
    return (place(back_blocks, span), grad_w_qkv, grad_w_out_t)


def solution(mesh):
    return jax.shard_map(
        per_device,
        mesh=mesh,
        in_specs=(
            P("tm", ("req", "rows"), None),
            P("tm", ("req", "rows"), None),
            P(None, None, "sub"),
            P("sub", None),
            P(),
        ),
        out_specs=(
            P("tm", ("req", "rows"), "sub"),
            P(("req", "tm", "rows"), None, "sub"),
            P(("req", "tm", "rows"), "sub"),
        ),
        check_vma=False,
    )
```

time: 79.5 us -> 67.1 us (0.84)
  starting transfers between devices: 33.5 us -> 27.2 us
  local copies, waits for them, and re-layouts: 3.28 us -> 0.22 us
  waiting for transfers between devices: 24.7 us -> 22.8 us
  Pallas kernels: 16.6 us -> 15.5 us
    ppermute x18, starting transfers between devices: 33.5 us -> 27.2 us  [shift_send(): lax.ppermute(array, axis, [(i, (i + step) % size) for i in range(size)])]
    unnamed x10 -> x8, local copies, waits for them, and re-layouts: 3.17 us -> 0.02 us
    ppermute x18, waiting for transfers between devices: 24.7 us -> 22.8 us  [shift_send(): lax.ppermute(array, axis, [(i, (i + step) % size) for i in range(size)])]
    pallas_call x3 -> x5, Pallas kernels: 14.7 us -> 13.4 us  [the longest x1 7.43 us: attend(): pl.pallas_call(functools.partial(attend_kernel, owners, heads), out_shape...]
  transfers between devices with their start and end apart: 18 -> 18, of which waited for: 7 -> 7; matrix products, arithmetic and copies ran while one was open for 1% -> 1% of each run, Pallas kernels for 2% -> 7%
where the time goes in v2:
time: 67.1 us; the launch traced here: 66.9 us
  starting transfers between devices  27.2 us (41%)
  waiting for transfers between devices  22.8 us (34%)
  Pallas kernels  15.5 us (23%)
  between operations  0.77 us (1%)
    ppermute x18, starting transfers between devices, shift_send(): lax.ppermute(array, axis, [(i, (i + step) % size) for i in range(size)])  27.2 us
    ppermute x18, waiting for transfers between devices, shift_send(): lax.ppermute(array, axis, [(i, (i + step) % size) for i in range(size)])  22.8 us
    pallas_call x1, Pallas kernels, attend(): pl.pallas_call(functools.partial(attend_kernel, owners, heads), out_shape...  7.43 us
    pallas_call x1, Pallas kernels, send_blocks(): pl.pallas_call(functools.partial(send_kernel, count, width), out_shape=[s...  2.43 us
    pallas_call x2, Pallas kernels, weight_terms(): pl.pallas_call(functools.partial(weight_kernel, owners, sides, block, len...  2.2 us
  transfers between devices with their start and end apart: 18, of which 7 were waited for; matrix products, arithmetic and copies ran while one was open for 1% of the time, Pallas kernels for 7%

profile of v2, /device:TPU:0, one launch (start us, length us, event | category | flops | bytes accessed | tf_op | source)
XLA Modules:
  0.0 66.9 jit_solution(1372342510885175924)
XLA Ops:
  0.7 2.4 %send_blocks.1 = (bf16[128,640]{1,0:T(8,128)(2,1)}, bf16[128,640]{1,0:T(8,128)(2,1)}, bf16[128,640]{1,0:T(8,128)(2,1)}) custom-call(bf16[8,64,640]{2,1,0:T(8,128)(2,1)} %lat_ref.3, bf16[8,64,640]{2,1,0:T(8,128)(2,1)} %cot_ref.3), custom_call_target="tpu_custom_call" | custom-call | tf_op jit(solution)/shard_map/send_blocks/pallas_call | solution.py:160
  3.1 3.1 %collective-permute-start = (bf16[128,640]{1,0:T(8,128)(2,1)}, bf16[128,640]{1,0:T(8,128)(2,1)S(1)}, u32[]{:S(2)}, u32[]{:S(2)}) collective-permute-start(bf16[128,640]{1,0:T(8,128)(2,1)} %get-tuple-element.41), channel_id=1, source_target_pairs={{0,4},{4,8},{8,12},{12,0},{1,5},{5,9},{9,13},{13,1},{2,6},{6,10},{... | collective-permute-start | bytes 491528 | tf_op jit(solution)/shard_map/ppermute | solution.py:24
  6.2 2.6 %collective-permute-start.2 = (bf16[128,640]{1,0:T(8,128)(2,1)}, bf16[128,640]{1,0:T(8,128)(2,1)S(1)}, u32[]{:S(2)}, u32[]{:S(2)}) collective-permute-start(bf16[128,640]{1,0:T(8,128)(2,1)} %get-tuple-element.42), channel_id=1, source_target_pairs={{0,8},{4,12},{8,0},{12,4},{1,9},{5,13},{9,1},{13,5},{2,10},{6,14},... | collective-permute-start | bytes 491528 | tf_op jit(solution)/shard_map/ppermute | solution.py:24
  8.8 1.3 %collective-permute-start.4 = (bf16[128,640]{1,0:T(8,128)(2,1)}, bf16[128,640]{1,0:T(8,128)(2,1)S(1)}, u32[]{:S(2)}, u32[]{:S(2)}) collective-permute-start(bf16[128,640]{1,0:T(8,128)(2,1)} %get-tuple-element.43), channel_id=1, source_target_pairs={{0,12},{4,0},{8,4},{12,8},{1,13},{5,1},{9,5},{13,9},{2,14},{6,2},{... | collective-permute-start | bytes 491528 | tf_op jit(solution)/shard_map/ppermute | solution.py:24
  10.3 0.3 multiply_sine_fusion
  10.6 3.0 %collective-permute-done.refs_2_ = bf16[128,640]{1,0:T(8,128)(2,1)S(1)} collective-permute-done((bf16[128,640]{1,0:T(8,128)(2,1)}, bf16[128,640]{1,0:T(8,128)(2,1)S(1)}, u32[]{:S(2)}, u32[]{:S(2)}) %collective-permute-start) | collective-permute-done | bytes 163872 | tf_op jit(solution)/shard_map/ppermute | solution.py:24
  13.6 6.2 %collective-permute-done.2.refs_4_ = bf16[128,640]{1,0:T(8,128)(2,1)S(1)} collective-permute-done((bf16[128,640]{1,0:T(8,128)(2,1)}, bf16[128,640]{1,0:T(8,128)(2,1)S(1)}, u32[]{:S(2)}, u32[]{:S(2)}) %collective-permute-start.2) | collective-permute-done | bytes 163872 | tf_op jit(solution)/shard_map/ppermute | solution.py:24
  19.8 0.5 collective-permute-start.5
  20.3 0.1 rev.4
  20.4 1.3 %tables.1 = (f32[128,512]{1,0:T(8,128)S(1)}, bf16[128,640]{1,0:T(8,128)(2,1)S(1)}, bf16[128,640]{1,0:T(8,128)(2,1)S(1)}) custom-call(f32[4,128]{1,0:T(4,128)S(1)} %pad.4.bias_ref, bf16[8,64,640]{2,1,0:T(8,128)(2,1)S(1)} %copy-done.1, bf16[8,64,640]{2,1,0:T(8,128)(2,1)S(1)} %copy-done.2), custom_call_target="tpu_custom_call" | custom-call | tf_op jit(solution)/shard_map/tables/pallas_call | solution.py:197
  21.8 7.4 %attend.1 = (bf16[512,640]{1,0:T(8,128)(2,1)S(1)}, bf16[512,640]{1,0:T(8,128)(2,1)S(1)}, bf16[512,640]{1,0:T(8,128)(2,1)S(1)}, bf16[512,640]{1,0:T(8,128)(2,1)S(...) custom-call(bf16[128,640]{1,0:T(8,128)(2,1)S(1)} %get-tuple-element.39.refs_0_, ...), custom_call_target="tpu_custom_call" | custom-call | tf_op jit(solution)/shard_map/attend/pallas_call | solution.py:322
  29.3 0.1 collective-permute-start.7
  29.4 1.3 %weight_terms.2 = (f32[4,80,640]{2,1,0:T(8,128)S(1)}, bf16[4,80,640]{2,1,0:T(8,128)(2,1)S(1)}) custom-call(bf16[512,640]{1,0:T(8,128)(2,1)S(1)} %get-tuple-element.45.refs_0_, bf16[512,640]{1,0:T(8,128)(2,1)S(1)} %get-tuple-element.46.refs_1_, bf16[512,640]{1,0:T(8,128)(2,1)S(1)} %get-tuple-element.47.refs_2_), custom_call_target="tpu_custom_call" | custom-call | tf_op jit(solution)/shard_map/weight_terms/pallas_call | solution.py:365
  30.7 1.6 %collective-permute-start.6 = (bf16[4,80,640]{2,1,0:T(8,128)(2,1)S(1)}, bf16[4,80,640]{2,1,0:T(8,128)(2,1)S(1)}, u32[]{:S(2)}, u32[]{:S(2)}) collective-permute-start(bf16[4,80,640]{2,1,0:T(8,128)(2,1)S(1)} %get-tuple-element.48), channel_id=1, source_target_pairs={{0,2},{2,0},{1,3},{3,1},{4,6},{6,4},{5,7},{7,5},{8,10},{10,8},{9,1... | collective-permute-start | bytes 1228808 | tf_op jit(solution)/shard_map/ppermute | solution.py:24
  32.4 0.9 %weight_terms.3 = (f32[4,80,640]{2,1,0:T(8,128)S(1)}, bf16[4,80,640]{2,1,0:T(8,128)(2,1)S(1)}) custom-call(bf16[512,640]{1,0:T(8,128)(2,1)S(1)} %get-tuple-element.45.refs_0_, bf16[512,640]{1,0:T(8,128)(2,1)S(1)} %get-tuple-element.66.refs_1_), custom_call_target="tpu_custom_call" | custom-call | tf_op jit(solution)/shard_map/weight_terms/pallas_call | solution.py:365
  33.2 0.6 collective-permute-start.14
  33.8 4.0 %collective-permute-start.8 = (bf16[128,320]{1,0:T(8,128)(2,1)S(1)}, bf16[128,320]{1,0:T(8,128)(2,1)S(1)}, u32[]{:S(2)}, u32[]{:S(2)}) collective-permute-start(bf16[128,320]{1,0:T(8,128)(2,1)S(1)} %get-tuple-element.52), channel_id=1, source_target_pairs={{0,4},{4,8},{8,12},{12,0},{1,5},{5,9},{9,13},{13,1},{2,6},{6,10},{... | collective-permute-start | bytes 245768 | tf_op jit(solution)/shard_map/ppermute | solution.py:24
  37.8 1.6 %collective-permute-start.9 = (bf16[128,320]{1,0:T(8,128)(2,1)S(1)}, bf16[128,320]{1,0:T(8,128)(2,1)S(1)}, u32[]{:S(2)}, u32[]{:S(2)}) collective-permute-start(bf16[128,320]{1,0:T(8,128)(2,1)S(1)} %get-tuple-element.53), channel_id=1, source_target_pairs={{0,8},{4,12},{8,0},{12,4},{1,9},{5,13},{9,1},{13,5},{2,10},{6,14},... | collective-permute-start | bytes 245768 | tf_op jit(solution)/shard_map/ppermute | solution.py:24
  39.4 0.7 %collective-permute-start.10 = (bf16[128,320]{1,0:T(8,128)(2,1)S(1)}, bf16[128,320]{1,0:T(8,128)(2,1)S(1)}, u32[]{:S(2)}, u32[]{:S(2)}) collective-permute-start(bf16[128,320]{1,0:T(8,128)(2,1)S(1)} %get-tuple-element.54), channel_id=1, source_target_pairs={{0,12},{4,0},{8,4},{12,8},{1,13},{5,1},{9,5},{13,9},{2,14},{6,2},{... | collective-permute-start | bytes 245768 | tf_op jit(solution)/shard_map/ppermute | solution.py:24
  40.1 2.4 %collective-permute-done.8.refs_1_ = bf16[128,320]{1,0:T(8,128)(2,1)S(1)} collective-permute-done((bf16[128,320]{1,0:T(8,128)(2,1)S(1)}, bf16[128,320]{1,0:T(8,128)(2,1)S(1)}, u32[]{:S(2)}, u32[]{:S(2)}) %collective-permute-start.8) | collective-permute-done | bytes 81952 | tf_op jit(solution)/shard_map/ppermute | solution.py:24
  42.6 3.5 %collective-permute-done.9.refs_2_ = bf16[128,320]{1,0:T(8,128)(2,1)S(1)} collective-permute-done((bf16[128,320]{1,0:T(8,128)(2,1)S(1)}, bf16[128,320]{1,0:T(8,128)(2,1)S(1)}, u32[]{:S(2)}, u32[]{:S(2)}) %collective-permute-start.9) | collective-permute-done | bytes 81952 | tf_op jit(solution)/shard_map/ppermute | solution.py:24
  46.2 2.6 %collective-permute-start.11 = (bf16[80,640]{1,0:T(8,128)(2,1)S(1)}, bf16[80,640]{1,0:T(8,128)(2,1)S(1)}, u32[]{:S(2)}, u32[]{:S(2)}) collective-permute-start(bf16[80,640]{1,0:T(8,128)(2,1)S(1)} %get-tuple-element.62), channel_id=1, source_target_pairs={{0,4},{4,8},{8,12},{12,0},{1,5},{5,9},{9,13},{13,1},{2,6},{6,10},{... | collective-permute-start | bytes 307208 | tf_op jit(solution)/shard_map/ppermute | solution.py:24
  48.8 1.0 %collective-permute-start.12 = (bf16[80,640]{1,0:T(8,128)(2,1)S(1)}, bf16[80,640]{1,0:T(8,128)(2,1)S(1)}, u32[]{:S(2)}, u32[]{:S(2)}) collective-permute-start(bf16[80,640]{1,0:T(8,128)(2,1)S(1)} %get-tuple-element.63), channel_id=1, source_target_pairs={{0,8},{4,12},{8,0},{12,4},{1,9},{5,13},{9,1},{13,5},{2,10},{6,14},... | collective-permute-start | bytes 307208 | tf_op jit(solution)/shard_map/ppermute | solution.py:24
  49.8 1.5 %collective-permute-start.13 = (bf16[80,640]{1,0:T(8,128)(2,1)S(1)}, bf16[80,640]{1,0:T(8,128)(2,1)S(1)}, u32[]{:S(2)}, u32[]{:S(2)}) collective-permute-start(bf16[80,640]{1,0:T(8,128)(2,1)S(1)} %get-tuple-element.64), channel_id=1, source_target_pairs={{0,12},{4,0},{8,4},{12,8},{1,13},{5,1},{9,5},{13,9},{2,14},{6,2},{... | collective-permute-start | bytes 307208 | tf_op jit(solution)/shard_map/ppermute | solution.py:24
  51.2 0.2 collective-permute-done.14.refs_0_
  51.5 3.6 %collective-permute-start.15 = (bf16[80,640]{1,0:T(8,128)(2,1)S(1)}, bf16[80,640]{1,0:T(8,128)(2,1)S(1)}, u32[]{:S(2)}, u32[]{:S(2)}) collective-permute-start(bf16[80,640]{1,0:T(8,128)(2,1)S(1)} %get-tuple-element.70), channel_id=1, source_target_pairs={{0,4},{4,8},{8,12},{12,0},{1,5},{5,9},{9,13},{13,1},{2,6},{6,10},{... | collective-permute-start | bytes 307208 | tf_op jit(solution)/shard_map/ppermute | solution.py:24
  55.1 2.1 %collective-permute-start.16 = (bf16[80,640]{1,0:T(8,128)(2,1)S(1)}, bf16[80,640]{1,0:T(8,128)(2,1)S(1)}, u32[]{:S(2)}, u32[]{:S(2)}) collective-permute-start(bf16[80,640]{1,0:T(8,128)(2,1)S(1)} %get-tuple-element.71), channel_id=1, source_target_pairs={{0,8},{4,12},{8,0},{12,4},{1,9},{5,13},{9,1},{13,5},{2,10},{6,14},... | collective-permute-start | bytes 307208 | tf_op jit(solution)/shard_map/ppermute | solution.py:24
  57.2 0.3 collective-permute-start.17
  57.5 1.0 %place.1 = bf16[8,64,320]{2,1,0:T(8,128)(2,1)} custom-call(bf16[128,320]{1,0:T(8,128)(2,1)S(1)} %get-tuple-element.55.refs_0_, bf16[128,320]{1,0:T(8,128)(2,1)S(1)} %collective-permute-done.8.refs_1_, bf16[128,320]{1,0:T(8,128)(2,1)S(1)} %collective-permute-done.9.refs_2_, bf16[128,320]{1,0:T(8,128)(2,1)S(1)} %collective-permute-done.10.refs_3_), custom_call_target="tpu_custom_call" | custom-call | tf_op jit(solution)/shard_map/place/pallas_call | solution.py:457
  58.5 1.9 %collective-permute-done.15.refs_5_ = bf16[80,640]{1,0:T(8,128)(2,1)S(1)} collective-permute-done((bf16[80,640]{1,0:T(8,128)(2,1)S(1)}, bf16[80,640]{1,0:T(8,128)(2,1)S(1)}, u32[]{:S(2)}, u32[]{:S(2)}) %collective-permute-start.15) | collective-permute-done | bytes 102432 | tf_op jit(solution)/shard_map/ppermute | solution.py:24
  60.4 5.6 %collective-permute-done.16.refs_6_ = bf16[80,640]{1,0:T(8,128)(2,1)S(1)} collective-permute-done((bf16[80,640]{1,0:T(8,128)(2,1)S(1)}, bf16[80,640]{1,0:T(8,128)(2,1)S(1)}, u32[]{:S(2)}, u32[]{:S(2)}) %collective-permute-start.16) | collective-permute-done | bytes 102432 | tf_op jit(solution)/shard_map/ppermute | solution.py:24
  66.0 0.9 %finish.1 = (f32[3,80,320]{2,1,0:T(8,128)}, f32[80,320]{1,0:T(8,128)}) custom-call(f32[80,640]{1,0:T(8,128)S(1)} %get-tuple-element.61.refs_0_, bf16[80,640]{1,0:T(8,128)(2,1)S(1)} %collective-permute-done.11.refs_1_, bf16[80,640]{1,0:T(8,128)(2,1)S(1)} %collective-permute-done.12.refs_2_, bf16[80,640]{1,0:T(8,128)(2,1)S(1)} %collective-permute-done.13.refs_3_, ...), custom_call_target="tpu_custom_call" | custom-call | tf_op jit(solution)/shard_map/finish/pallas_call | solution.py:425
  (31 shorter events, 0.6 us)
Async XLA Ops:
  0.6 19.6 %copy-start = (f32[8,63]{1,0:T(8,128)S(1)}, f32[8,63]{1,0:T(8,128)}, u32[]{:S(2)}) copy-start(f32[8,63]{1,0:T(8,128)} %param.9) | copy-start | bytes 6052
  0.6 19.7 %copy-start.2 = (bf16[8,64,640]{2,1,0:T(8,128)(2,1)S(1)}, bf16[8,64,640]{2,1,0:T(8,128)(2,1)}, u32[]{:S(2)}) copy-start(bf16[8,64,640]{2,1,0:T(8,128)(2,1)} %cot_ref.3) | copy-start | bytes 1966084
  0.7 19.7 %copy-start.1 = (bf16[8,64,640]{2,1,0:T(8,128)(2,1)S(1)}, bf16[8,64,640]{2,1,0:T(8,128)(2,1)}, u32[]{:S(2)}) copy-start(bf16[8,64,640]{2,1,0:T(8,128)(2,1)} %lat_ref.3) | copy-start | bytes 1966084
  0.7 21.1 %copy-start.3 = (bf16[320,640]{1,0:T(8,128)(2,1)S(1)}, bf16[320,640]{1,0:T(8,128)(2,1)}, u32[]{:S(2)}) copy-start(bf16[320,640]{1,0:T(8,128)(2,1)} %refs_11_.1) | copy-start | bytes 1228804
  3.1 10.4 %collective-permute-start = (bf16[128,640]{1,0:T(8,128)(2,1)}, bf16[128,640]{1,0:T(8,128)(2,1)S(1)}, u32[]{:S(2)}, u32[]{:S(2)}) collective-permute-start(bf16[128,640]{1,0:T(8,128)(2,1)} %get-tuple-element.41), channel_id=1, source_target_pairs={{0,4},{4,8},{8,12},{12,0},{1,5},{5,9},{9,13},{13,1},{2,6},{6,10},{... | collective-permute-start | bytes 491528 | tf_op jit(solution)/shard_map/ppermute | solution.py:24
  6.2 13.6 %collective-permute-start.2 = (bf16[128,640]{1,0:T(8,128)(2,1)}, bf16[128,640]{1,0:T(8,128)(2,1)S(1)}, u32[]{:S(2)}, u32[]{:S(2)}) collective-permute-start(bf16[128,640]{1,0:T(8,128)(2,1)} %get-tuple-element.42), channel_id=1, source_target_pairs={{0,8},{4,12},{8,0},{12,4},{1,9},{5,13},{9,1},{13,5},{2,10},{6,14},... | collective-permute-start | bytes 491528 | tf_op jit(solution)/shard_map/ppermute | solution.py:24
  8.8 11.0 %collective-permute-start.4 = (bf16[128,640]{1,0:T(8,128)(2,1)}, bf16[128,640]{1,0:T(8,128)(2,1)S(1)}, u32[]{:S(2)}, u32[]{:S(2)}) collective-permute-start(bf16[128,640]{1,0:T(8,128)(2,1)} %get-tuple-element.43), channel_id=1, source_target_pairs={{0,12},{4,0},{8,4},{12,8},{1,13},{5,1},{9,5},{13,9},{2,14},{6,2},{... | collective-permute-start | bytes 491528 | tf_op jit(solution)/shard_map/ppermute | solution.py:24
  13.6 8.2 %collective-permute-start.1 = (bf16[128,640]{1,0:T(8,128)(2,1)S(1)}, bf16[128,640]{1,0:T(8,128)(2,1)S(1)}, u32[]{:S(2)}, u32[]{:S(2)}) collective-permute-start(bf16[128,640]{1,0:T(8,128)(2,1)S(1)} %collective-permute-done.refs_2_), channel_id=1, source_target_pairs={{0,1},{1,0},{2,3},{3,2},{4,5},{5,4},{6,7},{7,6},{8,9},{9,8},{10,11... | collective-permute-start | bytes 491528 | tf_op jit(solution)/shard_map/ppermute | solution.py:24
  19.7 2.0 %collective-permute-start.3 = (bf16[128,640]{1,0:T(8,128)(2,1)S(1)}, bf16[128,640]{1,0:T(8,128)(2,1)S(1)}, u32[]{:S(2)}, u32[]{:S(2)}) collective-permute-start(bf16[128,640]{1,0:T(8,128)(2,1)S(1)} %collective-permute-done.2.refs_4_), channel_id=1, source_target_pairs={{0,1},{1,0},{2,3},{3,2},{4,5},{5,4},{6,7},{7,6},{8,9},{9,8},{10,11... | collective-permute-start | bytes 491528 | tf_op jit(solution)/shard_map/ppermute | solution.py:24
  19.8 2.0 %collective-permute-start.5 = (bf16[128,640]{1,0:T(8,128)(2,1)S(1)}, bf16[128,640]{1,0:T(8,128)(2,1)S(1)}, u32[]{:S(2)}, u32[]{:S(2)}) collective-permute-start(bf16[128,640]{1,0:T(8,128)(2,1)S(1)} %collective-permute-done.4.refs_6_), channel_id=1, source_target_pairs={{0,1},{1,0},{2,3},{3,2},{4,5},{5,4},{6,7},{7,6},{8,9},{9,8},{10,11... | collective-permute-start | bytes 491528 | tf_op jit(solution)/shard_map/ppermute | solution.py:24
  29.3 3.0 %collective-permute-start.7 = (bf16[4,128,320]{2,1,0:T(8,128)(2,1)S(1)}, bf16[4,128,320]{2,1,0:T(8,128)(2,1)S(1)}, u32[]{:S(2)}, u32[]{:S(2)}) collective-permute-start(bf16[4,128,320]{2,1,0:T(8,128)(2,1)S(1)} %get-tuple-element.50), channel_id=1, source_target_pairs={{0,1},{1,0},{2,3},{3,2},{4,5},{5,4},{6,7},{7,6},{8,9},{9,8},{10,11... | collective-permute-start | bytes 983048 | tf_op jit(solution)/shard_map/ppermute | solution.py:24
  30.7 15.4 %collective-permute-start.6 = (bf16[4,80,640]{2,1,0:T(8,128)(2,1)S(1)}, bf16[4,80,640]{2,1,0:T(8,128)(2,1)S(1)}, u32[]{:S(2)}, u32[]{:S(2)}) collective-permute-start(bf16[4,80,640]{2,1,0:T(8,128)(2,1)S(1)} %get-tuple-element.48), channel_id=1, source_target_pairs={{0,2},{2,0},{1,3},{3,1},{4,6},{6,4},{5,7},{7,5},{8,10},{10,8},{9,1... | collective-permute-start | bytes 1228808 | tf_op jit(solution)/shard_map/ppermute | solution.py:24
  33.2 18.2 %collective-permute-start.14 = (bf16[4,80,640]{2,1,0:T(8,128)(2,1)S(1)}, bf16[4,80,640]{2,1,0:T(8,128)(2,1)S(1)}, u32[]{:S(2)}, u32[]{:S(2)}) collective-permute-start(bf16[4,80,640]{2,1,0:T(8,128)(2,1)S(1)} %get-tuple-element.68), channel_id=1, source_target_pairs={{0,2},{2,0},{1,3},{3,1},{4,6},{6,4},{5,7},{7,5},{8,10},{10,8},{9,1... | collective-permute-start | bytes 1228808 | tf_op jit(solution)/shard_map/ppermute | solution.py:24
  33.8 8.8 %collective-permute-start.8 = (bf16[128,320]{1,0:T(8,128)(2,1)S(1)}, bf16[128,320]{1,0:T(8,128)(2,1)S(1)}, u32[]{:S(2)}, u32[]{:S(2)}) collective-permute-start(bf16[128,320]{1,0:T(8,128)(2,1)S(1)} %get-tuple-element.52), channel_id=1, source_target_pairs={{0,4},{4,8},{8,12},{12,0},{1,5},{5,9},{9,13},{13,1},{2,6},{6,10},{... | collective-permute-start | bytes 245768 | tf_op jit(solution)/shard_map/ppermute | solution.py:24
  37.8 8.3 %collective-permute-start.9 = (bf16[128,320]{1,0:T(8,128)(2,1)S(1)}, bf16[128,320]{1,0:T(8,128)(2,1)S(1)}, u32[]{:S(2)}, u32[]{:S(2)}) collective-permute-start(bf16[128,320]{1,0:T(8,128)(2,1)S(1)} %get-tuple-element.53), channel_id=1, source_target_pairs={{0,8},{4,12},{8,0},{12,4},{1,9},{5,13},{9,1},{13,5},{2,10},{6,14},... | collective-permute-start | bytes 245768 | tf_op jit(solution)/shard_map/ppermute | solution.py:24
  39.4 6.7 %collective-permute-start.10 = (bf16[128,320]{1,0:T(8,128)(2,1)S(1)}, bf16[128,320]{1,0:T(8,128)(2,1)S(1)}, u32[]{:S(2)}, u32[]{:S(2)}) collective-permute-start(bf16[128,320]{1,0:T(8,128)(2,1)S(1)} %get-tuple-element.54), channel_id=1, source_target_pairs={{0,12},{4,0},{8,4},{12,8},{1,13},{5,1},{9,5},{13,9},{2,14},{6,2},{... | collective-permute-start | bytes 245768 | tf_op jit(solution)/shard_map/ppermute | solution.py:24
  46.2 11.0 %collective-permute-start.11 = (bf16[80,640]{1,0:T(8,128)(2,1)S(1)}, bf16[80,640]{1,0:T(8,128)(2,1)S(1)}, u32[]{:S(2)}, u32[]{:S(2)}) collective-permute-start(bf16[80,640]{1,0:T(8,128)(2,1)S(1)} %get-tuple-element.62), channel_id=1, source_target_pairs={{0,4},{4,8},{8,12},{12,0},{1,5},{5,9},{9,13},{13,1},{2,6},{6,10},{... | collective-permute-start | bytes 307208 | tf_op jit(solution)/shard_map/ppermute | solution.py:24
  48.8 9.7 %collective-permute-start.12 = (bf16[80,640]{1,0:T(8,128)(2,1)S(1)}, bf16[80,640]{1,0:T(8,128)(2,1)S(1)}, u32[]{:S(2)}, u32[]{:S(2)}) collective-permute-start(bf16[80,640]{1,0:T(8,128)(2,1)S(1)} %get-tuple-element.63), channel_id=1, source_target_pairs={{0,8},{4,12},{8,0},{12,4},{1,9},{5,13},{9,1},{13,5},{2,10},{6,14},... | collective-permute-start | bytes 307208 | tf_op jit(solution)/shard_map/ppermute | solution.py:24
  49.8 8.8 %collective-permute-start.13 = (bf16[80,640]{1,0:T(8,128)(2,1)S(1)}, bf16[80,640]{1,0:T(8,128)(2,1)S(1)}, u32[]{:S(2)}, u32[]{:S(2)}) collective-permute-start(bf16[80,640]{1,0:T(8,128)(2,1)S(1)} %get-tuple-element.64), channel_id=1, source_target_pairs={{0,12},{4,0},{8,4},{12,8},{1,13},{5,1},{9,5},{13,9},{2,14},{6,2},{... | collective-permute-start | bytes 307208 | tf_op jit(solution)/shard_map/ppermute | solution.py:24
  51.5 8.9 %collective-permute-start.15 = (bf16[80,640]{1,0:T(8,128)(2,1)S(1)}, bf16[80,640]{1,0:T(8,128)(2,1)S(1)}, u32[]{:S(2)}, u32[]{:S(2)}) collective-permute-start(bf16[80,640]{1,0:T(8,128)(2,1)S(1)} %get-tuple-element.70), channel_id=1, source_target_pairs={{0,4},{4,8},{8,12},{12,0},{1,5},{5,9},{9,13},{13,1},{2,6},{6,10},{... | collective-permute-start | bytes 307208 | tf_op jit(solution)/shard_map/ppermute | solution.py:24
  55.1 10.9 %collective-permute-start.16 = (bf16[80,640]{1,0:T(8,128)(2,1)S(1)}, bf16[80,640]{1,0:T(8,128)(2,1)S(1)}, u32[]{:S(2)}, u32[]{:S(2)}) collective-permute-start(bf16[80,640]{1,0:T(8,128)(2,1)S(1)} %get-tuple-element.71), channel_id=1, source_target_pairs={{0,8},{4,12},{8,0},{12,4},{1,9},{5,13},{9,1},{13,5},{2,10},{6,14},... | collective-permute-start | bytes 307208 | tf_op jit(solution)/shard_map/ppermute | solution.py:24
  57.2 8.8 %collective-permute-start.17 = (bf16[80,640]{1,0:T(8,128)(2,1)S(1)}, bf16[80,640]{1,0:T(8,128)(2,1)S(1)}, u32[]{:S(2)}, u32[]{:S(2)}) collective-permute-start(bf16[80,640]{1,0:T(8,128)(2,1)S(1)} %get-tuple-element.72), channel_id=1, source_target_pairs={{0,12},{4,0},{8,4},{12,8},{1,13},{5,1},{9,5},{13,9},{2,14},{6,2},{... | collective-permute-start | bytes 307208 | tf_op jit(solution)/shard_map/ppermute | solution.py:24

commit v3 on v2

--- a/solution.py
+++ b/solution.py
@@ -10,7 +10,6 @@
 
 H = 8
 VMEM = pl.BlockSpec(memory_space=pltpu.VMEM)
-HBM = pl.BlockSpec(memory_space=pltpu.HBM)
 BF16 = jnp.bfloat16
 F32 = jnp.float32
 
@@ -53,70 +52,11 @@
     return jnp.where(col == source, 1.0, 0.0).astype(BF16)
 
 
-def fetch(ref, owner, width, into, sem):
-    start = pl.multiple_of(owner * width, width)
-    return [
-        pltpu.make_async_copy(ref.at[f, pl.ds(start, width), :], into.at[f], sem)
-        for f in range(into.shape[0])
-    ]
-
-
-def block_of(ref, owner, width):
-    return ref.at[:, pl.ds(pl.multiple_of(owner * width, width), width), :]
-
-
-def turned(order, rows):
-    frames, width, channels = rows.shape
-    return dot_nn(order, rows.reshape(frames * width, channels)).astype(BF16)
-
-
-def send_kernel(count, width, lat_ref, cot_ref, *refs):
-    sends, rows_ref, sems = refs[: count - 1], refs[count - 1], refs[count]
-    me = lax.axis_index("tm")
-    core = lax.axis_index("sub")
-
-    def copies(ref):
-        return [
-            pltpu.make_async_copy(
-                block_of(ref, lax.rem(me + step, count), width),
-                rows_ref.at[step - 1],
-                sems.at[step - 1],
-            )
-            for step in range(1, count)
-        ]
-
-    def move(ref):
-        moves = copies(ref)
-        for copy in moves:
-            copy.start()
-        order = by_position(rows_ref.shape[1], width)
-        for step, copy in enumerate(moves):
-            copy.wait()
-            sends[step][...] = turned(order, rows_ref[step])
-
-    @pl.when(core == 0)
-    def _():
-        move(lat_ref)
-
-    @pl.when(core != 0)
-    def _():
-        move(cot_ref)
-
-
-def table_kernel(frames, owners, bias_ref, lat_ref, cot_ref, table_ref, own_lat, own_cot, *scratch):
+def table_kernel(frames, owners, bias_ref, table_ref):
     heads, lanes = bias_ref.shape
     group = table_ref.shape[0]
     span = frames // owners
     me = lax.axis_index("tm")
-    copies = []
-    if scratch:
-        rows_ref, sems = scratch
-        width = rows_ref.shape[2]
-        for at, ref in enumerate((lat_ref, cot_ref)):
-            copies.append(
-                pltpu.make_async_copy(block_of(ref, me, width), rows_ref.at[at], sems.at[at])
-            )
-            copies[-1].start()
 
     def place_of(index):
         return lax.rem(lax.div(index, span), group // frames)
@@ -142,36 +82,19 @@
         skewed = pltpu.roll(spread, (1 - frames) % lanes, 1, stride=1, stride_axis=0)
         turned_bias = exact(left, exact(skewed[:, :group], right))
         table_ref[:, h * group : (h + 1) * group] = jnp.where(same, turned_bias, -1e30)
-    if scratch:
-        order = by_position(span, width)
-        for at, ref in enumerate((own_lat, own_cot)):
-            copies[at].wait()
-            ref[...] = turned(order, rows_ref[at])
-    else:
-        own_lat[...] = lat_ref[...]
-        own_cot[...] = cot_ref[...]
-
-
-def send_blocks(latents, cotangent, count):
-    frames, positions, channels = latents.shape
+
+
+def send_blocks(latents, cotangent, count, parts):
+    frames, positions, _ = latents.shape
     width = positions // count
-    if width % 16 == 0:
-        shape = jax.ShapeDtypeStruct((frames * width, channels), BF16)
-        return pl.pallas_call(
-            functools.partial(send_kernel, count, width),
-            out_shape=[shape] * (count - 1),
-            in_specs=[HBM] * 2,
-            out_specs=[VMEM] * (count - 1),
-            scratch_shapes=[
-                pltpu.VMEM((count - 1, frames, width, channels), BF16),
-                pltpu.SemaphoreType.DMA((count - 1,)),
-            ],
-            compiler_params=params(60 << 20),
-            name="send_blocks",
-        )(latents, cotangent)
     me = lax.axis_index("tm")
     sent = jnp.where(lax.axis_index("sub") == 0, latents, cotangent)
-    return [cut(sent, lax.rem(me + step, count), width) for step in range(1, count)]
+    blocks = [cut(sent, lax.rem(me + step, count), width) for step in range(1, count)]
+    first, sends = 0, []
+    for part in parts:
+        sends.append([b[first : first + frames * part] for b in blocks])
+        first += frames * part
+    return sends
 
 
 def cut(array, owner, width):
@@ -179,30 +102,18 @@
     return jnp.swapaxes(block, 0, 1).reshape(-1, array.shape[2])
 
 
-def tables(time_bias, latents, cotangent, heads, owners, group):
-    span, positions, channels = latents.shape
-    frames, width = span * owners, positions // owners
-    first = lax.axis_index("sub") * heads
-    own = jnp.flip(lax.dynamic_slice_in_dim(time_bias, first, heads, 0), 1)
+def bias_of_rows(time_bias, heads, frames, owners, group):
+    own = lax.dynamic_slice_in_dim(time_bias, lax.axis_index("sub") * heads, heads, 0)
     lanes = -(-max(2 * frames - 1, group) // 128) * 128
     own = jnp.pad(own, ((0, 0), (0, lanes - own.shape[1])))
-    scratch, specs = [], [VMEM] * 3
-    if width % 16 == 0:
-        scratch = [pltpu.VMEM((2, span, width, channels), BF16), pltpu.SemaphoreType.DMA((2,))]
-        specs = [VMEM, HBM, HBM]
-    else:
-        me = lax.axis_index("tm")
-        latents, cotangent = cut(latents, me, width), cut(cotangent, me, width)
-    rows = jax.ShapeDtypeStruct((span * width, channels), BF16)
     return pl.pallas_call(
         functools.partial(table_kernel, frames, owners),
-        out_shape=[jax.ShapeDtypeStruct((group, heads * group), F32), rows, rows],
-        in_specs=specs,
-        out_specs=[VMEM] * 3,
-        scratch_shapes=scratch,
-        compiler_params=params(),
-        name="tables",
-    )(own, latents, cotangent)
+        out_shape=jax.ShapeDtypeStruct((group, heads * group), F32),
+        in_specs=[VMEM],
+        out_specs=VMEM,
+        compiler_params=params(),
+        name="bias_of_rows",
+    )(own)
 
 
 def attend_kernel(owners, heads, *refs):
@@ -236,8 +147,9 @@
         cot_ref[at, :] = cot
 
     hidden = hidden_ref[...]
+    qkv = dot_nt(hidden, w_qkv_ref[...].reshape(3 * width, channels)).astype(BF16)
     for t, ref in enumerate((q_ref, k_ref, v_ref)):
-        ref[...] = dot_nt(hidden, w_qkv_ref[t]).astype(BF16)
+        ref[...] = qkv[:, t * width : (t + 1) * width]
     g_ref[...] = dot_nt(cot_ref[...], w_out_ref[...]).astype(BF16)
 
     lane = lax.broadcasted_iota(jnp.int32, (group, width), 1)
@@ -263,25 +175,18 @@
                 ref[at, :] = value[k * piece : (k + 1) * piece, :]
 
         query, key, value, grad = rows_of(q_ref), rows_of(k_ref), rows_of(v_ref), rows_of(g_ref)
-        keys, values = stack(key), stack(value)
-        scores = dot_nt(query, keys) * inv_root + table_ref[...]
-        grad_probs = dot_nt(grad, values)
-        low, grad_scores = [], []
-        for h in range(heads):
-            part = slice(h * group, (h + 1) * group)
-            own = scores[:, part]
-            raw = jnp.exp(own - jnp.max(own, axis=1, keepdims=True))
-            probs = raw / jnp.sum(raw, axis=1, keepdims=True)
-            up = grad_probs[:, part]
-            row_dot = jnp.sum(probs * up, axis=1, keepdims=True)
-            low.append(probs.astype(BF16))
-            grad_scores.append((probs * (up - row_dot) * inv_root).astype(BF16))
-        low = jnp.concatenate(low, axis=1)
-        grad_scores = jnp.concatenate(grad_scores, axis=1)
-        attn_out = dot_nn(low, values)
-        grad_query = dot_nn(grad_scores, keys)
-        grad_key = dot_nn(flip(grad_scores), stack(query))
-        grad_value = dot_nn(flip(low), stack(grad))
+        queries, grads = stack(query), stack(grad)
+        scores = dot_nt(key, queries) * inv_root + table_ref[...]
+        grad_probs = dot_nt(value, grads)
+        raw = jnp.exp(scores - jnp.max(scores, axis=0, keepdims=True))
+        probs = raw / jnp.sum(raw, axis=0, keepdims=True)
+        row_dot = jnp.sum(probs * grad_probs, axis=0, keepdims=True)
+        low = probs.astype(BF16)
+        grad_scores = (probs * (grad_probs - row_dot) * inv_root).astype(BF16)
+        grad_key = dot_nn(grad_scores, queries)
+        grad_value = dot_nn(low, grads)
+        grad_query = dot_nn(flip(grad_scores), stack(key))
+        attn_out = dot_nn(flip(low), stack(value))
         put(dqk_ref, jnp.concatenate([grad_query, grad_key], axis=1).astype(BF16))
         put(dvo_ref, jnp.concatenate([grad_value, attn_out], axis=1).astype(BF16))
 
@@ -330,14 +235,21 @@
     )(*inputs, pe, table, w_qkv, w_out)
 
 
-def weight_kernel(owners, sides, block, count, *refs):
-    lefts, grad_ref, outs = refs[:count], refs[count], refs[count + 1 :]
+def weight_kernel(owners, sides, block, parts, count, *refs):
+    grads, lefts, outs = refs[:parts], refs[parts : parts + count], refs[parts + count :]
     me, side = lax.axis_index("tm"), lax.axis_index("rows")
-    grads = grad_ref[...]
-    full = dot_tn(lefts[0][...], grads)
-    if count == 2:
+    values = [ref[...] for ref in grads]
+
+    def product(lefts):
+        total = dot_tn(lefts[0][...], values[0])
+        for left, value in zip(lefts[1:], values[1:]):
+            total = total + dot_tn(left[...], value)
+        return total
+
+    full = product(lefts[:parts])
+    if count > parts:
         lane = lax.broadcasted_iota(jnp.int32, full.shape, 1)
-        full = jnp.where(lane < full.shape[1] // 2, full, dot_tn(lefts[1][...], grads))
+        full = jnp.where(lane < full.shape[1] // 2, full, product(lefts[parts:]))
     if block % 16:
         outs[0][...] = full
         return
@@ -354,8 +266,8 @@
                     outs[j][slot] = piece if j == 0 else piece.astype(BF16)
 
 
-def weight_terms(lefts, grads, owners, sides):
-    channels, columns = lefts[0].shape[1], grads.shape[1]
+def weight_terms(grads, lefts, owners, sides):
+    channels, columns = lefts[0].shape[1], grads[0].shape[1]
     block = channels // (owners * sides)
     if block % 16 == 0:
         keep = jax.ShapeDtypeStruct((owners, block, columns), F32)
@@ -363,13 +275,13 @@
     else:
         outs = [jax.ShapeDtypeStruct((channels, columns), F32)]
     result = pl.pallas_call(
-        functools.partial(weight_kernel, owners, sides, block, len(lefts)),
+        functools.partial(weight_kernel, owners, sides, block, len(grads), len(lefts)),
         out_shape=outs,
-        in_specs=[VMEM] * (len(lefts) + 1),
+        in_specs=[VMEM] * (len(grads) + len(lefts)),
         out_specs=[VMEM] * len(outs),
         compiler_params=params(),
         name="weight_terms",
-    )(*lefts, grads)
+    )(*grads, *lefts)
     if block % 16 == 0:
         return result[0], list(result[1:])
     full = result[0].reshape(owners, sides, block, columns)
@@ -387,9 +299,9 @@
         outs[slot][...] = total.astype(outs[slot].dtype)
 
 
-def combine(keep, arrived, own_dtype):
+def combine(keep, arrived):
     owners = keep.shape[0]
-    outs = [jax.ShapeDtypeStruct(keep.shape[1:], own_dtype)]
+    outs = [jax.ShapeDtypeStruct(keep.shape[1:], F32)]
     outs += [jax.ShapeDtypeStruct(keep.shape[1:], BF16)] * (owners - 1)
     result = pl.pallas_call(
         combine_kernel,
@@ -400,6 +312,28 @@
         name="combine",
     )(keep, *arrived)
     return result[0], result[1:]
+
+
+def join_kernel(parts, *refs):
+    keeps, arrived, outs = refs[:parts], refs[parts : 2 * parts], refs[2 * parts :]
+    for slot, out in enumerate(outs):
+        sums = [keep[slot] + ref[slot].astype(F32) for keep, ref in zip(keeps, arrived)]
+        total = jnp.concatenate(sums, axis=0)
+        half = total.shape[0] // 2
+        out[...] = jnp.concatenate([total[:half], total[half:]], axis=1).astype(BF16)
+
+
+def join(keeps, arrived):
+    owners, _, width = keeps[0].shape
+    rows = sum(keep.shape[1] for keep in keeps)
+    return pl.pallas_call(
+        functools.partial(join_kernel, len(keeps)),
+        out_shape=[jax.ShapeDtypeStruct((rows // 2, 2 * width), BF16)] * owners,
+        in_specs=[VMEM] * (2 * len(keeps)),
+        out_specs=[VMEM] * owners,
+        compiler_params=params(),
+        name="join",
+    )(*keeps, *arrived)
 
 
 def finish_kernel(count, *refs):
@@ -445,13 +379,18 @@
     order = by_position(frames, width, back=True)
     for step, ref in enumerate(blocks):
         start = pl.multiple_of(lax.rem(me - step + count, count) * width, width)
-        rows = dot_nn(order, ref[...]).astype(BF16)
+        rows = dot_nn(order, unfold(ref[...])).astype(BF16)
         out_ref[:, pl.ds(start, width), :] = rows.reshape(frames, width, channels)
+
+
+def unfold(block):
+    channels = block.shape[1] // 2
+    return jnp.concatenate([block[:, :channels], block[:, channels:]], axis=0)
 
 
 def place(blocks, frames):
     count = len(blocks)
-    chunk, channels = blocks[0].shape
+    chunk, channels = 2 * blocks[0].shape[0], blocks[0].shape[1] // 2
     width = chunk // frames
     if width % 16 == 0:
         return pl.pallas_call(
@@ -462,7 +401,8 @@
             compiler_params=params(),
             name="place",
         )(*blocks)
-    ordered = jnp.roll(jnp.stack(blocks[::-1]), lax.axis_index("tm") + 1, 0)
+    ordered = jnp.stack([unfold(b) for b in blocks[::-1]])
+    ordered = jnp.roll(ordered, lax.axis_index("tm") + 1, 0)
     ordered = ordered.reshape(count, width, frames, channels)
     return jnp.transpose(ordered, (2, 0, 1, 3)).reshape(frames, count * width, channels)
 
@@ -475,32 +415,39 @@
     group = max(frames, 128)
     me = lax.axis_index("tm")
 
-    sends = send_blocks(latents, cotangent, owners)
-    table, own_lat, own_cot = tables(time_bias, latents, cotangent, heads, owners, group)
+    parts = [positions // owners]
+
+    sends = send_blocks(latents, cotangent, owners, parts)
+    table = bias_of_rows(time_bias, heads, frames, owners, group)
+    own_lat, own_cot = ([cut(a, me, positions // owners)] for a in (latents, cotangent))
     owner = lax.rem(me - jnp.arange(owners, dtype=jnp.int32) + owners, owners)
     frame_pos = owner[:, None] * span + jnp.arange(span, dtype=jnp.int32)[None]
     pe = positional(frame_pos.reshape(-1), channels)
-    inputs = [own_lat, own_cot]
-    for step, block in enumerate(sends):
-        mine = shift_send(block, "tm", step + 1)
-        inputs += [mine, shift_send(mine, "sub", 1)]
-    hidden, cot, grad_qk, grad_vo, back_keep, back_send = attend(
-        inputs, pe, table, jnp.transpose(w_qkv, (1, 2, 0)), w_out, owners, heads
-    )
-
-    own_back, back_blocks = combine(back_keep, [shift_send(back_send, "sub", 1)], BF16)
+    w_rows = jnp.transpose(w_qkv, (1, 2, 0))
+    results = []
+    for at, blocks in enumerate(sends):
+        inputs = [own_lat[at], own_cot[at]]
+        for step, block in enumerate(blocks):
+            mine = shift_send(block, "tm", step + 1)
+            inputs += [mine, shift_send(mine, "sub", 1)]
+        results.append(attend(inputs, pe, table, w_rows, w_out, owners, heads))
+    hidden, cot, grad_qk, grad_vo, back_keep, back_send = (list(r) for r in zip(*results))
+
+    back_send = lax.optimization_barrier(back_send)
+    back_blocks = join(back_keep, [shift_send(b, "sub", 1) for b in back_send])
+    own_back = back_blocks[0]
     back_blocks = [own_back] + [
-        shift_send(block, "tm", step + 1) for step, block in enumerate(back_blocks)
+        shift_send(block, "tm", step + 1) for step, block in enumerate(back_blocks[1:])
     ]
     sums = []
-    for lefts, grads in (((hidden, cot), grad_vo), ((hidden,), grad_qk)):
+    for lefts, grads in ((hidden + cot, grad_vo), (hidden, grad_qk)):
         if grads is grad_qk:
-            grads, _ = lax.optimization_barrier((grads, own_back))
-        keep, side_blocks = weight_terms(lefts, grads, owners, sides)
+            grads, own_back = lax.optimization_barrier((grads, own_back))
+        keep, side_blocks = weight_terms(grads, lefts, owners, sides)
         arrived = [shift_send(b, "rows", j + 1) for j, b in enumerate(side_blocks)]
         if grads is grad_vo:
             arrived, back_blocks = lax.optimization_barrier((arrived, back_blocks))
-        own, blocks = combine(keep, arrived, F32)
+        own, blocks = combine(keep, arrived)
         sums.append([own] + [shift_send(b, "tm", step + 1) for step, b in enumerate(blocks)])
     grad_w_qkv, grad_w_out_t = finish(*sums)
     return (place(back_blocks, span), grad_w_qkv, grad_w_out_t)

time: 67.1 us -> 63.6 us (0.948)
  Pallas kernels: 15.5 us -> 12.1 us
  waiting for transfers between devices: 22.8 us -> 20.8 us
  other arithmetic: 0.43 us -> 1.6 us
  local copies, waits for them, and re-layouts: 0.22 us -> 1.37 us
    pallas_call x2, Pallas kernels: 3.73 us -> 0.96 us  [the longest x1 0.83 us: bias_of_rows(): pl.pallas_call(functools.partial(table_kernel, frames, owners), out_shape...]
    ppermute x18, waiting for transfers between devices: 22.8 us -> 20.8 us  [shift_send(): lax.ppermute(array, axis, [(i, (i + step) % size) for i in range(size)])]
    transpose x0 -> x7, local copies, waits for them, and re-layouts: none -> 1.26 us  [cut(): return jnp.swapaxes(block, 0, 1).reshape(-1, array.shape[2])]
    select_n x0 -> x1, other arithmetic: none -> 1.17 us  [send_blocks(): sent = jnp.where(lax.axis_index('sub') == 0, latents, cotangent)]
  transfers between devices with their start and end apart: 18 -> 18, of which waited for: 7 -> 9; matrix products, arithmetic and copies ran while one was open for 1% -> 3% of each run, Pallas kernels for 7% -> 7%
where the time goes in v3:
time: 63.6 us; the launch traced here: 63.4 us
  starting transfers between devices  26.7 us (42%)
  waiting for transfers between devices  20.8 us (33%)
  Pallas kernels  12.1 us (19%)
  other arithmetic  1.6 us (3%)
  local copies, waits for them, and re-layouts  1.37 us (2%)
  between operations  0.8 us (1%)
    ppermute x18, starting transfers between devices, shift_send(): lax.ppermute(array, axis, [(i, (i + step) % size) for i in range(size)])  26.7 us
    ppermute x18, waiting for transfers between devices, shift_send(): lax.ppermute(array, axis, [(i, (i + step) % size) for i in range(size)])  20.8 us
    pallas_call x1, Pallas kernels, attend(): pl.pallas_call(functools.partial(attend_kernel, owners, heads), out_shape...  6.81 us
    pallas_call x2, Pallas kernels, weight_terms(): pl.pallas_call(functools.partial(weight_kernel, owners, sides, block, len...  2.2 us
  transfers between devices with their start and end apart: 18, of which 9 were waited for; matrix products, arithmetic and copies ran while one was open for 3% of the time, Pallas kernels for 7%

profile of v3, /device:TPU:0, one launch (start us, length us, event | category | flops | bytes accessed | tf_op | source)
XLA Modules:
  0.0 63.4 jit_solution(11925863345812465053)
XLA Ops:
  0.7 1.2 %broadcast_select_fusion = bf16[8,64,640]{2,1,0:T(8,128)(2,1)S(1)} fusion(bf16[8,64,640]{2,1,0:T(8,128)(2,1)} %param.5, bf16[8,64,640]{2,1,0:T(8,128)(2,1)} %param.6, pred[]{:T(512)S(6)} %eq.3), kind=kLoop, calls=%fused_computation | loop fusion | flops 327680 | bytes 1966081 | tf_op jit(solution)/shard_map/jit(_where)/select_n | solution.py:91
  2.0 3.1 %collective-permute-start = (bf16[128,640]{1,0:T(8,128)(2,1)S(1)}, bf16[128,640]{1,0:T(8,128)(2,1)S(1)}, u32[]{:S(2)}, u32[]{:S(2)}) collective-permute-start(bf16[128,640]{1,0:T(8,128)(2,1)S(1)} %bitcast.32), channel_id=1, source_target_pairs={{0,4},{4,8},{8,12},{12,0},{1,5},{5,9},{9,13},{13,1},{2,6},{6,10},{... | collective-permute-start | bytes 491528 | tf_op jit(solution)/shard_map/ppermute | solution.py:23
  5.1 2.7 %collective-permute-start.2 = (bf16[128,640]{1,0:T(8,128)(2,1)S(1)}, bf16[128,640]{1,0:T(8,128)(2,1)S(1)}, u32[]{:S(2)}, u32[]{:S(2)}) collective-permute-start(bf16[128,640]{1,0:T(8,128)(2,1)S(1)} %bitcast.31), channel_id=1, source_target_pairs={{0,8},{4,12},{8,0},{12,4},{1,9},{5,13},{9,1},{13,5},{2,10},{6,14},... | collective-permute-start | bytes 491528 | tf_op jit(solution)/shard_map/ppermute | solution.py:23
  7.8 1.4 %collective-permute-start.4 = (bf16[128,640]{1,0:T(8,128)(2,1)S(1)}, bf16[128,640]{1,0:T(8,128)(2,1)S(1)}, u32[]{:S(2)}, u32[]{:S(2)}) collective-permute-start(bf16[128,640]{1,0:T(8,128)(2,1)S(1)} %bitcast.30), channel_id=1, source_target_pairs={{0,12},{4,0},{8,4},{12,8},{1,13},{5,1},{9,5},{13,9},{2,14},{6,2},{... | collective-permute-start | bytes 491528 | tf_op jit(solution)/shard_map/ppermute | solution.py:23
  9.6 1.0 %dynamic-slice_bitcast_fusion.3 = (bf16[16,8,640]{2,0,1:T(8,128)(2,1)S(1)}, bf16[16,8,640]{2,0,1:T(8,128)(2,1)S(1)}) fusion(bf16[8,64,640]{2,1,0:T(8,128)(2,1)} %param.6, s32[]{:T(128)S(6)} %select_n.24, bf16[8,64,640]{2,1,0:T(8,128)(2,1)} %param.5), kind=kLoop, calls=%fused_computation.9 | loop fusion | bytes 655364 | tf_op jit(solution)/shard_map/transpose | solution.py:102
  10.6 1.5 %collective-permute-done.refs_2_ = bf16[128,640]{1,0:T(8,128)(2,1)S(1)} collective-permute-done((bf16[128,640]{1,0:T(8,128)(2,1)S(1)}, bf16[128,640]{1,0:T(8,128)(2,1)S(1)}, u32[]{:S(2)}, u32[]{:S(2)}) %collective-permute-start) | collective-permute-done | bytes 163872 | tf_op jit(solution)/shard_map/ppermute | solution.py:23
  12.2 6.2 %collective-permute-done.2.refs_4_ = bf16[128,640]{1,0:T(8,128)(2,1)S(1)} collective-permute-done((bf16[128,640]{1,0:T(8,128)(2,1)S(1)}, bf16[128,640]{1,0:T(8,128)(2,1)S(1)}, u32[]{:S(2)}, u32[]{:S(2)}) %collective-permute-start.2) | collective-permute-done | bytes 163872 | tf_op jit(solution)/shard_map/ppermute | solution.py:23
  18.4 0.5 collective-permute-start.5
  18.9 0.8 %bias_of_rows.1.refs_9_ = f32[128,512]{1,0:T(8,128)S(1)} custom-call(f32[4,128]{1,0:T(4,128)S(1)} %pad.4.bias_ref), custom_call_target="tpu_custom_call" | custom-call | tf_op jit(solution)/shard_map/bias_of_rows/pallas_call | solution.py:109
  20.0 6.8 %attend.1 = (bf16[512,640]{1,0:T(8,128)(2,1)S(1)}, bf16[512,640]{1,0:T(8,128)(2,1)S(1)}, bf16[512,640]{1,0:T(8,128)(2,1)S(1)}, bf16[512,640]{1,0:T(8,128)(2,1)S(...) custom-call(bf16[128,640]{1,0:T(8,128)(2,1)S(1)} %bitcast.28, bf16[128,640]{1,0:T(8,128)(2,1)S(1)} %bitcast.27, ...), custom_call_target="tpu_custom_call" | custom-call | tf_op jit(solution)/shard_map/attend/pallas_call | solution.py:227
  26.8 0.4 collective-permute-start.7
  27.2 1.3 %weight_terms.2 = (f32[4,80,640]{2,1,0:T(8,128)S(1)}, bf16[4,80,640]{2,1,0:T(8,128)(2,1)S(1)}) custom-call(bf16[512,640]{1,0:T(8,128)(2,1)S(1)} %get-tuple-element.33.refs_0_, bf16[512,640]{1,0:T(8,128)(2,1)S(1)} %get-tuple-element.34.refs_1_, bf16[512,640]{1,0:T(8,128)(2,1)S(1)} %get-tuple-element.35.refs_2_), custom_call_target="tpu_custom_call" | custom-call | tf_op jit(solution)/shard_map/weight_terms/pallas_call | solution.py:277
  28.6 1.5 %collective-permute-start.6 = (bf16[4,80,640]{2,1,0:T(8,128)(2,1)S(1)}, bf16[4,80,640]{2,1,0:T(8,128)(2,1)S(1)}, u32[]{:S(2)}, u32[]{:S(2)}) collective-permute-start(bf16[4,80,640]{2,1,0:T(8,128)(2,1)S(1)} %get-tuple-element.36), channel_id=1, source_target_pairs={{0,2},{2,0},{1,3},{3,1},{4,6},{6,4},{5,7},{7,5},{8,10},{10,8},{9,1... | collective-permute-start | bytes 1228808 | tf_op jit(solution)/shard_map/ppermute | solution.py:23
  30.2 0.9 %weight_terms.3 = (f32[4,80,640]{2,1,0:T(8,128)S(1)}, bf16[4,80,640]{2,1,0:T(8,128)(2,1)S(1)}) custom-call(bf16[512,640]{1,0:T(8,128)(2,1)S(1)} %get-tuple-element.54.refs_0_, bf16[512,640]{1,0:T(8,128)(2,1)S(1)} %get-tuple-element.34.refs_1_), custom_call_target="tpu_custom_call" | custom-call | tf_op jit(solution)/shard_map/weight_terms/pallas_call | solution.py:277
  31.1 0.6 collective-permute-start.14
  31.7 3.6 %collective-permute-start.8 = (bf16[64,640]{1,0:T(8,128)(2,1)S(1)}, bf16[64,640]{1,0:T(8,128)(2,1)S(1)}, u32[]{:S(2)}, u32[]{:S(2)}) collective-permute-start(bf16[64,640]{1,0:T(8,128)(2,1)S(1)} %get-tuple-element.40), channel_id=1, source_target_pairs={{0,4},{4,8},{8,12},{12,0},{1,5},{5,9},{9,13},{13,1},{2,6},{6,10},{... | collective-permute-start | bytes 245768 | tf_op jit(solution)/shard_map/ppermute | solution.py:23
  35.3 2.0 %collective-permute-start.9 = (bf16[64,640]{1,0:T(8,128)(2,1)S(1)}, bf16[64,640]{1,0:T(8,128)(2,1)S(1)}, u32[]{:S(2)}, u32[]{:S(2)}) collective-permute-start(bf16[64,640]{1,0:T(8,128)(2,1)S(1)} %get-tuple-element.41), channel_id=1, source_target_pairs={{0,8},{4,12},{8,0},{12,4},{1,9},{5,13},{9,1},{13,5},{2,10},{6,14},... | collective-permute-start | bytes 245768 | tf_op jit(solution)/shard_map/ppermute | solution.py:23
  37.3 0.4 collective-permute-start.10
  37.7 2.4 %collective-permute-done.8.refs_1_ = bf16[64,640]{1,0:T(8,128)(2,1)S(1)} collective-permute-done((bf16[64,640]{1,0:T(8,128)(2,1)S(1)}, bf16[64,640]{1,0:T(8,128)(2,1)S(1)}, u32[]{:S(2)}, u32[]{:S(2)}) %collective-permute-start.8) | collective-permute-done | bytes 81952 | tf_op jit(solution)/shard_map/ppermute | solution.py:23
  40.1 2.5 %collective-permute-done.9.refs_2_ = bf16[64,640]{1,0:T(8,128)(2,1)S(1)} collective-permute-done((bf16[64,640]{1,0:T(8,128)(2,1)S(1)}, bf16[64,640]{1,0:T(8,128)(2,1)S(1)}, u32[]{:S(2)}, u32[]{:S(2)}) %collective-permute-start.9) | collective-permute-done | bytes 81952 | tf_op jit(solution)/shard_map/ppermute | solution.py:23
  42.6 0.4 collective-permute-done.10.refs_3_
  43.1 1.9 %collective-permute-start.11 = (bf16[80,640]{1,0:T(8,128)(2,1)S(1)}, bf16[80,640]{1,0:T(8,128)(2,1)S(1)}, u32[]{:S(2)}, u32[]{:S(2)}) collective-permute-start(bf16[80,640]{1,0:T(8,128)(2,1)S(1)} %get-tuple-element.50), channel_id=1, source_target_pairs={{0,4},{4,8},{8,12},{12,0},{1,5},{5,9},{9,13},{13,1},{2,6},{6,10},{... | collective-permute-start | bytes 307208 | tf_op jit(solution)/shard_map/ppermute | solution.py:23
  45.0 1.7 %collective-permute-start.12 = (bf16[80,640]{1,0:T(8,128)(2,1)S(1)}, bf16[80,640]{1,0:T(8,128)(2,1)S(1)}, u32[]{:S(2)}, u32[]{:S(2)}) collective-permute-start(bf16[80,640]{1,0:T(8,128)(2,1)S(1)} %get-tuple-element.51), channel_id=1, source_target_pairs={{0,8},{4,12},{8,0},{12,4},{1,9},{5,13},{9,1},{13,5},{2,10},{6,14},... | collective-permute-start | bytes 307208 | tf_op jit(solution)/shard_map/ppermute | solution.py:23
  46.7 0.7 %collective-permute-start.13 = (bf16[80,640]{1,0:T(8,128)(2,1)S(1)}, bf16[80,640]{1,0:T(8,128)(2,1)S(1)}, u32[]{:S(2)}, u32[]{:S(2)}) collective-permute-start(bf16[80,640]{1,0:T(8,128)(2,1)S(1)} %get-tuple-element.52), channel_id=1, source_target_pairs={{0,12},{4,0},{8,4},{12,8},{1,13},{5,1},{9,5},{13,9},{2,14},{6,2},{... | collective-permute-start | bytes 307208 | tf_op jit(solution)/shard_map/ppermute | solution.py:23
  47.4 1.6 %collective-permute-done.14.refs_0_ = bf16[4,80,640]{2,1,0:T(8,128)(2,1)S(1)} collective-permute-done((bf16[4,80,640]{2,1,0:T(8,128)(2,1)S(1)}, bf16[4,80,640]{2,1,0:T(8,128)(2,1)S(1)}, u32[]{:S(2)}, u32[]{:S(2)}) %collective-permute-start.14) | collective-permute-done | bytes 409632 | tf_op jit(solution)/shard_map/ppermute | solution.py:23
  49.1 3.8 %collective-permute-start.15 = (bf16[80,640]{1,0:T(8,128)(2,1)S(1)}, bf16[80,640]{1,0:T(8,128)(2,1)S(1)}, u32[]{:S(2)}, u32[]{:S(2)}) collective-permute-start(bf16[80,640]{1,0:T(8,128)(2,1)S(1)} %get-tuple-element.58), channel_id=1, source_target_pairs={{0,4},{4,8},{8,12},{12,0},{1,5},{5,9},{9,13},{13,1},{2,6},{6,10},{... | collective-permute-start | bytes 307208 | tf_op jit(solution)/shard_map/ppermute | solution.py:23
  52.9 1.8 %collective-permute-start.16 = (bf16[80,640]{1,0:T(8,128)(2,1)S(1)}, bf16[80,640]{1,0:T(8,128)(2,1)S(1)}, u32[]{:S(2)}, u32[]{:S(2)}) collective-permute-start(bf16[80,640]{1,0:T(8,128)(2,1)S(1)} %get-tuple-element.59), channel_id=1, source_target_pairs={{0,8},{4,12},{8,0},{12,4},{1,9},{5,13},{9,1},{13,5},{2,10},{6,14},... | collective-permute-start | bytes 307208 | tf_op jit(solution)/shard_map/ppermute | solution.py:23
  54.7 0.6 collective-permute-start.17
  55.3 1.1 %place.1 = bf16[8,64,320]{2,1,0:T(8,128)(2,1)} custom-call(bf16[64,640]{1,0:T(8,128)(2,1)S(1)} %get-tuple-element.43.refs_0_, bf16[64,640]{1,0:T(8,128)(2,1)S(1)} %collective-permute-done.8.refs_1_, bf16[64,640]{1,0:T(8,128)(2,1)S(1)} %collective-permute-done.9.refs_2_, bf16[64,640]{1,0:T(8,128)(2,1)S(1)} %collective-permute-done.10.refs_3_), custom_call_target="tpu_custom_call" | custom-call | tf_op jit(solution)/shard_map/place/pallas_call | solution.py:396
  56.4 1.5 %collective-permute-done.15.refs_5_ = bf16[80,640]{1,0:T(8,128)(2,1)S(1)} collective-permute-done((bf16[80,640]{1,0:T(8,128)(2,1)S(1)}, bf16[80,640]{1,0:T(8,128)(2,1)S(1)}, u32[]{:S(2)}, u32[]{:S(2)}) %collective-permute-start.15) | collective-permute-done | bytes 102432 | tf_op jit(solution)/shard_map/ppermute | solution.py:23
  57.9 4.6 %collective-permute-done.16.refs_6_ = bf16[80,640]{1,0:T(8,128)(2,1)S(1)} collective-permute-done((bf16[80,640]{1,0:T(8,128)(2,1)S(1)}, bf16[80,640]{1,0:T(8,128)(2,1)S(1)}, u32[]{:S(2)}, u32[]{:S(2)}) %collective-permute-start.16) | collective-permute-done | bytes 102432 | tf_op jit(solution)/shard_map/ppermute | solution.py:23
  62.5 0.9 %finish.1 = (f32[3,80,320]{2,1,0:T(8,128)}, f32[80,320]{1,0:T(8,128)}) custom-call(f32[80,640]{1,0:T(8,128)S(1)} %get-tuple-element.49.refs_0_, bf16[80,640]{1,0:T(8,128)(2,1)S(1)} %collective-permute-done.11.refs_1_, bf16[80,640]{1,0:T(8,128)(2,1)S(1)} %collective-permute-done.12.refs_2_, bf16[80,640]{1,0:T(8,128)(2,1)S(1)} %collective-permute-done.13.refs_3_, ...), custom_call_target="tpu_custom_call" | custom-call | tf_op jit(solution)/shard_map/finish/pallas_call | solution.py:359
  (33 shorter events, 1.2 us)
Async XLA Ops:
  0.6 18.3 %copy-start = (f32[8,63]{1,0:T(8,128)S(1)}, f32[8,63]{1,0:T(8,128)}, u32[]{:S(2)}) copy-start(f32[8,63]{1,0:T(8,128)} %param.9) | copy-start | bytes 6052
  2.0 10.2 %collective-permute-start = (bf16[128,640]{1,0:T(8,128)(2,1)S(1)}, bf16[128,640]{1,0:T(8,128)(2,1)S(1)}, u32[]{:S(2)}, u32[]{:S(2)}) collective-permute-start(bf16[128,640]{1,0:T(8,128)(2,1)S(1)} %bitcast.32), channel_id=1, source_target_pairs={{0,4},{4,8},{8,12},{12,0},{1,5},{5,9},{9,13},{13,1},{2,6},{6,10},{... | collective-permute-start | bytes 491528 | tf_op jit(solution)/shard_map/ppermute | solution.py:23
  5.0 15.0 %copy-start.1 = (bf16[320,640]{1,0:T(8,128)(2,1)S(1)}, bf16[320,640]{1,0:T(8,128)(2,1)}, u32[]{:S(2)}) copy-start(bf16[320,640]{1,0:T(8,128)(2,1)} %refs_11_.1) | copy-start | bytes 1228804
  5.1 13.3 %collective-permute-start.2 = (bf16[128,640]{1,0:T(8,128)(2,1)S(1)}, bf16[128,640]{1,0:T(8,128)(2,1)S(1)}, u32[]{:S(2)}, u32[]{:S(2)}) collective-permute-start(bf16[128,640]{1,0:T(8,128)(2,1)S(1)} %bitcast.31), channel_id=1, source_target_pairs={{0,8},{4,12},{8,0},{12,4},{1,9},{5,13},{9,1},{13,5},{2,10},{6,14},... | collective-permute-start | bytes 491528 | tf_op jit(solution)/shard_map/ppermute | solution.py:23
  7.8 10.6 %collective-permute-start.4 = (bf16[128,640]{1,0:T(8,128)(2,1)S(1)}, bf16[128,640]{1,0:T(8,128)(2,1)S(1)}, u32[]{:S(2)}, u32[]{:S(2)}) collective-permute-start(bf16[128,640]{1,0:T(8,128)(2,1)S(1)} %bitcast.30), channel_id=1, source_target_pairs={{0,12},{4,0},{8,4},{12,8},{1,13},{5,1},{9,5},{13,9},{2,14},{6,2},{... | collective-permute-start | bytes 491528 | tf_op jit(solution)/shard_map/ppermute | solution.py:23
  12.2 7.7 %collective-permute-start.1 = (bf16[128,640]{1,0:T(8,128)(2,1)S(1)}, bf16[128,640]{1,0:T(8,128)(2,1)S(1)}, u32[]{:S(2)}, u32[]{:S(2)}) collective-permute-start(bf16[128,640]{1,0:T(8,128)(2,1)S(1)} %collective-permute-done.refs_2_), channel_id=1, source_target_pairs={{0,1},{1,0},{2,3},{3,2},{4,5},{5,4},{6,7},{7,6},{8,9},{9,8},{10,11... | collective-permute-start | bytes 491528 | tf_op jit(solution)/shard_map/ppermute | solution.py:23
  18.4 1.5 %collective-permute-start.3 = (bf16[128,640]{1,0:T(8,128)(2,1)S(1)}, bf16[128,640]{1,0:T(8,128)(2,1)S(1)}, u32[]{:S(2)}, u32[]{:S(2)}) collective-permute-start(bf16[128,640]{1,0:T(8,128)(2,1)S(1)} %collective-permute-done.2.refs_4_), channel_id=1, source_target_pairs={{0,1},{1,0},{2,3},{3,2},{4,5},{5,4},{6,7},{7,6},{8,9},{9,8},{10,11... | collective-permute-start | bytes 491528 | tf_op jit(solution)/shard_map/ppermute | solution.py:23
  18.4 1.6 %collective-permute-start.5 = (bf16[128,640]{1,0:T(8,128)(2,1)S(1)}, bf16[128,640]{1,0:T(8,128)(2,1)S(1)}, u32[]{:S(2)}, u32[]{:S(2)}) collective-permute-start(bf16[128,640]{1,0:T(8,128)(2,1)S(1)} %collective-permute-done.4.refs_6_), channel_id=1, source_target_pairs={{0,1},{1,0},{2,3},{3,2},{4,5},{5,4},{6,7},{7,6},{8,9},{9,8},{10,11... | collective-permute-start | bytes 491528 | tf_op jit(solution)/shard_map/ppermute | solution.py:23
  26.8 3.3 %collective-permute-start.7 = (bf16[4,128,320]{2,1,0:T(8,128)(2,1)S(1)}, bf16[4,128,320]{2,1,0:T(8,128)(2,1)S(1)}, u32[]{:S(2)}, u32[]{:S(2)}) collective-permute-start(bf16[4,128,320]{2,1,0:T(8,128)(2,1)S(1)} %get-tuple-element.38), channel_id=1, source_target_pairs={{0,1},{1,0},{2,3},{3,2},{4,5},{5,4},{6,7},{7,6},{8,9},{9,8},{10,11... | collective-permute-start | bytes 983048 | tf_op jit(solution)/shard_map/ppermute | solution.py:23
  28.6 14.4 %collective-permute-start.6 = (bf16[4,80,640]{2,1,0:T(8,128)(2,1)S(1)}, bf16[4,80,640]{2,1,0:T(8,128)(2,1)S(1)}, u32[]{:S(2)}, u32[]{:S(2)}) collective-permute-start(bf16[4,80,640]{2,1,0:T(8,128)(2,1)S(1)} %get-tuple-element.36), channel_id=1, source_target_pairs={{0,2},{2,0},{1,3},{3,1},{4,6},{6,4},{5,7},{7,5},{8,10},{10,8},{9,1... | collective-permute-start | bytes 1228808 | tf_op jit(solution)/shard_map/ppermute | solution.py:23
  31.1 17.9 %collective-permute-start.14 = (bf16[4,80,640]{2,1,0:T(8,128)(2,1)S(1)}, bf16[4,80,640]{2,1,0:T(8,128)(2,1)S(1)}, u32[]{:S(2)}, u32[]{:S(2)}) collective-permute-start(bf16[4,80,640]{2,1,0:T(8,128)(2,1)S(1)} %get-tuple-element.56), channel_id=1, source_target_pairs={{0,2},{2,0},{1,3},{3,1},{4,6},{6,4},{5,7},{7,5},{8,10},{10,8},{9,1... | collective-permute-start | bytes 1228808 | tf_op jit(solution)/shard_map/ppermute | solution.py:23
  31.7 8.4 %collective-permute-start.8 = (bf16[64,640]{1,0:T(8,128)(2,1)S(1)}, bf16[64,640]{1,0:T(8,128)(2,1)S(1)}, u32[]{:S(2)}, u32[]{:S(2)}) collective-permute-start(bf16[64,640]{1,0:T(8,128)(2,1)S(1)} %get-tuple-element.40), channel_id=1, source_target_pairs={{0,4},{4,8},{8,12},{12,0},{1,5},{5,9},{9,13},{13,1},{2,6},{6,10},{... | collective-permute-start | bytes 245768 | tf_op jit(solution)/shard_map/ppermute | solution.py:23
  35.3 7.3 %collective-permute-start.9 = (bf16[64,640]{1,0:T(8,128)(2,1)S(1)}, bf16[64,640]{1,0:T(8,128)(2,1)S(1)}, u32[]{:S(2)}, u32[]{:S(2)}) collective-permute-start(bf16[64,640]{1,0:T(8,128)(2,1)S(1)} %get-tuple-element.41), channel_id=1, source_target_pairs={{0,8},{4,12},{8,0},{12,4},{1,9},{5,13},{9,1},{13,5},{2,10},{6,14},... | collective-permute-start | bytes 245768 | tf_op jit(solution)/shard_map/ppermute | solution.py:23
  37.3 5.7 %collective-permute-start.10 = (bf16[64,640]{1,0:T(8,128)(2,1)S(1)}, bf16[64,640]{1,0:T(8,128)(2,1)S(1)}, u32[]{:S(2)}, u32[]{:S(2)}) collective-permute-start(bf16[64,640]{1,0:T(8,128)(2,1)S(1)} %get-tuple-element.42), channel_id=1, source_target_pairs={{0,12},{4,0},{8,4},{12,8},{1,13},{5,1},{9,5},{13,9},{2,14},{6,2},{... | collective-permute-start | bytes 245768 | tf_op jit(solution)/shard_map/ppermute | solution.py:23
  43.1 11.6 %collective-permute-start.11 = (bf16[80,640]{1,0:T(8,128)(2,1)S(1)}, bf16[80,640]{1,0:T(8,128)(2,1)S(1)}, u32[]{:S(2)}, u32[]{:S(2)}) collective-permute-start(bf16[80,640]{1,0:T(8,128)(2,1)S(1)} %get-tuple-element.50), channel_id=1, source_target_pairs={{0,4},{4,8},{8,12},{12,0},{1,5},{5,9},{9,13},{13,1},{2,6},{6,10},{... | collective-permute-start | bytes 307208 | tf_op jit(solution)/shard_map/ppermute | solution.py:23
  45.0 11.4 %collective-permute-start.12 = (bf16[80,640]{1,0:T(8,128)(2,1)S(1)}, bf16[80,640]{1,0:T(8,128)(2,1)S(1)}, u32[]{:S(2)}, u32[]{:S(2)}) collective-permute-start(bf16[80,640]{1,0:T(8,128)(2,1)S(1)} %get-tuple-element.51), channel_id=1, source_target_pairs={{0,8},{4,12},{8,0},{12,4},{1,9},{5,13},{9,1},{13,5},{2,10},{6,14},... | collective-permute-start | bytes 307208 | tf_op jit(solution)/shard_map/ppermute | solution.py:23
  46.7 9.7 %collective-permute-start.13 = (bf16[80,640]{1,0:T(8,128)(2,1)S(1)}, bf16[80,640]{1,0:T(8,128)(2,1)S(1)}, u32[]{:S(2)}, u32[]{:S(2)}) collective-permute-start(bf16[80,640]{1,0:T(8,128)(2,1)S(1)} %get-tuple-element.52), channel_id=1, source_target_pairs={{0,12},{4,0},{8,4},{12,8},{1,13},{5,1},{9,5},{13,9},{2,14},{6,2},{... | collective-permute-start | bytes 307208 | tf_op jit(solution)/shard_map/ppermute | solution.py:23
  49.1 8.9 %collective-permute-start.15 = (bf16[80,640]{1,0:T(8,128)(2,1)S(1)}, bf16[80,640]{1,0:T(8,128)(2,1)S(1)}, u32[]{:S(2)}, u32[]{:S(2)}) collective-permute-start(bf16[80,640]{1,0:T(8,128)(2,1)S(1)} %get-tuple-element.58), channel_id=1, source_target_pairs={{0,4},{4,8},{8,12},{12,0},{1,5},{5,9},{9,13},{13,1},{2,6},{6,10},{... | collective-permute-start | bytes 307208 | tf_op jit(solution)/shard_map/ppermute | solution.py:23
  52.9 9.6 %collective-permute-start.16 = (bf16[80,640]{1,0:T(8,128)(2,1)S(1)}, bf16[80,640]{1,0:T(8,128)(2,1)S(1)}, u32[]{:S(2)}, u32[]{:S(2)}) collective-permute-start(bf16[80,640]{1,0:T(8,128)(2,1)S(1)} %get-tuple-element.59), channel_id=1, source_target_pairs={{0,8},{4,12},{8,0},{12,4},{1,9},{5,13},{9,1},{13,5},{2,10},{6,14},... | collective-permute-start | bytes 307208 | tf_op jit(solution)/shard_map/ppermute | solution.py:23
  54.7 7.8 %collective-permute-start.17 = (bf16[80,640]{1,0:T(8,128)(2,1)S(1)}, bf16[80,640]{1,0:T(8,128)(2,1)S(1)}, u32[]{:S(2)}, u32[]{:S(2)}) collective-permute-start(bf16[80,640]{1,0:T(8,128)(2,1)S(1)} %get-tuple-element.60), channel_id=1, source_target_pairs={{0,12},{4,0},{8,4},{12,8},{1,13},{5,1},{9,5},{13,9},{2,14},{6,2},{... | collective-permute-start | bytes 307208 | tf_op jit(solution)/shard_map/ppermute | solution.py:23

commit v4 on v3

--- a/solution.py
+++ b/solution.py
@@ -84,17 +84,11 @@
         table_ref[:, h * group : (h + 1) * group] = jnp.where(same, turned_bias, -1e30)
 
 
-def send_blocks(latents, cotangent, count, parts):
-    frames, positions, _ = latents.shape
-    width = positions // count
+def send_blocks(latents, cotangent, count):
+    width = latents.shape[1] // count
     me = lax.axis_index("tm")
     sent = jnp.where(lax.axis_index("sub") == 0, latents, cotangent)
-    blocks = [cut(sent, lax.rem(me + step, count), width) for step in range(1, count)]
-    first, sends = 0, []
-    for part in parts:
-        sends.append([b[first : first + frames * part] for b in blocks])
-        first += frames * part
-    return sends
+    return [cut(sent, lax.rem(me + step, count), width) for step in range(1, count)]
 
 
 def cut(array, owner, width):
@@ -119,9 +113,9 @@
 def attend_kernel(owners, heads, *refs):
     parts = 2 * owners
     inputs, refs = refs[:parts], refs[parts:]
-    pe_ref, table_ref, w_qkv_ref, w_out_ref = refs[:4]
-    hidden_ref, cot_ref, dqk_ref, dvo_ref, back_keep, back_send = refs[4:10]
-    q_ref, k_ref, v_ref, g_ref = refs[10:]
+    pe_ref, table_ref, w_qkv_ref, w_out_ref, w_own_ref, w_other_ref = refs[:6]
+    hidden_ref, cot_ref, dqk_ref, dvo_ref, back_keep, back_send = refs[6:12]
+    q_ref, k_ref, v_ref, g_ref = refs[12:]
 
     core = lax.axis_index("sub")
     rows, channels = hidden_ref.shape
@@ -164,55 +158,47 @@
             [value[:, h * group : (h + 1) * group].T for h in range(heads)], axis=1
         )
 
-    for start in range(0, chunk, piece):
-        spans = [slice(k * chunk + start, k * chunk + start + piece) for k in range(owners)]
-
-        def rows_of(ref, spans=spans):
-            return jnp.concatenate([ref[at, :] for at in spans], axis=0)
-
-        def put(ref, value, spans=spans):
-            for k, at in enumerate(spans):
-                ref[at, :] = value[k * piece : (k + 1) * piece, :]
-
-        query, key, value, grad = rows_of(q_ref), rows_of(k_ref), rows_of(v_ref), rows_of(g_ref)
-        queries, grads = stack(query), stack(grad)
-        scores = dot_nt(key, queries) * inv_root + table_ref[...]
-        grad_probs = dot_nt(value, grads)
-        raw = jnp.exp(scores - jnp.max(scores, axis=0, keepdims=True))
-        probs = raw / jnp.sum(raw, axis=0, keepdims=True)
-        row_dot = jnp.sum(probs * grad_probs, axis=0, keepdims=True)
-        low = probs.astype(BF16)
-        grad_scores = (probs * (grad_probs - row_dot) * inv_root).astype(BF16)
-        grad_key = dot_nn(grad_scores, queries)
-        grad_value = dot_nn(low, grads)
-        grad_query = dot_nn(flip(grad_scores), stack(key))
-        attn_out = dot_nn(flip(low), stack(value))
-        put(dqk_ref, jnp.concatenate([grad_query, grad_key], axis=1).astype(BF16))
-        put(dvo_ref, jnp.concatenate([grad_value, attn_out], axis=1).astype(BF16))
-
-    grad_v = dvo_ref[:, :width]
-    back = dot_nn(dqk_ref[...], w_qkv_ref[0:2].reshape(2 * width, channels))
-    back = (back + dot_nn(grad_v, w_qkv_ref[2])).astype(BF16).astype(F32)
-    lower, upper = back[:, :width], back[:, width:]
-    cot = cot_ref[...].astype(F32)
-
-    def store(own, other, base):
+    def rows_of(ref, start):
+        return jnp.concatenate(
+            [ref[k * chunk + start : k * chunk + start + piece, :] for k in range(owners)], axis=0
+        )
+
+    def put(ref, start, *halves):
+        value = jnp.concatenate(halves, axis=1).astype(BF16)
         for k in range(owners):
-            slot = (owners - k) % owners
-            at = slice(k * chunk, (k + 1) * chunk)
-            back_keep[slot] = own[at, :] + base[at, :]
-            back_send[slot] = other[at, :].astype(BF16)
-
-    @pl.when(core == 0)
-    def _():
-        store(lower, upper, cot[:, :width])
-
-    @pl.when(core != 0)
-    def _():
-        store(upper, lower, cot[:, width:])
-
-
-def attend(inputs, pe, table, w_qkv, w_out, owners, heads):
+            at = k * chunk + start
+            ref[at : at + piece, :] = value[k * piece : (k + 1) * piece, :]
+
+    starts = list(range(0, chunk, piece))
+    wide = 2
+    for some in [starts[i : i + wide] for i in range(0, len(starts), wide)]:
+        rows = [[rows_of(ref, at) for ref in (q_ref, k_ref, v_ref, g_ref)] for at in some]
+        queries, grads = [stack(r[0]) for r in rows], [stack(r[3]) for r in rows]
+        scores = [dot_nt(r[1], q) * inv_root + table_ref[...] for r, q in zip(rows, queries)]
+        grad_probs = [dot_nt(r[2], g) for r, g in zip(rows, grads)]
+        raw = [jnp.exp(x - jnp.max(x, axis=0, keepdims=True)) for x in scores]
+        probs = [x / jnp.sum(x, axis=0, keepdims=True) for x in raw]
+        low = [p.astype(BF16) for p in probs]
+        grad_value = [dot_nn(p, g) for p, g in zip(low, grads)]
+        row_dot = [jnp.sum(p * u, axis=0, keepdims=True) for p, u in zip(probs, grad_probs)]
+        grad_scores = [
+            (p * (u - d) * inv_root).astype(BF16) for p, u, d in zip(probs, grad_probs, row_dot)
+        ]
+        attn_out = [dot_nn(flip(p), stack(r[2])) for p, r in zip(low, rows)]
+        grad_key = [dot_nn(d, q) for d, q in zip(grad_scores, queries)]
+        grad_query = [dot_nn(flip(d), stack(r[1])) for d, r in zip(grad_scores, rows)]
+        for n, at in enumerate(some):
+            put(dqk_ref, at, grad_query[n], grad_key[n])
+            put(dvo_ref, at, grad_value[n], attn_out[n])
+
+    grads = jnp.concatenate([dqk_ref[...], dvo_ref[:, :width]], axis=1)
+    for w_ref, back_ref in ((w_own_ref, back_keep), (w_other_ref, back_send)):
+        back = dot_nn(grads, w_ref[...]).astype(BF16)
+        for k in range(owners):
+            back_ref[(owners - k) % owners] = back[k * chunk : (k + 1) * chunk, :]
+
+
+def attend(inputs, pe, table, w_qkv, w_out, w_back, owners, heads):
     chunk, channels = inputs[0].shape
     rows = chunk * owners
     width = w_qkv.shape[1]
@@ -221,18 +207,18 @@
         jax.ShapeDtypeStruct((rows, channels), BF16),
         jax.ShapeDtypeStruct((rows, 2 * width), BF16),
         jax.ShapeDtypeStruct((rows, 2 * width), BF16),
-        jax.ShapeDtypeStruct((owners, chunk, width), F32),
+        jax.ShapeDtypeStruct((owners, chunk, width), BF16),
         jax.ShapeDtypeStruct((owners, chunk, width), BF16),
     ]
     return pl.pallas_call(
         functools.partial(attend_kernel, owners, heads),
         out_shape=outs,
-        in_specs=[VMEM] * (len(inputs) + 4),
+        in_specs=[VMEM] * (len(inputs) + 6),
         out_specs=[VMEM] * len(outs),
         scratch_shapes=[pltpu.VMEM((rows, width), BF16)] * 4,
         compiler_params=params(),
         name="attend",
-    )(*inputs, pe, table, w_qkv, w_out)
+    )(*inputs, pe, table, w_qkv, w_out, *w_back)
 
 
 def weight_kernel(owners, sides, block, parts, count, *refs):
@@ -240,30 +226,36 @@
     me, side = lax.axis_index("tm"), lax.axis_index("rows")
     values = [ref[...] for ref in grads]
 
-    def product(lefts):
-        total = dot_tn(lefts[0][...], values[0])
+    def product(lefts, columns):
+        total = dot_tn(lefts[0][...], values[0][:, columns])
         for left, value in zip(lefts[1:], values[1:]):
-            total = total + dot_tn(left[...], value)
+            total = total + dot_tn(left[...], value[:, columns])
         return total
 
-    full = product(lefts[:parts])
+    columns = values[0].shape[1]
     if count > parts:
-        lane = lax.broadcasted_iota(jnp.int32, full.shape, 1)
-        full = jnp.where(lane < full.shape[1] // 2, full, product(lefts[parts:]))
+        low, high = columns // 2 // 128 * 128, -(-(columns // 2) // 128) * 128
+        lower = product(lefts[:parts], slice(0, high))
+        upper = product(lefts[parts:], slice(low, columns))
+        pieces = [lower[:, :low]]
+        if high > low:
+            lane = lax.broadcasted_iota(jnp.int32, (lower.shape[0], high - low), 1) + low
+            shared = jnp.where(lane < columns // 2, lower[:, low:], upper[:, : high - low])
+            pieces.append(shared)
+        full = jnp.concatenate(pieces + [upper[:, high - low :]], axis=1)
+    else:
+        full = product(lefts, slice(0, columns))
     if block % 16:
         outs[0][...] = full
         return
     for z in range(owners):
         slot = lax.rem(z - me + owners, owners)
-        for x in range(sides):
-            first = (z * sides + x) * block
-            piece = full[first : first + block, :]
-            turn = lax.rem(x - side + sides, sides)
-            for j in range(sides):
-
-                @pl.when(turn == j)
-                def _(piece=piece, j=j, slot=slot):
-                    outs[j][slot] = piece if j == 0 else piece.astype(BF16)
+        rows = [full[(z * sides + x) * block :][:block] for x in range(sides)]
+        for j in range(sides):
+            turned = rows[j]
+            for shift in range(1, sides):
+                turned = jnp.where(side == shift, rows[(j + shift) % sides], turned)
+            outs[j][slot] = turned if j == 0 else turned.astype(BF16)
 
 
 def weight_terms(grads, lefts, owners, sides):
@@ -314,26 +306,23 @@
     return result[0], result[1:]
 
 
-def join_kernel(parts, *refs):
-    keeps, arrived, outs = refs[:parts], refs[parts : 2 * parts], refs[2 * parts :]
+def join_kernel(keep_ref, arrived_ref, *outs):
     for slot, out in enumerate(outs):
-        sums = [keep[slot] + ref[slot].astype(F32) for keep, ref in zip(keeps, arrived)]
-        total = jnp.concatenate(sums, axis=0)
+        total = keep_ref[slot].astype(F32) + arrived_ref[slot].astype(F32)
         half = total.shape[0] // 2
         out[...] = jnp.concatenate([total[:half], total[half:]], axis=1).astype(BF16)
 
 
-def join(keeps, arrived):
-    owners, _, width = keeps[0].shape
-    rows = sum(keep.shape[1] for keep in keeps)
+def join(keep, arrived):
+    owners, rows, width = keep.shape
     return pl.pallas_call(
-        functools.partial(join_kernel, len(keeps)),
+        join_kernel,
         out_shape=[jax.ShapeDtypeStruct((rows // 2, 2 * width), BF16)] * owners,
-        in_specs=[VMEM] * (2 * len(keeps)),
+        in_specs=[VMEM] * 2,
         out_specs=[VMEM] * owners,
         compiler_params=params(),
         name="join",
-    )(*keeps, *arrived)
+    )(keep, arrived)
 
 
 def finish_kernel(count, *refs):
@@ -371,7 +360,7 @@
 
 
 def place_kernel(*refs):
-    blocks, out_ref = refs[:-1], refs[-1]
+    blocks, cot_ref, out_ref = refs[:-2], refs[-2], refs[-1]
     count = len(blocks)
     frames, positions, channels = out_ref.shape
     width = positions // count
@@ -379,8 +368,9 @@
     order = by_position(frames, width, back=True)
     for step, ref in enumerate(blocks):
         start = pl.multiple_of(lax.rem(me - step + count, count) * width, width)
-        rows = dot_nn(order, unfold(ref[...])).astype(BF16)
-        out_ref[:, pl.ds(start, width), :] = rows.reshape(frames, width, channels)
+        rows = dot_nn(order, unfold(ref[...])).reshape(frames, width, channels)
+        at = pl.ds(start, width)
+        out_ref[:, at, :] = (cot_ref[:, at, :].astype(F32) + rows).astype(BF16)
 
 
 def unfold(block):
@@ -388,7 +378,8 @@
     return jnp.concatenate([block[:, :channels], block[:, channels:]], axis=0)
 
 
-def place(blocks, frames):
+def place(blocks, cot):
+    frames = cot.shape[0]
     count = len(blocks)
     chunk, channels = 2 * blocks[0].shape[0], blocks[0].shape[1] // 2
     width = chunk // frames
@@ -396,15 +387,16 @@
         return pl.pallas_call(
             place_kernel,
             out_shape=jax.ShapeDtypeStruct((frames, count * width, channels), BF16),
-            in_specs=[VMEM] * count,
+            in_specs=[VMEM] * (count + 1),
             out_specs=VMEM,
             compiler_params=params(),
             name="place",
-        )(*blocks)
+        )(*blocks, cot)
     ordered = jnp.stack([unfold(b) for b in blocks[::-1]])
     ordered = jnp.roll(ordered, lax.axis_index("tm") + 1, 0)
     ordered = ordered.reshape(count, width, frames, channels)
-    return jnp.transpose(ordered, (2, 0, 1, 3)).reshape(frames, count * width, channels)
+    moved = jnp.transpose(ordered, (2, 0, 1, 3)).reshape(frames, count * width, channels)
+    return (cot.astype(F32) + moved.astype(F32)).astype(BF16)
 
 
 def per_device(latents, cotangent, w_qkv, w_out, time_bias):
@@ -415,26 +407,31 @@
     group = max(frames, 128)
     me = lax.axis_index("tm")
 
-    parts = [positions // owners]
-
-    sends = send_blocks(latents, cotangent, owners, parts)
+    core = lax.axis_index("sub")
+    width = w_qkv.shape[2]
+
+    sends = send_blocks(latents, cotangent, owners)
     table = bias_of_rows(time_bias, heads, frames, owners, group)
-    own_lat, own_cot = ([cut(a, me, positions // owners)] for a in (latents, cotangent))
+    inputs = [cut(a, me, positions // owners) for a in (latents, cotangent)]
     owner = lax.rem(me - jnp.arange(owners, dtype=jnp.int32) + owners, owners)
     frame_pos = owner[:, None] * span + jnp.arange(span, dtype=jnp.int32)[None]
     pe = positional(frame_pos.reshape(-1), channels)
     w_rows = jnp.transpose(w_qkv, (1, 2, 0))
-    results = []
-    for at, blocks in enumerate(sends):
-        inputs = [own_lat[at], own_cot[at]]
-        for step, block in enumerate(blocks):
-            mine = shift_send(block, "tm", step + 1)
-            inputs += [mine, shift_send(mine, "sub", 1)]
-        results.append(attend(inputs, pe, table, w_rows, w_out, owners, heads))
-    hidden, cot, grad_qk, grad_vo, back_keep, back_send = (list(r) for r in zip(*results))
-
-    back_send = lax.optimization_barrier(back_send)
-    back_blocks = join(back_keep, [shift_send(b, "sub", 1) for b in back_send])
+    w_flat = w_rows.reshape(3 * width, channels)
+    w_back = [
+        lax.dynamic_slice_in_dim(w_flat, which * width, width, 1) for which in (core, 1 - core)
+    ]
+    for step, block in enumerate(sends):
+        mine = shift_send(block, "tm", step + 1)
+        if step == 0:
+            mine, w_back = lax.optimization_barrier((mine, w_back))
+        inputs += [mine, shift_send(mine, "sub", 1)]
+    hidden, cot, grad_qk, grad_vo, back_keep, back_send = attend(
+        inputs, pe, table, w_rows, w_out, w_back, owners, heads
+    )
+    hidden, cot, grad_qk, grad_vo = [hidden], [cot], [grad_qk], [grad_vo]
+
+    back_blocks = join(back_keep, shift_send(back_send, "sub", 1))
     own_back = back_blocks[0]
     back_blocks = [own_back] + [
         shift_send(block, "tm", step + 1) for step, block in enumerate(back_blocks[1:])
@@ -446,11 +443,14 @@
         keep, side_blocks = weight_terms(grads, lefts, owners, sides)
         arrived = [shift_send(b, "rows", j + 1) for j, b in enumerate(side_blocks)]
         if grads is grad_vo:
-            arrived, back_blocks = lax.optimization_barrier((arrived, back_blocks))
+            arrived, back_blocks[1] = lax.optimization_barrier((arrived, back_blocks[1]))
+            arrived, back_blocks[2] = lax.optimization_barrier((arrived, back_blocks[2]))
+            arrived, back_blocks[3] = lax.optimization_barrier((arrived, back_blocks[3]))
         own, blocks = combine(keep, arrived)
         sums.append([own] + [shift_send(b, "tm", step + 1) for step, b in enumerate(blocks)])
     grad_w_qkv, grad_w_out_t = finish(*sums)
-    return (place(back_blocks, span), grad_w_qkv, grad_w_out_t)
+    own_cot = lax.dynamic_slice_in_dim(cotangent, core * width, width, 2)
+    return (place(back_blocks, own_cot), grad_w_qkv, grad_w_out_t)
 
 
 def solution(mesh):

time: 63.6 us -> 62.6 us (0.984)
  local copies, waits for them, and re-layouts: 1.37 us -> 3.04 us
  waiting for transfers between devices: 20.8 us -> 19.3 us
  Pallas kernels: 12.1 us -> 10.8 us
    dynamic_slice x0 -> x2, local copies, waits for them, and re-layouts: none -> 1.74 us  [the longest x1 1.53 us: per_device(): lax.dynamic_slice_in_dim(w_flat, which * width, width, 1)]
    ppermute x18, waiting for transfers between devices: 20.8 us -> 19.3 us  [shift_send(): lax.ppermute(array, axis, [(i, (i + step) % size) for i in range(size)])]
    pallas_call x1, Pallas kernels: 6.81 us -> 6.13 us  [attend(): pl.pallas_call(functools.partial(attend_kernel, owners, heads), out_shape...]
  transfers between devices with their start and end apart: 18 -> 18, of which waited for: 9 -> 9; matrix products, arithmetic and copies ran while one was open for 3% -> 5% of each run, Pallas kernels for 7% -> 6%
where the time goes in v4:
time: 62.6 us; the launch traced here: 62.4 us
  starting transfers between devices  26.9 us (43%)
  waiting for transfers between devices  19.3 us (31%)
  Pallas kernels  10.8 us (17%)
  local copies, waits for them, and re-layouts  3.04 us (5%)
  other arithmetic  1.6 us (3%)
  between operations  0.83 us (1%)
    ppermute x18, starting transfers between devices, shift_send(): lax.ppermute(array, axis, [(i, (i + step) % size) for i in range(size)])  26.9 us
    ppermute x18, waiting for transfers between devices, shift_send(): lax.ppermute(array, axis, [(i, (i + step) % size) for i in range(size)])  19.3 us
    pallas_call x1, Pallas kernels, attend(): pl.pallas_call(functools.partial(attend_kernel, owners, heads), out_shape...  6.13 us
    pallas_call x2, Pallas kernels, weight_terms(): pl.pallas_call(functools.partial(weight_kernel, owners, sides, block, len...  1.59 us
    dynamic_slice x1, local copies, waits for them, and re-layouts, per_device(): lax.dynamic_slice_in_dim(w_flat, which * width, width, 1)  1.53 us
  transfers between devices with their start and end apart: 18, of which 9 were waited for; matrix products, arithmetic and copies ran while one was open for 5% of the time, Pallas kernels for 6%

profile of v4, /device:TPU:0, one launch (start us, length us, event | category | flops | bytes accessed | tf_op | source)
XLA Modules:
  0.0 62.4 jit_solution(5693761321343732438)
XLA Ops:
  0.7 1.2 %broadcast_select_fusion = bf16[8,64,640]{2,1,0:T(8,128)(2,1)S(1)} fusion(bf16[8,64,640]{2,1,0:T(8,128)(2,1)} %param.5, bf16[8,64,640]{2,1,0:T(8,128)(2,1)} %param.6, pred[]{:T(512)S(6)} %eq.3), kind=kLoop, calls=%fused_computation | loop fusion | flops 327680 | bytes 1966081 | tf_op jit(solution)/shard_map/jit(_where)/select_n | solution.py:90
  2.0 3.1 %collective-permute-start = (bf16[128,640]{1,0:T(8,128)(2,1)S(1)}, bf16[128,640]{1,0:T(8,128)(2,1)S(1)}, u32[]{:S(2)}, u32[]{:S(2)}) collective-permute-start(bf16[128,640]{1,0:T(8,128)(2,1)S(1)} %bitcast.35), channel_id=1, source_target_pairs={{0,4},{4,8},{8,12},{12,0},{1,5},{5,9},{9,13},{13,1},{2,6},{6,10},{... | collective-permute-start | bytes 491528 | tf_op jit(solution)/shard_map/ppermute | solution.py:23
  5.1 2.7 %collective-permute-start.2 = (bf16[128,640]{1,0:T(8,128)(2,1)S(1)}, bf16[128,640]{1,0:T(8,128)(2,1)S(1)}, u32[]{:S(2)}, u32[]{:S(2)}) collective-permute-start(bf16[128,640]{1,0:T(8,128)(2,1)S(1)} %bitcast.34), channel_id=1, source_target_pairs={{0,8},{4,12},{8,0},{12,4},{1,9},{5,13},{9,1},{13,5},{2,10},{6,14},... | collective-permute-start | bytes 491528 | tf_op jit(solution)/shard_map/ppermute | solution.py:23
  7.8 1.4 %collective-permute-start.4 = (bf16[128,640]{1,0:T(8,128)(2,1)S(1)}, bf16[128,640]{1,0:T(8,128)(2,1)S(1)}, u32[]{:S(2)}, u32[]{:S(2)}) collective-permute-start(bf16[128,640]{1,0:T(8,128)(2,1)S(1)} %bitcast.33), channel_id=1, source_target_pairs={{0,12},{4,0},{8,4},{12,8},{1,13},{5,1},{9,5},{13,9},{2,14},{6,2},{... | collective-permute-start | bytes 491528 | tf_op jit(solution)/shard_map/ppermute | solution.py:23
  9.6 1.0 %dynamic-slice_bitcast_fusion.3 = (bf16[16,8,640]{2,0,1:T(8,128)(2,1)S(1)}, bf16[16,8,640]{2,0,1:T(8,128)(2,1)S(1)}) fusion(bf16[8,64,640]{2,1,0:T(8,128)(2,1)S(1)} %copy-done.3, s32[]{:T(128)S(6)} %select_n.31, bf16[8,64,640]{2,1,0:T(8,128)(2,1)} %param.5), kind=kLoop, calls=%fused_computation.9 | loop fusion | bytes 655364 | tf_op jit(solution)/shard_map/transpose | solution.py:96
  10.6 1.5 %constant_dynamic-slice_fusion.2 = (bf16[960,320]{1,0:T(8,128)(2,1)}, bf16[960,320]{1,0:T(8,128)(2,1)S(1)}) fusion(bf16[960,640]{1,0:T(8,128)(2,1)S(1)} %bitcast.32, s32[]{:T(128)S(6)} %select_n.36, s32[]{:T(128)S(6)} %select_n.35), kind=kLoop, calls=%fused_computation.16 | loop fusion | bytes 2457608 | tf_op jit(solution)/shard_map/dynamic_slice | solution.py:422
  12.2 6.2 %collective-permute-done.2.refs_4_ = bf16[128,640]{1,0:T(8,128)(2,1)S(1)} collective-permute-done((bf16[128,640]{1,0:T(8,128)(2,1)S(1)}, bf16[128,640]{1,0:T(8,128)(2,1)S(1)}, u32[]{:S(2)}, u32[]{:S(2)}) %collective-permute-start.2) | collective-permute-done | bytes 163872 | tf_op jit(solution)/shard_map/ppermute | solution.py:23
  18.4 0.5 collective-permute-start.5
  19.0 0.8 %bias_of_rows.1.refs_9_ = f32[128,512]{1,0:T(8,128)S(1)} custom-call(f32[4,128]{1,0:T(4,128)S(1)} %pad.4.bias_ref), custom_call_target="tpu_custom_call" | custom-call | tf_op jit(solution)/shard_map/bias_of_rows/pallas_call | solution.py:103
  20.0 6.1 %attend.1 = (bf16[512,640]{1,0:T(8,128)(2,1)S(1)}, bf16[512,640]{1,0:T(8,128)(2,1)S(1)}, bf16[512,640]{1,0:T(8,128)(2,1)S(1)}, bf16[512,640]{1,0:T(8,128)(2,1)S(...) custom-call(bf16[128,640]{1,0:T(8,128)(2,1)S(1)} %bitcast.30, bf16[128,640]{1,0:T(8,128)(2,1)S(1)} %bitcast.29, ...), custom_call_target="tpu_custom_call" | custom-call | tf_op jit(solution)/shard_map/attend/pallas_call | solution.py:213
  26.2 0.3 collective-permute-start.6
  26.5 0.9 %weight_terms.2 = (f32[4,80,640]{2,1,0:T(8,128)S(1)}, bf16[4,80,640]{2,1,0:T(8,128)(2,1)S(1)}) custom-call(bf16[512,640]{1,0:T(8,128)(2,1)S(1)} %get-tuple-element.43.refs_0_, bf16[512,640]{1,0:T(8,128)(2,1)S(1)} %get-tuple-element.44.refs_1_, bf16[512,640]{1,0:T(8,128)(2,1)S(1)} %get-tuple-element.45.refs_2_), custom_call_target="tpu_custom_call" | custom-call | tf_op jit(solution)/shard_map/weight_terms/pallas_call | solution.py:269
  27.4 1.6 %collective-permute-start.7 = (bf16[4,80,640]{2,1,0:T(8,128)(2,1)S(1)}, bf16[4,80,640]{2,1,0:T(8,128)(2,1)S(1)}, u32[]{:S(2)}, u32[]{:S(2)}) collective-permute-start(bf16[4,80,640]{2,1,0:T(8,128)(2,1)S(1)} %get-tuple-element.46), channel_id=1, source_target_pairs={{0,2},{2,0},{1,3},{3,1},{4,6},{6,4},{5,7},{7,5},{8,10},{10,8},{9,1... | collective-permute-start | bytes 1228808 | tf_op jit(solution)/shard_map/ppermute | solution.py:23
  29.1 0.7 %weight_terms.3 = (f32[4,80,640]{2,1,0:T(8,128)S(1)}, bf16[4,80,640]{2,1,0:T(8,128)(2,1)S(1)}) custom-call(bf16[512,640]{1,0:T(8,128)(2,1)S(1)} %get-tuple-element.62.refs_0_, bf16[512,640]{1,0:T(8,128)(2,1)S(1)} %get-tuple-element.44.refs_1_), custom_call_target="tpu_custom_call" | custom-call | tf_op jit(solution)/shard_map/weight_terms/pallas_call | solution.py:269
  29.8 0.6 collective-permute-start.14
  30.4 3.7 %collective-permute-start.8 = (bf16[64,640]{1,0:T(8,128)(2,1)S(1)}, bf16[64,640]{1,0:T(8,128)(2,1)S(1)}, u32[]{:S(2)}, u32[]{:S(2)}) collective-permute-start(bf16[64,640]{1,0:T(8,128)(2,1)S(1)} %get-tuple-element.47), channel_id=1, source_target_pairs={{0,4},{4,8},{8,12},{12,0},{1,5},{5,9},{9,13},{13,1},{2,6},{6,10},{... | collective-permute-start | bytes 245768 | tf_op jit(solution)/shard_map/ppermute | solution.py:23
  34.1 1.9 %collective-permute-start.9 = (bf16[64,640]{1,0:T(8,128)(2,1)S(1)}, bf16[64,640]{1,0:T(8,128)(2,1)S(1)}, u32[]{:S(2)}, u32[]{:S(2)}) collective-permute-start(bf16[64,640]{1,0:T(8,128)(2,1)S(1)} %get-tuple-element.50), channel_id=1, source_target_pairs={{0,8},{4,12},{8,0},{12,4},{1,9},{5,13},{9,1},{13,5},{2,10},{6,14},... | collective-permute-start | bytes 245768 | tf_op jit(solution)/shard_map/ppermute | solution.py:23
  36.0 0.5 collective-permute-start.10
  36.5 3.3 %collective-permute-done.7.refs_0_ = bf16[4,80,640]{2,1,0:T(8,128)(2,1)S(1)} collective-permute-done((bf16[4,80,640]{2,1,0:T(8,128)(2,1)S(1)}, bf16[4,80,640]{2,1,0:T(8,128)(2,1)S(1)}, u32[]{:S(2)}, u32[]{:S(2)}) %collective-permute-start.7) | collective-permute-done | bytes 409632 | tf_op jit(solution)/shard_map/ppermute | solution.py:23
  39.8 1.8 %collective-permute-done.9.refs_2_ = bf16[64,640]{1,0:T(8,128)(2,1)S(1)} collective-permute-done((bf16[64,640]{1,0:T(8,128)(2,1)S(1)}, bf16[64,640]{1,0:T(8,128)(2,1)S(1)}, u32[]{:S(2)}, u32[]{:S(2)}) %collective-permute-start.9) | collective-permute-done | bytes 81952 | tf_op jit(solution)/shard_map/ppermute | solution.py:23
  41.6 0.3 collective-permute-done.10.refs_3_
  42.0 2.0 %collective-permute-start.11 = (bf16[80,640]{1,0:T(8,128)(2,1)S(1)}, bf16[80,640]{1,0:T(8,128)(2,1)S(1)}, u32[]{:S(2)}, u32[]{:S(2)}) collective-permute-start(bf16[80,640]{1,0:T(8,128)(2,1)S(1)} %get-tuple-element.58), channel_id=1, source_target_pairs={{0,4},{4,8},{8,12},{12,0},{1,5},{5,9},{9,13},{13,1},{2,6},{6,10},{... | collective-permute-start | bytes 307208 | tf_op jit(solution)/shard_map/ppermute | solution.py:23
  44.0 1.6 %collective-permute-start.12 = (bf16[80,640]{1,0:T(8,128)(2,1)S(1)}, bf16[80,640]{1,0:T(8,128)(2,1)S(1)}, u32[]{:S(2)}, u32[]{:S(2)}) collective-permute-start(bf16[80,640]{1,0:T(8,128)(2,1)S(1)} %get-tuple-element.59), channel_id=1, source_target_pairs={{0,8},{4,12},{8,0},{12,4},{1,9},{5,13},{9,1},{13,5},{2,10},{6,14},... | collective-permute-start | bytes 307208 | tf_op jit(solution)/shard_map/ppermute | solution.py:23
  45.5 0.9 %collective-permute-start.13 = (bf16[80,640]{1,0:T(8,128)(2,1)S(1)}, bf16[80,640]{1,0:T(8,128)(2,1)S(1)}, u32[]{:S(2)}, u32[]{:S(2)}) collective-permute-start(bf16[80,640]{1,0:T(8,128)(2,1)S(1)} %get-tuple-element.60), channel_id=1, source_target_pairs={{0,12},{4,0},{8,4},{12,8},{1,13},{5,1},{9,5},{13,9},{2,14},{6,2},{... | collective-permute-start | bytes 307208 | tf_op jit(solution)/shard_map/ppermute | solution.py:23
  46.4 1.4 %collective-permute-done.14.refs_0_ = bf16[4,80,640]{2,1,0:T(8,128)(2,1)S(1)} collective-permute-done((bf16[4,80,640]{2,1,0:T(8,128)(2,1)S(1)}, bf16[4,80,640]{2,1,0:T(8,128)(2,1)S(1)}, u32[]{:S(2)}, u32[]{:S(2)}) %collective-permute-start.14) | collective-permute-done | bytes 409632 | tf_op jit(solution)/shard_map/ppermute | solution.py:23
  47.9 3.8 %collective-permute-start.15 = (bf16[80,640]{1,0:T(8,128)(2,1)S(1)}, bf16[80,640]{1,0:T(8,128)(2,1)S(1)}, u32[]{:S(2)}, u32[]{:S(2)}) collective-permute-start(bf16[80,640]{1,0:T(8,128)(2,1)S(1)} %get-tuple-element.66), channel_id=1, source_target_pairs={{0,4},{4,8},{8,12},{12,0},{1,5},{5,9},{9,13},{13,1},{2,6},{6,10},{... | collective-permute-start | bytes 307208 | tf_op jit(solution)/shard_map/ppermute | solution.py:23
  51.7 1.9 %collective-permute-start.16 = (bf16[80,640]{1,0:T(8,128)(2,1)S(1)}, bf16[80,640]{1,0:T(8,128)(2,1)S(1)}, u32[]{:S(2)}, u32[]{:S(2)}) collective-permute-start(bf16[80,640]{1,0:T(8,128)(2,1)S(1)} %get-tuple-element.67), channel_id=1, source_target_pairs={{0,8},{4,12},{8,0},{12,4},{1,9},{5,13},{9,1},{13,5},{2,10},{6,14},... | collective-permute-start | bytes 307208 | tf_op jit(solution)/shard_map/ppermute | solution.py:23
  53.6 0.6 collective-permute-start.17
  54.4 1.1 %place.1 = bf16[8,64,320]{2,1,0:T(8,128)(2,1)} custom-call(bf16[64,640]{1,0:T(8,128)(2,1)S(1)} %get-tuple-element.42.refs_0_, bf16[64,640]{1,0:T(8,128)(2,1)S(1)} %collective-permute-done.8.refs_1_, bf16[64,640]{1,0:T(8,128)(2,1)S(1)} %collective-permute-done.9.refs_2_, bf16[64,640]{1,0:T(8,128)(2,1)S(1)} %collective-permute-done.10.refs_3_, ...), custom_call_target="tpu_custom_call" | custom-call | tf_op jit(solution)/shard_map/place/pallas_call | solution.py:387
  55.5 1.3 %collective-permute-done.15.refs_5_ = bf16[80,640]{1,0:T(8,128)(2,1)S(1)} collective-permute-done((bf16[80,640]{1,0:T(8,128)(2,1)S(1)}, bf16[80,640]{1,0:T(8,128)(2,1)S(1)}, u32[]{:S(2)}, u32[]{:S(2)}) %collective-permute-start.15) | collective-permute-done | bytes 102432 | tf_op jit(solution)/shard_map/ppermute | solution.py:23
  56.8 4.7 %collective-permute-done.16.refs_6_ = bf16[80,640]{1,0:T(8,128)(2,1)S(1)} collective-permute-done((bf16[80,640]{1,0:T(8,128)(2,1)S(1)}, bf16[80,640]{1,0:T(8,128)(2,1)S(1)}, u32[]{:S(2)}, u32[]{:S(2)}) %collective-permute-start.16) | collective-permute-done | bytes 102432 | tf_op jit(solution)/shard_map/ppermute | solution.py:23
  61.5 0.9 %finish.1 = (f32[3,80,320]{2,1,0:T(8,128)}, f32[80,320]{1,0:T(8,128)}) custom-call(f32[80,640]{1,0:T(8,128)S(1)} %get-tuple-element.57.refs_0_, bf16[80,640]{1,0:T(8,128)(2,1)S(1)} %collective-permute-done.11.refs_1_, bf16[80,640]{1,0:T(8,128)(2,1)S(1)} %collective-permute-done.12.refs_2_, bf16[80,640]{1,0:T(8,128)(2,1)S(1)} %collective-permute-done.13.refs_3_, ...), custom_call_target="tpu_custom_call" | custom-call | tf_op jit(solution)/shard_map/finish/pallas_call | solution.py:348
  (39 shorter events, 1.4 us)
Async XLA Ops:
  0.6 18.3 %copy-start = (f32[8,63]{1,0:T(8,128)S(1)}, f32[8,63]{1,0:T(8,128)}, u32[]{:S(2)}) copy-start(f32[8,63]{1,0:T(8,128)} %param.9) | copy-start | bytes 6052
  1.8 7.8 %copy-start.3 = (bf16[8,64,640]{2,1,0:T(8,128)(2,1)S(1)}, bf16[8,64,640]{2,1,0:T(8,128)(2,1)}, u32[]{:S(2)}) copy-start(bf16[8,64,640]{2,1,0:T(8,128)(2,1)} %param.6) | copy-start | bytes 1966084
  1.9 8.7 %copy-start.2 = (bf16[640,3,320]{0,2,1:T(8,128)(2,1)S(1)}, bf16[640,3,320]{0,2,1:T(8,128)(2,1)}, u32[]{:S(2)}) copy-start(bf16[640,3,320]{0,2,1:T(8,128)(2,1)} %param.7) | copy-start | bytes 3686404
  2.0 10.2 %collective-permute-start = (bf16[128,640]{1,0:T(8,128)(2,1)S(1)}, bf16[128,640]{1,0:T(8,128)(2,1)S(1)}, u32[]{:S(2)}, u32[]{:S(2)}) collective-permute-start(bf16[128,640]{1,0:T(8,128)(2,1)S(1)} %bitcast.35), channel_id=1, source_target_pairs={{0,4},{4,8},{8,12},{12,0},{1,5},{5,9},{9,13},{13,1},{2,6},{6,10},{... | collective-permute-start | bytes 491528 | tf_op jit(solution)/shard_map/ppermute | solution.py:23
  5.1 13.3 %collective-permute-start.2 = (bf16[128,640]{1,0:T(8,128)(2,1)S(1)}, bf16[128,640]{1,0:T(8,128)(2,1)S(1)}, u32[]{:S(2)}, u32[]{:S(2)}) collective-permute-start(bf16[128,640]{1,0:T(8,128)(2,1)S(1)} %bitcast.34), channel_id=1, source_target_pairs={{0,8},{4,12},{8,0},{12,4},{1,9},{5,13},{9,1},{13,5},{2,10},{6,14},... | collective-permute-start | bytes 491528 | tf_op jit(solution)/shard_map/ppermute | solution.py:23
  7.8 10.6 %collective-permute-start.4 = (bf16[128,640]{1,0:T(8,128)(2,1)S(1)}, bf16[128,640]{1,0:T(8,128)(2,1)S(1)}, u32[]{:S(2)}, u32[]{:S(2)}) collective-permute-start(bf16[128,640]{1,0:T(8,128)(2,1)S(1)} %bitcast.33), channel_id=1, source_target_pairs={{0,12},{4,0},{8,4},{12,8},{1,13},{5,1},{9,5},{13,9},{2,14},{6,2},{... | collective-permute-start | bytes 491528 | tf_op jit(solution)/shard_map/ppermute | solution.py:23
  12.1 7.9 %copy-start.1 = (bf16[320,640]{1,0:T(8,128)(2,1)S(1)}, bf16[320,640]{1,0:T(8,128)(2,1)}, u32[]{:S(2)}) copy-start(bf16[320,640]{1,0:T(8,128)(2,1)} %refs_11_.1) | copy-start | bytes 1228804
  12.2 7.7 %collective-permute-start.1 = (bf16[128,640]{1,0:T(8,128)(2,1)S(1)}, bf16[128,640]{1,0:T(8,128)(2,1)S(1)}, u32[]{:S(2)}, u32[]{:S(2)}) collective-permute-start(bf16[128,640]{1,0:T(8,128)(2,1)S(1)} %collective-permute-done.refs_2_), channel_id=1, source_target_pairs={{0,1},{1,0},{2,3},{3,2},{4,5},{5,4},{6,7},{7,6},{8,9},{9,8},{10,11... | collective-permute-start | bytes 491528 | tf_op jit(solution)/shard_map/ppermute | solution.py:23
  18.4 1.5 %collective-permute-start.3 = (bf16[128,640]{1,0:T(8,128)(2,1)S(1)}, bf16[128,640]{1,0:T(8,128)(2,1)S(1)}, u32[]{:S(2)}, u32[]{:S(2)}) collective-permute-start(bf16[128,640]{1,0:T(8,128)(2,1)S(1)} %collective-permute-done.2.refs_4_), channel_id=1, source_target_pairs={{0,1},{1,0},{2,3},{3,2},{4,5},{5,4},{6,7},{7,6},{8,9},{9,8},{10,11... | collective-permute-start | bytes 491528 | tf_op jit(solution)/shard_map/ppermute | solution.py:23
  18.4 1.6 %collective-permute-start.5 = (bf16[128,640]{1,0:T(8,128)(2,1)S(1)}, bf16[128,640]{1,0:T(8,128)(2,1)S(1)}, u32[]{:S(2)}, u32[]{:S(2)}) collective-permute-start(bf16[128,640]{1,0:T(8,128)(2,1)S(1)} %collective-permute-done.4.refs_6_), channel_id=1, source_target_pairs={{0,1},{1,0},{2,3},{3,2},{4,5},{5,4},{6,7},{7,6},{8,9},{9,8},{10,11... | collective-permute-start | bytes 491528 | tf_op jit(solution)/shard_map/ppermute | solution.py:23
  26.2 2.8 %collective-permute-start.6 = (bf16[4,128,320]{2,1,0:T(8,128)(2,1)S(1)}, bf16[4,128,320]{2,1,0:T(8,128)(2,1)S(1)}, u32[]{:S(2)}, u32[]{:S(2)}) collective-permute-start(bf16[4,128,320]{2,1,0:T(8,128)(2,1)S(1)} %get-tuple-element.41), channel_id=1, source_target_pairs={{0,1},{1,0},{2,3},{3,2},{4,5},{5,4},{6,7},{7,6},{8,9},{9,8},{10,11... | collective-permute-start | bytes 983048 | tf_op jit(solution)/shard_map/ppermute | solution.py:23
  27.4 12.4 %collective-permute-start.7 = (bf16[4,80,640]{2,1,0:T(8,128)(2,1)S(1)}, bf16[4,80,640]{2,1,0:T(8,128)(2,1)S(1)}, u32[]{:S(2)}, u32[]{:S(2)}) collective-permute-start(bf16[4,80,640]{2,1,0:T(8,128)(2,1)S(1)} %get-tuple-element.46), channel_id=1, source_target_pairs={{0,2},{2,0},{1,3},{3,1},{4,6},{6,4},{5,7},{7,5},{8,10},{10,8},{9,1... | collective-permute-start | bytes 1228808 | tf_op jit(solution)/shard_map/ppermute | solution.py:23
  29.8 18.0 %collective-permute-start.14 = (bf16[4,80,640]{2,1,0:T(8,128)(2,1)S(1)}, bf16[4,80,640]{2,1,0:T(8,128)(2,1)S(1)}, u32[]{:S(2)}, u32[]{:S(2)}) collective-permute-start(bf16[4,80,640]{2,1,0:T(8,128)(2,1)S(1)} %get-tuple-element.64), channel_id=1, source_target_pairs={{0,2},{2,0},{1,3},{3,1},{4,6},{6,4},{5,7},{7,5},{8,10},{10,8},{9,1... | collective-permute-start | bytes 1228808 | tf_op jit(solution)/shard_map/ppermute | solution.py:23
  30.4 9.4 %collective-permute-start.8 = (bf16[64,640]{1,0:T(8,128)(2,1)S(1)}, bf16[64,640]{1,0:T(8,128)(2,1)S(1)}, u32[]{:S(2)}, u32[]{:S(2)}) collective-permute-start(bf16[64,640]{1,0:T(8,128)(2,1)S(1)} %get-tuple-element.47), channel_id=1, source_target_pairs={{0,4},{4,8},{8,12},{12,0},{1,5},{5,9},{9,13},{13,1},{2,6},{6,10},{... | collective-permute-start | bytes 245768 | tf_op jit(solution)/shard_map/ppermute | solution.py:23
  34.1 7.5 %collective-permute-start.9 = (bf16[64,640]{1,0:T(8,128)(2,1)S(1)}, bf16[64,640]{1,0:T(8,128)(2,1)S(1)}, u32[]{:S(2)}, u32[]{:S(2)}) collective-permute-start(bf16[64,640]{1,0:T(8,128)(2,1)S(1)} %get-tuple-element.50), channel_id=1, source_target_pairs={{0,8},{4,12},{8,0},{12,4},{1,9},{5,13},{9,1},{13,5},{2,10},{6,14},... | collective-permute-start | bytes 245768 | tf_op jit(solution)/shard_map/ppermute | solution.py:23
  36.0 5.9 %collective-permute-start.10 = (bf16[64,640]{1,0:T(8,128)(2,1)S(1)}, bf16[64,640]{1,0:T(8,128)(2,1)S(1)}, u32[]{:S(2)}, u32[]{:S(2)}) collective-permute-start(bf16[64,640]{1,0:T(8,128)(2,1)S(1)} %get-tuple-element.53), channel_id=1, source_target_pairs={{0,12},{4,0},{8,4},{12,8},{1,13},{5,1},{9,5},{13,9},{2,14},{6,2},{... | collective-permute-start | bytes 245768 | tf_op jit(solution)/shard_map/ppermute | solution.py:23
  42.0 11.6 %collective-permute-start.11 = (bf16[80,640]{1,0:T(8,128)(2,1)S(1)}, bf16[80,640]{1,0:T(8,128)(2,1)S(1)}, u32[]{:S(2)}, u32[]{:S(2)}) collective-permute-start(bf16[80,640]{1,0:T(8,128)(2,1)S(1)} %get-tuple-element.58), channel_id=1, source_target_pairs={{0,4},{4,8},{8,12},{12,0},{1,5},{5,9},{9,13},{13,1},{2,6},{6,10},{... | collective-permute-start | bytes 307208 | tf_op jit(solution)/shard_map/ppermute | solution.py:23
  44.0 11.5 %collective-permute-start.12 = (bf16[80,640]{1,0:T(8,128)(2,1)S(1)}, bf16[80,640]{1,0:T(8,128)(2,1)S(1)}, u32[]{:S(2)}, u32[]{:S(2)}) collective-permute-start(bf16[80,640]{1,0:T(8,128)(2,1)S(1)} %get-tuple-element.59), channel_id=1, source_target_pairs={{0,8},{4,12},{8,0},{12,4},{1,9},{5,13},{9,1},{13,5},{2,10},{6,14},... | collective-permute-start | bytes 307208 | tf_op jit(solution)/shard_map/ppermute | solution.py:23
  45.5 9.9 %collective-permute-start.13 = (bf16[80,640]{1,0:T(8,128)(2,1)S(1)}, bf16[80,640]{1,0:T(8,128)(2,1)S(1)}, u32[]{:S(2)}, u32[]{:S(2)}) collective-permute-start(bf16[80,640]{1,0:T(8,128)(2,1)S(1)} %get-tuple-element.60), channel_id=1, source_target_pairs={{0,12},{4,0},{8,4},{12,8},{1,13},{5,1},{9,5},{13,9},{2,14},{6,2},{... | collective-permute-start | bytes 307208 | tf_op jit(solution)/shard_map/ppermute | solution.py:23
  47.9 8.9 %collective-permute-start.15 = (bf16[80,640]{1,0:T(8,128)(2,1)S(1)}, bf16[80,640]{1,0:T(8,128)(2,1)S(1)}, u32[]{:S(2)}, u32[]{:S(2)}) collective-permute-start(bf16[80,640]{1,0:T(8,128)(2,1)S(1)} %get-tuple-element.66), channel_id=1, source_target_pairs={{0,4},{4,8},{8,12},{12,0},{1,5},{5,9},{9,13},{13,1},{2,6},{6,10},{... | collective-permute-start | bytes 307208 | tf_op jit(solution)/shard_map/ppermute | solution.py:23
  51.7 9.8 %collective-permute-start.16 = (bf16[80,640]{1,0:T(8,128)(2,1)S(1)}, bf16[80,640]{1,0:T(8,128)(2,1)S(1)}, u32[]{:S(2)}, u32[]{:S(2)}) collective-permute-start(bf16[80,640]{1,0:T(8,128)(2,1)S(1)} %get-tuple-element.67), channel_id=1, source_target_pairs={{0,8},{4,12},{8,0},{12,4},{1,9},{5,13},{9,1},{13,5},{2,10},{6,14},... | collective-permute-start | bytes 307208 | tf_op jit(solution)/shard_map/ppermute | solution.py:23
  53.6 7.9 %collective-permute-start.17 = (bf16[80,640]{1,0:T(8,128)(2,1)S(1)}, bf16[80,640]{1,0:T(8,128)(2,1)S(1)}, u32[]{:S(2)}, u32[]{:S(2)}) collective-permute-start(bf16[80,640]{1,0:T(8,128)(2,1)S(1)} %get-tuple-element.68), channel_id=1, source_target_pairs={{0,12},{4,0},{8,4},{12,8},{1,13},{5,1},{9,5},{13,9},{2,14},{6,2},{... | collective-permute-start | bytes 307208 | tf_op jit(solution)/shard_map/ppermute | solution.py:23

commit v5 on v4

--- a/solution.py
+++ b/solution.py
@@ -14,7 +14,7 @@
 F32 = jnp.float32
 
 
-def params(limit=48 << 20):
+def params(limit=32 << 20):
     return pltpu.CompilerParams(vmem_limit_bytes=limit)
 
 

time: 62.6 us -> 61.1 us (0.976)
  Pallas kernels: 10.8 us -> 9.31 us
  local copies, waits for them, and re-layouts: 3.04 us -> 2.17 us
  waiting for transfers between devices: 19.3 us -> 20.1 us
    pallas_call x1, Pallas kernels: 6.13 us -> 4.65 us  [attend(): pl.pallas_call(functools.partial(attend_kernel, owners, heads), out_shape...]
    dynamic_slice x1, local copies, waits for them, and re-layouts: 1.53 us -> 0.66 us  [per_device(): lax.dynamic_slice_in_dim(w_flat, which * width, width, 1)]
    ppermute x18, waiting for transfers between devices: 19.3 us -> 20.1 us  [shift_send(): lax.ppermute(array, axis, [(i, (i + step) % size) for i in range(size)])]
  transfers between devices with their start and end apart: 18 -> 18, of which waited for: 9 -> 9; matrix products, arithmetic and copies ran while one was open for 5% -> 4% of each run, Pallas kernels for 6% -> 6%
where the time goes in v5:
time: 61.1 us; the launch traced here: 60.9 us
  starting transfers between devices  26.9 us (44%)
  waiting for transfers between devices  20.1 us (33%)
  Pallas kernels  9.31 us (15%)
  local copies, waits for them, and re-layouts  2.17 us (4%)
  other arithmetic  1.6 us (3%)
  between operations  0.84 us (1%)
    ppermute x18, starting transfers between devices, shift_send(): lax.ppermute(array, axis, [(i, (i + step) % size) for i in range(size)])  26.9 us
    ppermute x18, waiting for transfers between devices, shift_send(): lax.ppermute(array, axis, [(i, (i + step) % size) for i in range(size)])  20.1 us
    pallas_call x1, Pallas kernels, attend(): pl.pallas_call(functools.partial(attend_kernel, owners, heads), out_shape...  4.65 us
    pallas_call x2, Pallas kernels, weight_terms(): pl.pallas_call(functools.partial(weight_kernel, owners, sides, block, len...  1.59 us
  transfers between devices with their start and end apart: 18, of which 9 were waited for; matrix products, arithmetic and copies ran while one was open for 4% of the time, Pallas kernels for 6%

profile of v5, /device:TPU:0, one launch (start us, length us, event | category | flops | bytes accessed | tf_op | source)
XLA Modules:
  0.0 60.9 jit_solution(10726831569376340548)
XLA Ops:
  0.7 1.2 %broadcast_select_fusion = bf16[8,64,640]{2,1,0:T(8,128)(2,1)S(1)} fusion(bf16[8,64,640]{2,1,0:T(8,128)(2,1)} %param.5, bf16[8,64,640]{2,1,0:T(8,128)(2,1)} %param.6, pred[]{:T(512)S(6)} %eq.3), kind=kLoop, calls=%fused_computation | loop fusion | flops 327680 | bytes 1966081 | tf_op jit(solution)/shard_map/jit(_where)/select_n | solution.py:90
  2.0 3.1 %collective-permute-start = (bf16[128,640]{1,0:T(8,128)(2,1)S(1)}, bf16[128,640]{1,0:T(8,128)(2,1)S(1)}, u32[]{:S(2)}, u32[]{:S(2)}) collective-permute-start(bf16[128,640]{1,0:T(8,128)(2,1)S(1)} %bitcast.35), channel_id=1, source_target_pairs={{0,4},{4,8},{8,12},{12,0},{1,5},{5,9},{9,13},{13,1},{2,6},{6,10},{... | collective-permute-start | bytes 491528 | tf_op jit(solution)/shard_map/ppermute | solution.py:23
  5.1 2.7 %collective-permute-start.2 = (bf16[128,640]{1,0:T(8,128)(2,1)S(1)}, bf16[128,640]{1,0:T(8,128)(2,1)S(1)}, u32[]{:S(2)}, u32[]{:S(2)}) collective-permute-start(bf16[128,640]{1,0:T(8,128)(2,1)S(1)} %bitcast.34), channel_id=1, source_target_pairs={{0,8},{4,12},{8,0},{12,4},{1,9},{5,13},{9,1},{13,5},{2,10},{6,14},... | collective-permute-start | bytes 491528 | tf_op jit(solution)/shard_map/ppermute | solution.py:23
  7.8 1.4 %collective-permute-start.4 = (bf16[128,640]{1,0:T(8,128)(2,1)S(1)}, bf16[128,640]{1,0:T(8,128)(2,1)S(1)}, u32[]{:S(2)}, u32[]{:S(2)}) collective-permute-start(bf16[128,640]{1,0:T(8,128)(2,1)S(1)} %bitcast.33), channel_id=1, source_target_pairs={{0,12},{4,0},{8,4},{12,8},{1,13},{5,1},{9,5},{13,9},{2,14},{6,2},{... | collective-permute-start | bytes 491528 | tf_op jit(solution)/shard_map/ppermute | solution.py:23
  9.6 1.0 %dynamic-slice_bitcast_fusion.3 = (bf16[16,8,640]{2,0,1:T(8,128)(2,1)S(1)}, bf16[16,8,640]{2,0,1:T(8,128)(2,1)S(1)}) fusion(bf16[8,64,640]{2,1,0:T(8,128)(2,1)S(1)} %copy-done.3, s32[]{:T(128)S(6)} %select_n.31, bf16[8,64,640]{2,1,0:T(8,128)(2,1)} %param.5), kind=kLoop, calls=%fused_computation.9 | loop fusion | bytes 655364 | tf_op jit(solution)/shard_map/transpose | solution.py:96
  10.6 0.7 %constant_dynamic-slice_fusion.2 = (bf16[960,320]{1,0:T(8,128)(2,1)S(1)}, bf16[960,320]{1,0:T(8,128)(2,1)S(1)}) fusion(bf16[960,640]{1,0:T(8,128)(2,1)S(1)} %bitcast.29, s32[]{:T(128)S(6)} %select_n.36, s32[]{:T(128)S(6)} %select_n.35), kind=kLoop, calls=%fused_computation.16 | loop fusion | bytes 2457608 | tf_op jit(solution)/shard_map/dynamic_slice | solution.py:422
  11.3 0.9 %collective-permute-done.refs_2_ = bf16[128,640]{1,0:T(8,128)(2,1)S(1)} collective-permute-done((bf16[128,640]{1,0:T(8,128)(2,1)S(1)}, bf16[128,640]{1,0:T(8,128)(2,1)S(1)}, u32[]{:S(2)}, u32[]{:S(2)}) %collective-permute-start) | collective-permute-done | bytes 163872 | tf_op jit(solution)/shard_map/ppermute | solution.py:23
  12.2 6.2 %collective-permute-done.2.refs_4_ = bf16[128,640]{1,0:T(8,128)(2,1)S(1)} collective-permute-done((bf16[128,640]{1,0:T(8,128)(2,1)S(1)}, bf16[128,640]{1,0:T(8,128)(2,1)S(1)}, u32[]{:S(2)}, u32[]{:S(2)}) %collective-permute-start.2) | collective-permute-done | bytes 163872 | tf_op jit(solution)/shard_map/ppermute | solution.py:23
  18.4 0.5 collective-permute-start.5
  19.0 0.8 %bias_of_rows.1.refs_9_ = f32[128,512]{1,0:T(8,128)S(1)} custom-call(f32[4,128]{1,0:T(4,128)S(1)} %pad.4.bias_ref), custom_call_target="tpu_custom_call" | custom-call | tf_op jit(solution)/shard_map/bias_of_rows/pallas_call | solution.py:103
  20.0 4.6 %attend.1 = (bf16[512,640]{1,0:T(8,128)(2,1)S(1)}, bf16[512,640]{1,0:T(8,128)(2,1)S(1)}, bf16[512,640]{1,0:T(8,128)(2,1)S(1)}, bf16[512,640]{1,0:T(8,128)(2,1)S(...) custom-call(bf16[128,640]{1,0:T(8,128)(2,1)S(1)} %bitcast.32, bf16[128,640]{1,0:T(8,128)(2,1)S(1)} %bitcast.31, ...), custom_call_target="tpu_custom_call" | custom-call | tf_op jit(solution)/shard_map/attend/pallas_call | solution.py:213
  24.7 0.4 collective-permute-start.6
  25.0 0.9 %weight_terms.2 = (f32[4,80,640]{2,1,0:T(8,128)S(1)}, bf16[4,80,640]{2,1,0:T(8,128)(2,1)S(1)}) custom-call(bf16[512,640]{1,0:T(8,128)(2,1)S(1)} %get-tuple-element.43.refs_0_, bf16[512,640]{1,0:T(8,128)(2,1)S(1)} %get-tuple-element.44.refs_1_, bf16[512,640]{1,0:T(8,128)(2,1)S(1)} %get-tuple-element.45.refs_2_), custom_call_target="tpu_custom_call" | custom-call | tf_op jit(solution)/shard_map/weight_terms/pallas_call | solution.py:269
  25.9 1.5 %collective-permute-start.7 = (bf16[4,80,640]{2,1,0:T(8,128)(2,1)S(1)}, bf16[4,80,640]{2,1,0:T(8,128)(2,1)S(1)}, u32[]{:S(2)}, u32[]{:S(2)}) collective-permute-start(bf16[4,80,640]{2,1,0:T(8,128)(2,1)S(1)} %get-tuple-element.46), channel_id=1, source_target_pairs={{0,2},{2,0},{1,3},{3,1},{4,6},{6,4},{5,7},{7,5},{8,10},{10,8},{9,1... | collective-permute-start | bytes 1228808 | tf_op jit(solution)/shard_map/ppermute | solution.py:23
  27.6 0.7 %weight_terms.3 = (f32[4,80,640]{2,1,0:T(8,128)S(1)}, bf16[4,80,640]{2,1,0:T(8,128)(2,1)S(1)}) custom-call(bf16[512,640]{1,0:T(8,128)(2,1)S(1)} %get-tuple-element.62.refs_0_, bf16[512,640]{1,0:T(8,128)(2,1)S(1)} %get-tuple-element.44.refs_1_), custom_call_target="tpu_custom_call" | custom-call | tf_op jit(solution)/shard_map/weight_terms/pallas_call | solution.py:269
  28.3 0.6 collective-permute-start.14
  28.9 3.7 %collective-permute-start.8 = (bf16[64,640]{1,0:T(8,128)(2,1)S(1)}, bf16[64,640]{1,0:T(8,128)(2,1)S(1)}, u32[]{:S(2)}, u32[]{:S(2)}) collective-permute-start(bf16[64,640]{1,0:T(8,128)(2,1)S(1)} %get-tuple-element.47), channel_id=1, source_target_pairs={{0,4},{4,8},{8,12},{12,0},{1,5},{5,9},{9,13},{13,1},{2,6},{6,10},{... | collective-permute-start | bytes 245768 | tf_op jit(solution)/shard_map/ppermute | solution.py:23
  32.6 1.9 %collective-permute-start.9 = (bf16[64,640]{1,0:T(8,128)(2,1)S(1)}, bf16[64,640]{1,0:T(8,128)(2,1)S(1)}, u32[]{:S(2)}, u32[]{:S(2)}) collective-permute-start(bf16[64,640]{1,0:T(8,128)(2,1)S(1)} %get-tuple-element.50), channel_id=1, source_target_pairs={{0,8},{4,12},{8,0},{12,4},{1,9},{5,13},{9,1},{13,5},{2,10},{6,14},... | collective-permute-start | bytes 245768 | tf_op jit(solution)/shard_map/ppermute | solution.py:23
  34.5 0.5 collective-permute-start.10
  35.0 3.3 %collective-permute-done.7.refs_0_ = bf16[4,80,640]{2,1,0:T(8,128)(2,1)S(1)} collective-permute-done((bf16[4,80,640]{2,1,0:T(8,128)(2,1)S(1)}, bf16[4,80,640]{2,1,0:T(8,128)(2,1)S(1)}, u32[]{:S(2)}, u32[]{:S(2)}) %collective-permute-start.7) | collective-permute-done | bytes 409632 | tf_op jit(solution)/shard_map/ppermute | solution.py:23
  38.3 1.8 %collective-permute-done.9.refs_2_ = bf16[64,640]{1,0:T(8,128)(2,1)S(1)} collective-permute-done((bf16[64,640]{1,0:T(8,128)(2,1)S(1)}, bf16[64,640]{1,0:T(8,128)(2,1)S(1)}, u32[]{:S(2)}, u32[]{:S(2)}) %collective-permute-start.9) | collective-permute-done | bytes 81952 | tf_op jit(solution)/shard_map/ppermute | solution.py:23
  40.5 2.0 %collective-permute-start.11 = (bf16[80,640]{1,0:T(8,128)(2,1)S(1)}, bf16[80,640]{1,0:T(8,128)(2,1)S(1)}, u32[]{:S(2)}, u32[]{:S(2)}) collective-permute-start(bf16[80,640]{1,0:T(8,128)(2,1)S(1)} %get-tuple-element.58), channel_id=1, source_target_pairs={{0,4},{4,8},{8,12},{12,0},{1,5},{5,9},{9,13},{13,1},{2,6},{6,10},{... | collective-permute-start | bytes 307208 | tf_op jit(solution)/shard_map/ppermute | solution.py:23
  42.5 1.6 %collective-permute-start.12 = (bf16[80,640]{1,0:T(8,128)(2,1)S(1)}, bf16[80,640]{1,0:T(8,128)(2,1)S(1)}, u32[]{:S(2)}, u32[]{:S(2)}) collective-permute-start(bf16[80,640]{1,0:T(8,128)(2,1)S(1)} %get-tuple-element.59), channel_id=1, source_target_pairs={{0,8},{4,12},{8,0},{12,4},{1,9},{5,13},{9,1},{13,5},{2,10},{6,14},... | collective-permute-start | bytes 307208 | tf_op jit(solution)/shard_map/ppermute | solution.py:23
  44.0 0.9 %collective-permute-start.13 = (bf16[80,640]{1,0:T(8,128)(2,1)S(1)}, bf16[80,640]{1,0:T(8,128)(2,1)S(1)}, u32[]{:S(2)}, u32[]{:S(2)}) collective-permute-start(bf16[80,640]{1,0:T(8,128)(2,1)S(1)} %get-tuple-element.60), channel_id=1, source_target_pairs={{0,12},{4,0},{8,4},{12,8},{1,13},{5,1},{9,5},{13,9},{2,14},{6,2},{... | collective-permute-start | bytes 307208 | tf_op jit(solution)/shard_map/ppermute | solution.py:23
  44.9 1.4 %collective-permute-done.14.refs_0_ = bf16[4,80,640]{2,1,0:T(8,128)(2,1)S(1)} collective-permute-done((bf16[4,80,640]{2,1,0:T(8,128)(2,1)S(1)}, bf16[4,80,640]{2,1,0:T(8,128)(2,1)S(1)}, u32[]{:S(2)}, u32[]{:S(2)}) %collective-permute-start.14) | collective-permute-done | bytes 409632 | tf_op jit(solution)/shard_map/ppermute | solution.py:23
  46.5 3.8 %collective-permute-start.15 = (bf16[80,640]{1,0:T(8,128)(2,1)S(1)}, bf16[80,640]{1,0:T(8,128)(2,1)S(1)}, u32[]{:S(2)}, u32[]{:S(2)}) collective-permute-start(bf16[80,640]{1,0:T(8,128)(2,1)S(1)} %get-tuple-element.66), channel_id=1, source_target_pairs={{0,4},{4,8},{8,12},{12,0},{1,5},{5,9},{9,13},{13,1},{2,6},{6,10},{... | collective-permute-start | bytes 307208 | tf_op jit(solution)/shard_map/ppermute | solution.py:23
  50.3 1.9 %collective-permute-start.16 = (bf16[80,640]{1,0:T(8,128)(2,1)S(1)}, bf16[80,640]{1,0:T(8,128)(2,1)S(1)}, u32[]{:S(2)}, u32[]{:S(2)}) collective-permute-start(bf16[80,640]{1,0:T(8,128)(2,1)S(1)} %get-tuple-element.67), channel_id=1, source_target_pairs={{0,8},{4,12},{8,0},{12,4},{1,9},{5,13},{9,1},{13,5},{2,10},{6,14},... | collective-permute-start | bytes 307208 | tf_op jit(solution)/shard_map/ppermute | solution.py:23
  52.1 0.6 collective-permute-start.17
  52.9 1.1 %place.1 = bf16[8,64,320]{2,1,0:T(8,128)(2,1)} custom-call(bf16[64,640]{1,0:T(8,128)(2,1)S(1)} %get-tuple-element.42.refs_0_, bf16[64,640]{1,0:T(8,128)(2,1)S(1)} %collective-permute-done.8.refs_1_, bf16[64,640]{1,0:T(8,128)(2,1)S(1)} %collective-permute-done.9.refs_2_, bf16[64,640]{1,0:T(8,128)(2,1)S(1)} %collective-permute-done.10.refs_3_, ...), custom_call_target="tpu_custom_call" | custom-call | tf_op jit(solution)/shard_map/place/pallas_call | solution.py:387
  54.0 1.3 %collective-permute-done.15.refs_5_ = bf16[80,640]{1,0:T(8,128)(2,1)S(1)} collective-permute-done((bf16[80,640]{1,0:T(8,128)(2,1)S(1)}, bf16[80,640]{1,0:T(8,128)(2,1)S(1)}, u32[]{:S(2)}, u32[]{:S(2)}) %collective-permute-start.15) | collective-permute-done | bytes 102432 | tf_op jit(solution)/shard_map/ppermute | solution.py:23
  55.3 4.7 %collective-permute-done.16.refs_6_ = bf16[80,640]{1,0:T(8,128)(2,1)S(1)} collective-permute-done((bf16[80,640]{1,0:T(8,128)(2,1)S(1)}, bf16[80,640]{1,0:T(8,128)(2,1)S(1)}, u32[]{:S(2)}, u32[]{:S(2)}) %collective-permute-start.16) | collective-permute-done | bytes 102432 | tf_op jit(solution)/shard_map/ppermute | solution.py:23
  60.0 0.9 %finish.1 = (f32[3,80,320]{2,1,0:T(8,128)}, f32[80,320]{1,0:T(8,128)}) custom-call(f32[80,640]{1,0:T(8,128)S(1)} %get-tuple-element.57.refs_0_, bf16[80,640]{1,0:T(8,128)(2,1)S(1)} %collective-permute-done.11.refs_1_, bf16[80,640]{1,0:T(8,128)(2,1)S(1)} %collective-permute-done.12.refs_2_, bf16[80,640]{1,0:T(8,128)(2,1)S(1)} %collective-permute-done.13.refs_3_, ...), custom_call_target="tpu_custom_call" | custom-call | tf_op jit(solution)/shard_map/finish/pallas_call | solution.py:348
  (39 shorter events, 1.7 us)
Async XLA Ops:
  0.6 18.3 %copy-start = (f32[8,63]{1,0:T(8,128)S(1)}, f32[8,63]{1,0:T(8,128)}, u32[]{:S(2)}) copy-start(f32[8,63]{1,0:T(8,128)} %param.9) | copy-start | bytes 6052
  1.8 7.8 %copy-start.3 = (bf16[8,64,640]{2,1,0:T(8,128)(2,1)S(1)}, bf16[8,64,640]{2,1,0:T(8,128)(2,1)}, u32[]{:S(2)}) copy-start(bf16[8,64,640]{2,1,0:T(8,128)(2,1)} %param.6) | copy-start | bytes 1966084
  1.9 8.7 %copy-start.1 = (bf16[640,3,320]{0,2,1:T(8,128)(2,1)S(1)}, bf16[640,3,320]{0,2,1:T(8,128)(2,1)}, u32[]{:S(2)}) copy-start(bf16[640,3,320]{0,2,1:T(8,128)(2,1)} %param.7) | copy-start | bytes 3686404
  2.0 10.2 %collective-permute-start = (bf16[128,640]{1,0:T(8,128)(2,1)S(1)}, bf16[128,640]{1,0:T(8,128)(2,1)S(1)}, u32[]{:S(2)}, u32[]{:S(2)}) collective-permute-start(bf16[128,640]{1,0:T(8,128)(2,1)S(1)} %bitcast.35), channel_id=1, source_target_pairs={{0,4},{4,8},{8,12},{12,0},{1,5},{5,9},{9,13},{13,1},{2,6},{6,10},{... | collective-permute-start | bytes 491528 | tf_op jit(solution)/shard_map/ppermute | solution.py:23
  5.1 13.3 %collective-permute-start.2 = (bf16[128,640]{1,0:T(8,128)(2,1)S(1)}, bf16[128,640]{1,0:T(8,128)(2,1)S(1)}, u32[]{:S(2)}, u32[]{:S(2)}) collective-permute-start(bf16[128,640]{1,0:T(8,128)(2,1)S(1)} %bitcast.34), channel_id=1, source_target_pairs={{0,8},{4,12},{8,0},{12,4},{1,9},{5,13},{9,1},{13,5},{2,10},{6,14},... | collective-permute-start | bytes 491528 | tf_op jit(solution)/shard_map/ppermute | solution.py:23
  7.8 10.6 %collective-permute-start.4 = (bf16[128,640]{1,0:T(8,128)(2,1)S(1)}, bf16[128,640]{1,0:T(8,128)(2,1)S(1)}, u32[]{:S(2)}, u32[]{:S(2)}) collective-permute-start(bf16[128,640]{1,0:T(8,128)(2,1)S(1)} %bitcast.33), channel_id=1, source_target_pairs={{0,12},{4,0},{8,4},{12,8},{1,13},{5,1},{9,5},{13,9},{2,14},{6,2},{... | collective-permute-start | bytes 491528 | tf_op jit(solution)/shard_map/ppermute | solution.py:23
  11.3 8.8 %copy-start.2 = (bf16[320,640]{1,0:T(8,128)(2,1)S(1)}, bf16[320,640]{1,0:T(8,128)(2,1)}, u32[]{:S(2)}) copy-start(bf16[320,640]{1,0:T(8,128)(2,1)} %refs_11_.1) | copy-start | bytes 1228804
  12.2 7.7 %collective-permute-start.1 = (bf16[128,640]{1,0:T(8,128)(2,1)S(1)}, bf16[128,640]{1,0:T(8,128)(2,1)S(1)}, u32[]{:S(2)}, u32[]{:S(2)}) collective-permute-start(bf16[128,640]{1,0:T(8,128)(2,1)S(1)} %collective-permute-done.refs_2_), channel_id=1, source_target_pairs={{0,1},{1,0},{2,3},{3,2},{4,5},{5,4},{6,7},{7,6},{8,9},{9,8},{10,11... | collective-permute-start | bytes 491528 | tf_op jit(solution)/shard_map/ppermute | solution.py:23
  18.4 1.5 %collective-permute-start.3 = (bf16[128,640]{1,0:T(8,128)(2,1)S(1)}, bf16[128,640]{1,0:T(8,128)(2,1)S(1)}, u32[]{:S(2)}, u32[]{:S(2)}) collective-permute-start(bf16[128,640]{1,0:T(8,128)(2,1)S(1)} %collective-permute-done.2.refs_4_), channel_id=1, source_target_pairs={{0,1},{1,0},{2,3},{3,2},{4,5},{5,4},{6,7},{7,6},{8,9},{9,8},{10,11... | collective-permute-start | bytes 491528 | tf_op jit(solution)/shard_map/ppermute | solution.py:23
  18.4 1.6 %collective-permute-start.5 = (bf16[128,640]{1,0:T(8,128)(2,1)S(1)}, bf16[128,640]{1,0:T(8,128)(2,1)S(1)}, u32[]{:S(2)}, u32[]{:S(2)}) collective-permute-start(bf16[128,640]{1,0:T(8,128)(2,1)S(1)} %collective-permute-done.4.refs_6_), channel_id=1, source_target_pairs={{0,1},{1,0},{2,3},{3,2},{4,5},{5,4},{6,7},{7,6},{8,9},{9,8},{10,11... | collective-permute-start | bytes 491528 | tf_op jit(solution)/shard_map/ppermute | solution.py:23
  24.7 2.8 %collective-permute-start.6 = (bf16[4,128,320]{2,1,0:T(8,128)(2,1)S(1)}, bf16[4,128,320]{2,1,0:T(8,128)(2,1)S(1)}, u32[]{:S(2)}, u32[]{:S(2)}) collective-permute-start(bf16[4,128,320]{2,1,0:T(8,128)(2,1)S(1)} %get-tuple-element.41), channel_id=1, source_target_pairs={{0,1},{1,0},{2,3},{3,2},{4,5},{5,4},{6,7},{7,6},{8,9},{9,8},{10,11... | collective-permute-start | bytes 983048 | tf_op jit(solution)/shard_map/ppermute | solution.py:23
  25.9 12.4 %collective-permute-start.7 = (bf16[4,80,640]{2,1,0:T(8,128)(2,1)S(1)}, bf16[4,80,640]{2,1,0:T(8,128)(2,1)S(1)}, u32[]{:S(2)}, u32[]{:S(2)}) collective-permute-start(bf16[4,80,640]{2,1,0:T(8,128)(2,1)S(1)} %get-tuple-element.46), channel_id=1, source_target_pairs={{0,2},{2,0},{1,3},{3,1},{4,6},{6,4},{5,7},{7,5},{8,10},{10,8},{9,1... | collective-permute-start | bytes 1228808 | tf_op jit(solution)/shard_map/ppermute | solution.py:23
  28.3 18.0 %collective-permute-start.14 = (bf16[4,80,640]{2,1,0:T(8,128)(2,1)S(1)}, bf16[4,80,640]{2,1,0:T(8,128)(2,1)S(1)}, u32[]{:S(2)}, u32[]{:S(2)}) collective-permute-start(bf16[4,80,640]{2,1,0:T(8,128)(2,1)S(1)} %get-tuple-element.64), channel_id=1, source_target_pairs={{0,2},{2,0},{1,3},{3,1},{4,6},{6,4},{5,7},{7,5},{8,10},{10,8},{9,1... | collective-permute-start | bytes 1228808 | tf_op jit(solution)/shard_map/ppermute | solution.py:23
  28.9 9.4 %collective-permute-start.8 = (bf16[64,640]{1,0:T(8,128)(2,1)S(1)}, bf16[64,640]{1,0:T(8,128)(2,1)S(1)}, u32[]{:S(2)}, u32[]{:S(2)}) collective-permute-start(bf16[64,640]{1,0:T(8,128)(2,1)S(1)} %get-tuple-element.47), channel_id=1, source_target_pairs={{0,4},{4,8},{8,12},{12,0},{1,5},{5,9},{9,13},{13,1},{2,6},{6,10},{... | collective-permute-start | bytes 245768 | tf_op jit(solution)/shard_map/ppermute | solution.py:23
  32.6 7.5 %collective-permute-start.9 = (bf16[64,640]{1,0:T(8,128)(2,1)S(1)}, bf16[64,640]{1,0:T(8,128)(2,1)S(1)}, u32[]{:S(2)}, u32[]{:S(2)}) collective-permute-start(bf16[64,640]{1,0:T(8,128)(2,1)S(1)} %get-tuple-element.50), channel_id=1, source_target_pairs={{0,8},{4,12},{8,0},{12,4},{1,9},{5,13},{9,1},{13,5},{2,10},{6,14},... | collective-permute-start | bytes 245768 | tf_op jit(solution)/shard_map/ppermute | solution.py:23
  34.5 5.9 %collective-permute-start.10 = (bf16[64,640]{1,0:T(8,128)(2,1)S(1)}, bf16[64,640]{1,0:T(8,128)(2,1)S(1)}, u32[]{:S(2)}, u32[]{:S(2)}) collective-permute-start(bf16[64,640]{1,0:T(8,128)(2,1)S(1)} %get-tuple-element.53), channel_id=1, source_target_pairs={{0,12},{4,0},{8,4},{12,8},{1,13},{5,1},{9,5},{13,9},{2,14},{6,2},{... | collective-permute-start | bytes 245768 | tf_op jit(solution)/shard_map/ppermute | solution.py:23
  40.5 11.6 %collective-permute-start.11 = (bf16[80,640]{1,0:T(8,128)(2,1)S(1)}, bf16[80,640]{1,0:T(8,128)(2,1)S(1)}, u32[]{:S(2)}, u32[]{:S(2)}) collective-permute-start(bf16[80,640]{1,0:T(8,128)(2,1)S(1)} %get-tuple-element.58), channel_id=1, source_target_pairs={{0,4},{4,8},{8,12},{12,0},{1,5},{5,9},{9,13},{13,1},{2,6},{6,10},{... | collective-permute-start | bytes 307208 | tf_op jit(solution)/shard_map/ppermute | solution.py:23
  42.5 11.5 %collective-permute-start.12 = (bf16[80,640]{1,0:T(8,128)(2,1)S(1)}, bf16[80,640]{1,0:T(8,128)(2,1)S(1)}, u32[]{:S(2)}, u32[]{:S(2)}) collective-permute-start(bf16[80,640]{1,0:T(8,128)(2,1)S(1)} %get-tuple-element.59), channel_id=1, source_target_pairs={{0,8},{4,12},{8,0},{12,4},{1,9},{5,13},{9,1},{13,5},{2,10},{6,14},... | collective-permute-start | bytes 307208 | tf_op jit(solution)/shard_map/ppermute | solution.py:23
  44.0 9.9 %collective-permute-start.13 = (bf16[80,640]{1,0:T(8,128)(2,1)S(1)}, bf16[80,640]{1,0:T(8,128)(2,1)S(1)}, u32[]{:S(2)}, u32[]{:S(2)}) collective-permute-start(bf16[80,640]{1,0:T(8,128)(2,1)S(1)} %get-tuple-element.60), channel_id=1, source_target_pairs={{0,12},{4,0},{8,4},{12,8},{1,13},{5,1},{9,5},{13,9},{2,14},{6,2},{... | collective-permute-start | bytes 307208 | tf_op jit(solution)/shard_map/ppermute | solution.py:23
  46.5 8.9 %collective-permute-start.15 = (bf16[80,640]{1,0:T(8,128)(2,1)S(1)}, bf16[80,640]{1,0:T(8,128)(2,1)S(1)}, u32[]{:S(2)}, u32[]{:S(2)}) collective-permute-start(bf16[80,640]{1,0:T(8,128)(2,1)S(1)} %get-tuple-element.66), channel_id=1, source_target_pairs={{0,4},{4,8},{8,12},{12,0},{1,5},{5,9},{9,13},{13,1},{2,6},{6,10},{... | collective-permute-start | bytes 307208 | tf_op jit(solution)/shard_map/ppermute | solution.py:23
  50.3 9.8 %collective-permute-start.16 = (bf16[80,640]{1,0:T(8,128)(2,1)S(1)}, bf16[80,640]{1,0:T(8,128)(2,1)S(1)}, u32[]{:S(2)}, u32[]{:S(2)}) collective-permute-start(bf16[80,640]{1,0:T(8,128)(2,1)S(1)} %get-tuple-element.67), channel_id=1, source_target_pairs={{0,8},{4,12},{8,0},{12,4},{1,9},{5,13},{9,1},{13,5},{2,10},{6,14},... | collective-permute-start | bytes 307208 | tf_op jit(solution)/shard_map/ppermute | solution.py:23
  52.1 7.9 %collective-permute-start.17 = (bf16[80,640]{1,0:T(8,128)(2,1)S(1)}, bf16[80,640]{1,0:T(8,128)(2,1)S(1)}, u32[]{:S(2)}, u32[]{:S(2)}) collective-permute-start(bf16[80,640]{1,0:T(8,128)(2,1)S(1)} %get-tuple-element.68), channel_id=1, source_target_pairs={{0,12},{4,0},{8,4},{12,8},{1,13},{5,1},{9,5},{13,9},{2,14},{6,2},{... | collective-permute-start | bytes 307208 | tf_op jit(solution)/shard_map/ppermute | solution.py:23

commit v6 on v5

--- a/solution.py
+++ b/solution.py
@@ -424,7 +424,7 @@
     for step, block in enumerate(sends):
         mine = shift_send(block, "tm", step + 1)
         if step == 0:
-            mine, w_back = lax.optimization_barrier((mine, w_back))
+            mine, w_back, table, inputs, pe = lax.optimization_barrier((mine, w_back, table, inputs, pe))
         inputs += [mine, shift_send(mine, "sub", 1)]
     hidden, cot, grad_qk, grad_vo, back_keep, back_send = attend(
         inputs, pe, table, w_rows, w_out, w_back, owners, heads

time: 61.1 us -> 61.1 us (level)
  no operation moved by 1% of the time
where the time goes in v6:
time: 61.1 us; the launch traced here: 60.9 us
  starting transfers between devices  26.9 us (44%)
  waiting for transfers between devices  20.1 us (33%)
  Pallas kernels  9.32 us (15%)
  local copies, waits for them, and re-layouts  2.18 us (4%)
  other arithmetic  1.6 us (3%)
  between operations  0.85 us (1%)
    ppermute x18, starting transfers between devices, shift_send(): lax.ppermute(array, axis, [(i, (i + step) % size) for i in range(size)])  26.9 us
    ppermute x18, waiting for transfers between devices, shift_send(): lax.ppermute(array, axis, [(i, (i + step) % size) for i in range(size)])  20.1 us
    pallas_call x1, Pallas kernels, attend(): pl.pallas_call(functools.partial(attend_kernel, owners, heads), out_shape...  4.66 us
    pallas_call x2, Pallas kernels, weight_terms(): pl.pallas_call(functools.partial(weight_kernel, owners, sides, block, len...  1.59 us
  transfers between devices with their start and end apart: 18, of which 9 were waited for; matrix products, arithmetic and copies ran while one was open for 4% of the time, Pallas kernels for 6%

profile of v6, /device:TPU:0, one launch (start us, length us, event | category | flops | bytes accessed | tf_op | source)
XLA Modules:
  0.0 60.9 jit_solution(9194900412917101300)
XLA Ops:
  0.7 1.2 %broadcast_select_fusion = bf16[8,64,640]{2,1,0:T(8,128)(2,1)S(1)} fusion(bf16[8,64,640]{2,1,0:T(8,128)(2,1)} %param.5, bf16[8,64,640]{2,1,0:T(8,128)(2,1)} %param.6, pred[]{:T(512)S(6)} %eq.3), kind=kLoop, calls=%fused_computation | loop fusion | flops 327680 | bytes 1966081 | tf_op jit(solution)/shard_map/jit(_where)/select_n | solution.py:90
  2.0 3.1 %collective-permute-start = (bf16[128,640]{1,0:T(8,128)(2,1)S(1)}, bf16[128,640]{1,0:T(8,128)(2,1)S(1)}, u32[]{:S(2)}, u32[]{:S(2)}) collective-permute-start(bf16[128,640]{1,0:T(8,128)(2,1)S(1)} %bitcast.35), channel_id=1, source_target_pairs={{0,4},{4,8},{8,12},{12,0},{1,5},{5,9},{9,13},{13,1},{2,6},{6,10},{... | collective-permute-start | bytes 491528 | tf_op jit(solution)/shard_map/ppermute | solution.py:23
  5.1 2.7 %collective-permute-start.2 = (bf16[128,640]{1,0:T(8,128)(2,1)S(1)}, bf16[128,640]{1,0:T(8,128)(2,1)S(1)}, u32[]{:S(2)}, u32[]{:S(2)}) collective-permute-start(bf16[128,640]{1,0:T(8,128)(2,1)S(1)} %bitcast.34), channel_id=1, source_target_pairs={{0,8},{4,12},{8,0},{12,4},{1,9},{5,13},{9,1},{13,5},{2,10},{6,14},... | collective-permute-start | bytes 491528 | tf_op jit(solution)/shard_map/ppermute | solution.py:23
  7.8 1.4 %collective-permute-start.4 = (bf16[128,640]{1,0:T(8,128)(2,1)S(1)}, bf16[128,640]{1,0:T(8,128)(2,1)S(1)}, u32[]{:S(2)}, u32[]{:S(2)}) collective-permute-start(bf16[128,640]{1,0:T(8,128)(2,1)S(1)} %bitcast.33), channel_id=1, source_target_pairs={{0,12},{4,0},{8,4},{12,8},{1,13},{5,1},{9,5},{13,9},{2,14},{6,2},{... | collective-permute-start | bytes 491528 | tf_op jit(solution)/shard_map/ppermute | solution.py:23
  9.2 1.0 %dynamic-slice_bitcast_fusion.2 = (bf16[16,8,640]{2,0,1:T(8,128)(2,1)S(1)}, bf16[16,8,640]{2,0,1:T(8,128)(2,1)S(1)}) fusion(bf16[8,64,640]{2,1,0:T(8,128)(2,1)S(1)} %copy-done.3, s32[]{:T(128)S(6)} %select_n.37, bf16[8,64,640]{2,1,0:T(8,128)(2,1)} %param.5), kind=kLoop, calls=%fused_computation.8 | loop fusion | bytes 655364 | tf_op jit(solution)/shard_map/transpose | solution.py:96
  10.8 0.8 %bias_of_rows.1.refs_9_ = f32[128,512]{1,0:T(8,128)S(1)} custom-call(f32[4,128]{1,0:T(4,128)S(1)} %pad.4.bias_ref), custom_call_target="tpu_custom_call" | custom-call | tf_op jit(solution)/shard_map/bias_of_rows/pallas_call | solution.py:103
  11.6 0.7 %constant_dynamic-slice_fusion.2 = (bf16[960,320]{1,0:T(8,128)(2,1)S(1)}, bf16[960,320]{1,0:T(8,128)(2,1)S(1)}) fusion(bf16[960,640]{1,0:T(8,128)(2,1)S(1)} %bitcast.29, s32[]{:T(128)S(6)} %select_n.35, s32[]{:T(128)S(6)} %select_n.34), kind=kLoop, calls=%fused_computation.16 | loop fusion | bytes 2457608 | tf_op jit(solution)/shard_map/dynamic_slice | solution.py:422
  12.4 6.0 %collective-permute-done.2.refs_4_ = bf16[128,640]{1,0:T(8,128)(2,1)S(1)} collective-permute-done((bf16[128,640]{1,0:T(8,128)(2,1)S(1)}, bf16[128,640]{1,0:T(8,128)(2,1)S(1)}, u32[]{:S(2)}, u32[]{:S(2)}) %collective-permute-start.2) | collective-permute-done | bytes 163872 | tf_op jit(solution)/shard_map/ppermute | solution.py:23
  18.4 0.5 collective-permute-start.5
  18.9 0.9 %collective-permute-done.3.refs_5_ = bf16[128,640]{1,0:T(8,128)(2,1)S(1)} collective-permute-done((bf16[128,640]{1,0:T(8,128)(2,1)S(1)}, bf16[128,640]{1,0:T(8,128)(2,1)S(1)}, u32[]{:S(2)}, u32[]{:S(2)}) %collective-permute-start.3) | collective-permute-done | bytes 163872 | tf_op jit(solution)/shard_map/ppermute | solution.py:23
  20.0 4.7 %attend.1 = (bf16[512,640]{1,0:T(8,128)(2,1)S(1)}, bf16[512,640]{1,0:T(8,128)(2,1)S(1)}, bf16[512,640]{1,0:T(8,128)(2,1)S(1)}, bf16[512,640]{1,0:T(8,128)(2,1)S(...) custom-call(bf16[128,640]{1,0:T(8,128)(2,1)S(1)} %bitcast.32, bf16[128,640]{1,0:T(8,128)(2,1)S(1)} %bitcast.31, ...), custom_call_target="tpu_custom_call" | custom-call | tf_op jit(solution)/shard_map/attend/pallas_call | solution.py:213
  24.7 0.3 collective-permute-start.6
  25.0 0.9 %weight_terms.2 = (f32[4,80,640]{2,1,0:T(8,128)S(1)}, bf16[4,80,640]{2,1,0:T(8,128)(2,1)S(1)}) custom-call(bf16[512,640]{1,0:T(8,128)(2,1)S(1)} %get-tuple-element.51.refs_0_, bf16[512,640]{1,0:T(8,128)(2,1)S(1)} %get-tuple-element.52.refs_1_, bf16[512,640]{1,0:T(8,128)(2,1)S(1)} %get-tuple-element.53.refs_2_), custom_call_target="tpu_custom_call" | custom-call | tf_op jit(solution)/shard_map/weight_terms/pallas_call | solution.py:269
  25.9 1.6 %collective-permute-start.7 = (bf16[4,80,640]{2,1,0:T(8,128)(2,1)S(1)}, bf16[4,80,640]{2,1,0:T(8,128)(2,1)S(1)}, u32[]{:S(2)}, u32[]{:S(2)}) collective-permute-start(bf16[4,80,640]{2,1,0:T(8,128)(2,1)S(1)} %get-tuple-element.54), channel_id=1, source_target_pairs={{0,2},{2,0},{1,3},{3,1},{4,6},{6,4},{5,7},{7,5},{8,10},{10,8},{9,1... | collective-permute-start | bytes 1228808 | tf_op jit(solution)/shard_map/ppermute | solution.py:23
  27.6 0.7 %weight_terms.3 = (f32[4,80,640]{2,1,0:T(8,128)S(1)}, bf16[4,80,640]{2,1,0:T(8,128)(2,1)S(1)}) custom-call(bf16[512,640]{1,0:T(8,128)(2,1)S(1)} %get-tuple-element.70.refs_0_, bf16[512,640]{1,0:T(8,128)(2,1)S(1)} %get-tuple-element.52.refs_1_), custom_call_target="tpu_custom_call" | custom-call | tf_op jit(solution)/shard_map/weight_terms/pallas_call | solution.py:269
  28.3 0.6 collective-permute-start.14
  28.9 3.7 %collective-permute-start.8 = (bf16[64,640]{1,0:T(8,128)(2,1)S(1)}, bf16[64,640]{1,0:T(8,128)(2,1)S(1)}, u32[]{:S(2)}, u32[]{:S(2)}) collective-permute-start(bf16[64,640]{1,0:T(8,128)(2,1)S(1)} %get-tuple-element.55), channel_id=1, source_target_pairs={{0,4},{4,8},{8,12},{12,0},{1,5},{5,9},{9,13},{13,1},{2,6},{6,10},{... | collective-permute-start | bytes 245768 | tf_op jit(solution)/shard_map/ppermute | solution.py:23
  32.6 1.9 %collective-permute-start.9 = (bf16[64,640]{1,0:T(8,128)(2,1)S(1)}, bf16[64,640]{1,0:T(8,128)(2,1)S(1)}, u32[]{:S(2)}, u32[]{:S(2)}) collective-permute-start(bf16[64,640]{1,0:T(8,128)(2,1)S(1)} %get-tuple-element.58), channel_id=1, source_target_pairs={{0,8},{4,12},{8,0},{12,4},{1,9},{5,13},{9,1},{13,5},{2,10},{6,14},... | collective-permute-start | bytes 245768 | tf_op jit(solution)/shard_map/ppermute | solution.py:23
  34.5 0.5 collective-permute-start.10
  35.0 3.3 %collective-permute-done.7.refs_0_ = bf16[4,80,640]{2,1,0:T(8,128)(2,1)S(1)} collective-permute-done((bf16[4,80,640]{2,1,0:T(8,128)(2,1)S(1)}, bf16[4,80,640]{2,1,0:T(8,128)(2,1)S(1)}, u32[]{:S(2)}, u32[]{:S(2)}) %collective-permute-start.7) | collective-permute-done | bytes 409632 | tf_op jit(solution)/shard_map/ppermute | solution.py:23
  38.3 1.8 %collective-permute-done.9.refs_2_ = bf16[64,640]{1,0:T(8,128)(2,1)S(1)} collective-permute-done((bf16[64,640]{1,0:T(8,128)(2,1)S(1)}, bf16[64,640]{1,0:T(8,128)(2,1)S(1)}, u32[]{:S(2)}, u32[]{:S(2)}) %collective-permute-start.9) | collective-permute-done | bytes 81952 | tf_op jit(solution)/shard_map/ppermute | solution.py:23
  40.5 2.0 %collective-permute-start.11 = (bf16[80,640]{1,0:T(8,128)(2,1)S(1)}, bf16[80,640]{1,0:T(8,128)(2,1)S(1)}, u32[]{:S(2)}, u32[]{:S(2)}) collective-permute-start(bf16[80,640]{1,0:T(8,128)(2,1)S(1)} %get-tuple-element.66), channel_id=1, source_target_pairs={{0,4},{4,8},{8,12},{12,0},{1,5},{5,9},{9,13},{13,1},{2,6},{6,10},{... | collective-permute-start | bytes 307208 | tf_op jit(solution)/shard_map/ppermute | solution.py:23
  42.5 1.6 %collective-permute-start.12 = (bf16[80,640]{1,0:T(8,128)(2,1)S(1)}, bf16[80,640]{1,0:T(8,128)(2,1)S(1)}, u32[]{:S(2)}, u32[]{:S(2)}) collective-permute-start(bf16[80,640]{1,0:T(8,128)(2,1)S(1)} %get-tuple-element.67), channel_id=1, source_target_pairs={{0,8},{4,12},{8,0},{12,4},{1,9},{5,13},{9,1},{13,5},{2,10},{6,14},... | collective-permute-start | bytes 307208 | tf_op jit(solution)/shard_map/ppermute | solution.py:23
  44.0 0.9 %collective-permute-start.13 = (bf16[80,640]{1,0:T(8,128)(2,1)S(1)}, bf16[80,640]{1,0:T(8,128)(2,1)S(1)}, u32[]{:S(2)}, u32[]{:S(2)}) collective-permute-start(bf16[80,640]{1,0:T(8,128)(2,1)S(1)} %get-tuple-element.68), channel_id=1, source_target_pairs={{0,12},{4,0},{8,4},{12,8},{1,13},{5,1},{9,5},{13,9},{2,14},{6,2},{... | collective-permute-start | bytes 307208 | tf_op jit(solution)/shard_map/ppermute | solution.py:23
  44.9 1.4 %collective-permute-done.14.refs_0_ = bf16[4,80,640]{2,1,0:T(8,128)(2,1)S(1)} collective-permute-done((bf16[4,80,640]{2,1,0:T(8,128)(2,1)S(1)}, bf16[4,80,640]{2,1,0:T(8,128)(2,1)S(1)}, u32[]{:S(2)}, u32[]{:S(2)}) %collective-permute-start.14) | collective-permute-done | bytes 409632 | tf_op jit(solution)/shard_map/ppermute | solution.py:23
  46.5 3.8 %collective-permute-start.15 = (bf16[80,640]{1,0:T(8,128)(2,1)S(1)}, bf16[80,640]{1,0:T(8,128)(2,1)S(1)}, u32[]{:S(2)}, u32[]{:S(2)}) collective-permute-start(bf16[80,640]{1,0:T(8,128)(2,1)S(1)} %get-tuple-element.74), channel_id=1, source_target_pairs={{0,4},{4,8},{8,12},{12,0},{1,5},{5,9},{9,13},{13,1},{2,6},{6,10},{... | collective-permute-start | bytes 307208 | tf_op jit(solution)/shard_map/ppermute | solution.py:23
  50.3 1.9 %collective-permute-start.16 = (bf16[80,640]{1,0:T(8,128)(2,1)S(1)}, bf16[80,640]{1,0:T(8,128)(2,1)S(1)}, u32[]{:S(2)}, u32[]{:S(2)}) collective-permute-start(bf16[80,640]{1,0:T(8,128)(2,1)S(1)} %get-tuple-element.75), channel_id=1, source_target_pairs={{0,8},{4,12},{8,0},{12,4},{1,9},{5,13},{9,1},{13,5},{2,10},{6,14},... | collective-permute-start | bytes 307208 | tf_op jit(solution)/shard_map/ppermute | solution.py:23
  52.1 0.6 collective-permute-start.17
  52.9 1.1 %place.1 = bf16[8,64,320]{2,1,0:T(8,128)(2,1)} custom-call(bf16[64,640]{1,0:T(8,128)(2,1)S(1)} %get-tuple-element.50.refs_0_, bf16[64,640]{1,0:T(8,128)(2,1)S(1)} %collective-permute-done.8.refs_1_, bf16[64,640]{1,0:T(8,128)(2,1)S(1)} %collective-permute-done.9.refs_2_, bf16[64,640]{1,0:T(8,128)(2,1)S(1)} %collective-permute-done.10.refs_3_, ...), custom_call_target="tpu_custom_call" | custom-call | tf_op jit(solution)/shard_map/place/pallas_call | solution.py:387
  54.0 1.3 %collective-permute-done.15.refs_5_ = bf16[80,640]{1,0:T(8,128)(2,1)S(1)} collective-permute-done((bf16[80,640]{1,0:T(8,128)(2,1)S(1)}, bf16[80,640]{1,0:T(8,128)(2,1)S(1)}, u32[]{:S(2)}, u32[]{:S(2)}) %collective-permute-start.15) | collective-permute-done | bytes 102432 | tf_op jit(solution)/shard_map/ppermute | solution.py:23
  55.3 4.7 %collective-permute-done.16.refs_6_ = bf16[80,640]{1,0:T(8,128)(2,1)S(1)} collective-permute-done((bf16[80,640]{1,0:T(8,128)(2,1)S(1)}, bf16[80,640]{1,0:T(8,128)(2,1)S(1)}, u32[]{:S(2)}, u32[]{:S(2)}) %collective-permute-start.16) | collective-permute-done | bytes 102432 | tf_op jit(solution)/shard_map/ppermute | solution.py:23
  60.0 0.9 %finish.1 = (f32[3,80,320]{2,1,0:T(8,128)}, f32[80,320]{1,0:T(8,128)}) custom-call(f32[80,640]{1,0:T(8,128)S(1)} %get-tuple-element.65.refs_0_, bf16[80,640]{1,0:T(8,128)(2,1)S(1)} %collective-permute-done.11.refs_1_, bf16[80,640]{1,0:T(8,128)(2,1)S(1)} %collective-permute-done.12.refs_2_, bf16[80,640]{1,0:T(8,128)(2,1)S(1)} %collective-permute-done.13.refs_3_, ...), custom_call_target="tpu_custom_call" | custom-call | tf_op jit(solution)/shard_map/finish/pallas_call | solution.py:348
  (39 shorter events, 1.9 us)
Async XLA Ops:
  0.6 10.0 %copy-start = (f32[8,63]{1,0:T(8,128)S(1)}, f32[8,63]{1,0:T(8,128)}, u32[]{:S(2)}) copy-start(f32[8,63]{1,0:T(8,128)} %param.9) | copy-start | bytes 6052
  1.8 7.3 %copy-start.3 = (bf16[8,64,640]{2,1,0:T(8,128)(2,1)S(1)}, bf16[8,64,640]{2,1,0:T(8,128)(2,1)}, u32[]{:S(2)}) copy-start(bf16[8,64,640]{2,1,0:T(8,128)(2,1)} %param.6) | copy-start | bytes 1966084
  2.0 10.3 %collective-permute-start = (bf16[128,640]{1,0:T(8,128)(2,1)S(1)}, bf16[128,640]{1,0:T(8,128)(2,1)S(1)}, u32[]{:S(2)}, u32[]{:S(2)}) collective-permute-start(bf16[128,640]{1,0:T(8,128)(2,1)S(1)} %bitcast.35), channel_id=1, source_target_pairs={{0,4},{4,8},{8,12},{12,0},{1,5},{5,9},{9,13},{13,1},{2,6},{6,10},{... | collective-permute-start | bytes 491528 | tf_op jit(solution)/shard_map/ppermute | solution.py:23
  5.0 6.6 %copy-start.1 = (bf16[640,3,320]{0,2,1:T(8,128)(2,1)S(1)}, bf16[640,3,320]{0,2,1:T(8,128)(2,1)}, u32[]{:S(2)}) copy-start(bf16[640,3,320]{0,2,1:T(8,128)(2,1)} %param.7) | copy-start | bytes 3686404
  5.1 13.3 %collective-permute-start.2 = (bf16[128,640]{1,0:T(8,128)(2,1)S(1)}, bf16[128,640]{1,0:T(8,128)(2,1)S(1)}, u32[]{:S(2)}, u32[]{:S(2)}) collective-permute-start(bf16[128,640]{1,0:T(8,128)(2,1)S(1)} %bitcast.34), channel_id=1, source_target_pairs={{0,8},{4,12},{8,0},{12,4},{1,9},{5,13},{9,1},{13,5},{2,10},{6,14},... | collective-permute-start | bytes 491528 | tf_op jit(solution)/shard_map/ppermute | solution.py:23
  7.8 10.6 %collective-permute-start.4 = (bf16[128,640]{1,0:T(8,128)(2,1)S(1)}, bf16[128,640]{1,0:T(8,128)(2,1)S(1)}, u32[]{:S(2)}, u32[]{:S(2)}) collective-permute-start(bf16[128,640]{1,0:T(8,128)(2,1)S(1)} %bitcast.33), channel_id=1, source_target_pairs={{0,12},{4,0},{8,4},{12,8},{1,13},{5,1},{9,5},{13,9},{2,14},{6,2},{... | collective-permute-start | bytes 491528 | tf_op jit(solution)/shard_map/ppermute | solution.py:23
  11.6 8.4 %copy-start.2 = (bf16[320,640]{1,0:T(8,128)(2,1)S(1)}, bf16[320,640]{1,0:T(8,128)(2,1)}, u32[]{:S(2)}) copy-start(bf16[320,640]{1,0:T(8,128)(2,1)} %refs_11_.1) | copy-start | bytes 1228804
  12.3 6.6 %collective-permute-start.1 = (bf16[128,640]{1,0:T(8,128)(2,1)S(1)}, bf16[128,640]{1,0:T(8,128)(2,1)S(1)}, u32[]{:S(2)}, u32[]{:S(2)}) collective-permute-start(bf16[128,640]{1,0:T(8,128)(2,1)S(1)} %collective-permute-done.refs_2_), channel_id=1, source_target_pairs={{0,1},{1,0},{2,3},{3,2},{4,5},{5,4},{6,7},{7,6},{8,9},{9,8},{10,11... | collective-permute-start | bytes 491528 | tf_op jit(solution)/shard_map/ppermute | solution.py:23
  18.4 1.4 %collective-permute-start.3 = (bf16[128,640]{1,0:T(8,128)(2,1)S(1)}, bf16[128,640]{1,0:T(8,128)(2,1)S(1)}, u32[]{:S(2)}, u32[]{:S(2)}) collective-permute-start(bf16[128,640]{1,0:T(8,128)(2,1)S(1)} %collective-permute-done.2.refs_4_), channel_id=1, source_target_pairs={{0,1},{1,0},{2,3},{3,2},{4,5},{5,4},{6,7},{7,6},{8,9},{9,8},{10,11... | collective-permute-start | bytes 491528 | tf_op jit(solution)/shard_map/ppermute | solution.py:23
  18.4 1.6 %collective-permute-start.5 = (bf16[128,640]{1,0:T(8,128)(2,1)S(1)}, bf16[128,640]{1,0:T(8,128)(2,1)S(1)}, u32[]{:S(2)}, u32[]{:S(2)}) collective-permute-start(bf16[128,640]{1,0:T(8,128)(2,1)S(1)} %collective-permute-done.4.refs_6_), channel_id=1, source_target_pairs={{0,1},{1,0},{2,3},{3,2},{4,5},{5,4},{6,7},{7,6},{8,9},{9,8},{10,11... | collective-permute-start | bytes 491528 | tf_op jit(solution)/shard_map/ppermute | solution.py:23
  24.7 2.8 %collective-permute-start.6 = (bf16[4,128,320]{2,1,0:T(8,128)(2,1)S(1)}, bf16[4,128,320]{2,1,0:T(8,128)(2,1)S(1)}, u32[]{:S(2)}, u32[]{:S(2)}) collective-permute-start(bf16[4,128,320]{2,1,0:T(8,128)(2,1)S(1)} %get-tuple-element.49), channel_id=1, source_target_pairs={{0,1},{1,0},{2,3},{3,2},{4,5},{5,4},{6,7},{7,6},{8,9},{9,8},{10,11... | collective-permute-start | bytes 983048 | tf_op jit(solution)/shard_map/ppermute | solution.py:23
  25.9 12.4 %collective-permute-start.7 = (bf16[4,80,640]{2,1,0:T(8,128)(2,1)S(1)}, bf16[4,80,640]{2,1,0:T(8,128)(2,1)S(1)}, u32[]{:S(2)}, u32[]{:S(2)}) collective-permute-start(bf16[4,80,640]{2,1,0:T(8,128)(2,1)S(1)} %get-tuple-element.54), channel_id=1, source_target_pairs={{0,2},{2,0},{1,3},{3,1},{4,6},{6,4},{5,7},{7,5},{8,10},{10,8},{9,1... | collective-permute-start | bytes 1228808 | tf_op jit(solution)/shard_map/ppermute | solution.py:23
  28.3 18.0 %collective-permute-start.14 = (bf16[4,80,640]{2,1,0:T(8,128)(2,1)S(1)}, bf16[4,80,640]{2,1,0:T(8,128)(2,1)S(1)}, u32[]{:S(2)}, u32[]{:S(2)}) collective-permute-start(bf16[4,80,640]{2,1,0:T(8,128)(2,1)S(1)} %get-tuple-element.72), channel_id=1, source_target_pairs={{0,2},{2,0},{1,3},{3,1},{4,6},{6,4},{5,7},{7,5},{8,10},{10,8},{9,1... | collective-permute-start | bytes 1228808 | tf_op jit(solution)/shard_map/ppermute | solution.py:23
  28.9 9.4 %collective-permute-start.8 = (bf16[64,640]{1,0:T(8,128)(2,1)S(1)}, bf16[64,640]{1,0:T(8,128)(2,1)S(1)}, u32[]{:S(2)}, u32[]{:S(2)}) collective-permute-start(bf16[64,640]{1,0:T(8,128)(2,1)S(1)} %get-tuple-element.55), channel_id=1, source_target_pairs={{0,4},{4,8},{8,12},{12,0},{1,5},{5,9},{9,13},{13,1},{2,6},{6,10},{... | collective-permute-start | bytes 245768 | tf_op jit(solution)/shard_map/ppermute | solution.py:23
  32.6 7.5 %collective-permute-start.9 = (bf16[64,640]{1,0:T(8,128)(2,1)S(1)}, bf16[64,640]{1,0:T(8,128)(2,1)S(1)}, u32[]{:S(2)}, u32[]{:S(2)}) collective-permute-start(bf16[64,640]{1,0:T(8,128)(2,1)S(1)} %get-tuple-element.58), channel_id=1, source_target_pairs={{0,8},{4,12},{8,0},{12,4},{1,9},{5,13},{9,1},{13,5},{2,10},{6,14},... | collective-permute-start | bytes 245768 | tf_op jit(solution)/shard_map/ppermute | solution.py:23
  34.5 5.9 %collective-permute-start.10 = (bf16[64,640]{1,0:T(8,128)(2,1)S(1)}, bf16[64,640]{1,0:T(8,128)(2,1)S(1)}, u32[]{:S(2)}, u32[]{:S(2)}) collective-permute-start(bf16[64,640]{1,0:T(8,128)(2,1)S(1)} %get-tuple-element.61), channel_id=1, source_target_pairs={{0,12},{4,0},{8,4},{12,8},{1,13},{5,1},{9,5},{13,9},{2,14},{6,2},{... | collective-permute-start | bytes 245768 | tf_op jit(solution)/shard_map/ppermute | solution.py:23
  40.5 11.6 %collective-permute-start.11 = (bf16[80,640]{1,0:T(8,128)(2,1)S(1)}, bf16[80,640]{1,0:T(8,128)(2,1)S(1)}, u32[]{:S(2)}, u32[]{:S(2)}) collective-permute-start(bf16[80,640]{1,0:T(8,128)(2,1)S(1)} %get-tuple-element.66), channel_id=1, source_target_pairs={{0,4},{4,8},{8,12},{12,0},{1,5},{5,9},{9,13},{13,1},{2,6},{6,10},{... | collective-permute-start | bytes 307208 | tf_op jit(solution)/shard_map/ppermute | solution.py:23
  42.5 11.5 %collective-permute-start.12 = (bf16[80,640]{1,0:T(8,128)(2,1)S(1)}, bf16[80,640]{1,0:T(8,128)(2,1)S(1)}, u32[]{:S(2)}, u32[]{:S(2)}) collective-permute-start(bf16[80,640]{1,0:T(8,128)(2,1)S(1)} %get-tuple-element.67), channel_id=1, source_target_pairs={{0,8},{4,12},{8,0},{12,4},{1,9},{5,13},{9,1},{13,5},{2,10},{6,14},... | collective-permute-start | bytes 307208 | tf_op jit(solution)/shard_map/ppermute | solution.py:23
  44.0 9.9 %collective-permute-start.13 = (bf16[80,640]{1,0:T(8,128)(2,1)S(1)}, bf16[80,640]{1,0:T(8,128)(2,1)S(1)}, u32[]{:S(2)}, u32[]{:S(2)}) collective-permute-start(bf16[80,640]{1,0:T(8,128)(2,1)S(1)} %get-tuple-element.68), channel_id=1, source_target_pairs={{0,12},{4,0},{8,4},{12,8},{1,13},{5,1},{9,5},{13,9},{2,14},{6,2},{... | collective-permute-start | bytes 307208 | tf_op jit(solution)/shard_map/ppermute | solution.py:23
  46.5 8.9 %collective-permute-start.15 = (bf16[80,640]{1,0:T(8,128)(2,1)S(1)}, bf16[80,640]{1,0:T(8,128)(2,1)S(1)}, u32[]{:S(2)}, u32[]{:S(2)}) collective-permute-start(bf16[80,640]{1,0:T(8,128)(2,1)S(1)} %get-tuple-element.74), channel_id=1, source_target_pairs={{0,4},{4,8},{8,12},{12,0},{1,5},{5,9},{9,13},{13,1},{2,6},{6,10},{... | collective-permute-start | bytes 307208 | tf_op jit(solution)/shard_map/ppermute | solution.py:23
  50.3 9.8 %collective-permute-start.16 = (bf16[80,640]{1,0:T(8,128)(2,1)S(1)}, bf16[80,640]{1,0:T(8,128)(2,1)S(1)}, u32[]{:S(2)}, u32[]{:S(2)}) collective-permute-start(bf16[80,640]{1,0:T(8,128)(2,1)S(1)} %get-tuple-element.75), channel_id=1, source_target_pairs={{0,8},{4,12},{8,0},{12,4},{1,9},{5,13},{9,1},{13,5},{2,10},{6,14},... | collective-permute-start | bytes 307208 | tf_op jit(solution)/shard_map/ppermute | solution.py:23
  52.1 7.9 %collective-permute-start.17 = (bf16[80,640]{1,0:T(8,128)(2,1)S(1)}, bf16[80,640]{1,0:T(8,128)(2,1)S(1)}, u32[]{:S(2)}, u32[]{:S(2)}) collective-permute-start(bf16[80,640]{1,0:T(8,128)(2,1)S(1)} %get-tuple-element.76), channel_id=1, source_target_pairs={{0,12},{4,0},{8,4},{12,8},{1,13},{5,1},{9,5},{13,9},{2,14},{6,2},{... | collective-permute-start | bytes 307208 | tf_op jit(solution)/shard_map/ppermute | solution.py:23

commit v7 on v5

--- a/solution.py
+++ b/solution.py
@@ -170,7 +170,7 @@
             ref[at : at + piece, :] = value[k * piece : (k + 1) * piece, :]
 
     starts = list(range(0, chunk, piece))
-    wide = 2
+    wide = 4
     for some in [starts[i : i + wide] for i in range(0, len(starts), wide)]:
         rows = [[rows_of(ref, at) for ref in (q_ref, k_ref, v_ref, g_ref)] for at in some]
         queries, grads = [stack(r[0]) for r in rows], [stack(r[3]) for r in rows]

time: 61.1 us -> 61 us (level)
  no operation moved by 1% of the time
where the time goes in v7:
time: 61 us; the launch traced here: 60.8 us
  starting transfers between devices  26.9 us (44%)
  waiting for transfers between devices  20.2 us (33%)
  Pallas kernels  9.22 us (15%)
  local copies, waits for them, and re-layouts  2.17 us (4%)
  other arithmetic  1.6 us (3%)
  between operations  0.84 us (1%)
    ppermute x18, starting transfers between devices, shift_send(): lax.ppermute(array, axis, [(i, (i + step) % size) for i in range(size)])  26.9 us
    ppermute x18, waiting for transfers between devices, shift_send(): lax.ppermute(array, axis, [(i, (i + step) % size) for i in range(size)])  20.2 us
    pallas_call x1, Pallas kernels, attend(): pl.pallas_call(functools.partial(attend_kernel, owners, heads), out_shape...  4.55 us
    pallas_call x2, Pallas kernels, weight_terms(): pl.pallas_call(functools.partial(weight_kernel, owners, sides, block, len...  1.59 us
  transfers between devices with their start and end apart: 18, of which 9 were waited for; matrix products, arithmetic and copies ran while one was open for 4% of the time, Pallas kernels for 6%

profile of v7, /device:TPU:0, one launch (start us, length us, event | category | flops | bytes accessed | tf_op | source)
XLA Modules:
  0.0 60.8 jit_solution(25236507809146019)
XLA Ops:
  0.7 1.2 %broadcast_select_fusion = bf16[8,64,640]{2,1,0:T(8,128)(2,1)S(1)} fusion(bf16[8,64,640]{2,1,0:T(8,128)(2,1)} %param.5, bf16[8,64,640]{2,1,0:T(8,128)(2,1)} %param.6, pred[]{:T(512)S(6)} %eq.3), kind=kLoop, calls=%fused_computation | loop fusion | flops 327680 | bytes 1966081 | tf_op jit(solution)/shard_map/jit(_where)/select_n | solution.py:90
  2.0 3.1 %collective-permute-start = (bf16[128,640]{1,0:T(8,128)(2,1)S(1)}, bf16[128,640]{1,0:T(8,128)(2,1)S(1)}, u32[]{:S(2)}, u32[]{:S(2)}) collective-permute-start(bf16[128,640]{1,0:T(8,128)(2,1)S(1)} %bitcast.35), channel_id=1, source_target_pairs={{0,4},{4,8},{8,12},{12,0},{1,5},{5,9},{9,13},{13,1},{2,6},{6,10},{... | collective-permute-start | bytes 491528 | tf_op jit(solution)/shard_map/ppermute | solution.py:23
  5.1 2.7 %collective-permute-start.2 = (bf16[128,640]{1,0:T(8,128)(2,1)S(1)}, bf16[128,640]{1,0:T(8,128)(2,1)S(1)}, u32[]{:S(2)}, u32[]{:S(2)}) collective-permute-start(bf16[128,640]{1,0:T(8,128)(2,1)S(1)} %bitcast.34), channel_id=1, source_target_pairs={{0,8},{4,12},{8,0},{12,4},{1,9},{5,13},{9,1},{13,5},{2,10},{6,14},... | collective-permute-start | bytes 491528 | tf_op jit(solution)/shard_map/ppermute | solution.py:23
  7.8 1.4 %collective-permute-start.4 = (bf16[128,640]{1,0:T(8,128)(2,1)S(1)}, bf16[128,640]{1,0:T(8,128)(2,1)S(1)}, u32[]{:S(2)}, u32[]{:S(2)}) collective-permute-start(bf16[128,640]{1,0:T(8,128)(2,1)S(1)} %bitcast.33), channel_id=1, source_target_pairs={{0,12},{4,0},{8,4},{12,8},{1,13},{5,1},{9,5},{13,9},{2,14},{6,2},{... | collective-permute-start | bytes 491528 | tf_op jit(solution)/shard_map/ppermute | solution.py:23
  9.6 1.0 %dynamic-slice_bitcast_fusion.3 = (bf16[16,8,640]{2,0,1:T(8,128)(2,1)S(1)}, bf16[16,8,640]{2,0,1:T(8,128)(2,1)S(1)}) fusion(bf16[8,64,640]{2,1,0:T(8,128)(2,1)S(1)} %copy-done.3, s32[]{:T(128)S(6)} %select_n.31, bf16[8,64,640]{2,1,0:T(8,128)(2,1)} %param.5), kind=kLoop, calls=%fused_computation.9 | loop fusion | bytes 655364 | tf_op jit(solution)/shard_map/transpose | solution.py:96
  10.6 0.7 %constant_dynamic-slice_fusion.2 = (bf16[960,320]{1,0:T(8,128)(2,1)S(1)}, bf16[960,320]{1,0:T(8,128)(2,1)S(1)}) fusion(bf16[960,640]{1,0:T(8,128)(2,1)S(1)} %bitcast.29, s32[]{:T(128)S(6)} %select_n.36, s32[]{:T(128)S(6)} %select_n.35), kind=kLoop, calls=%fused_computation.16 | loop fusion | bytes 2457608 | tf_op jit(solution)/shard_map/dynamic_slice | solution.py:422
  11.3 0.9 %collective-permute-done.refs_2_ = bf16[128,640]{1,0:T(8,128)(2,1)S(1)} collective-permute-done((bf16[128,640]{1,0:T(8,128)(2,1)S(1)}, bf16[128,640]{1,0:T(8,128)(2,1)S(1)}, u32[]{:S(2)}, u32[]{:S(2)}) %collective-permute-start) | collective-permute-done | bytes 163872 | tf_op jit(solution)/shard_map/ppermute | solution.py:23
  12.2 6.2 %collective-permute-done.2.refs_4_ = bf16[128,640]{1,0:T(8,128)(2,1)S(1)} collective-permute-done((bf16[128,640]{1,0:T(8,128)(2,1)S(1)}, bf16[128,640]{1,0:T(8,128)(2,1)S(1)}, u32[]{:S(2)}, u32[]{:S(2)}) %collective-permute-start.2) | collective-permute-done | bytes 163872 | tf_op jit(solution)/shard_map/ppermute | solution.py:23
  18.4 0.5 collective-permute-start.5
  19.0 0.8 %bias_of_rows.1.refs_9_ = f32[128,512]{1,0:T(8,128)S(1)} custom-call(f32[4,128]{1,0:T(4,128)S(1)} %pad.4.bias_ref), custom_call_target="tpu_custom_call" | custom-call | tf_op jit(solution)/shard_map/bias_of_rows/pallas_call | solution.py:103
  20.0 4.6 %attend.1 = (bf16[512,640]{1,0:T(8,128)(2,1)S(1)}, bf16[512,640]{1,0:T(8,128)(2,1)S(1)}, bf16[512,640]{1,0:T(8,128)(2,1)S(1)}, bf16[512,640]{1,0:T(8,128)(2,1)S(...) custom-call(bf16[128,640]{1,0:T(8,128)(2,1)S(1)} %bitcast.32, bf16[128,640]{1,0:T(8,128)(2,1)S(1)} %bitcast.31, ...), custom_call_target="tpu_custom_call" | custom-call | tf_op jit(solution)/shard_map/attend/pallas_call | solution.py:213
  24.6 0.4 collective-permute-start.6
  25.0 0.9 %weight_terms.2 = (f32[4,80,640]{2,1,0:T(8,128)S(1)}, bf16[4,80,640]{2,1,0:T(8,128)(2,1)S(1)}) custom-call(bf16[512,640]{1,0:T(8,128)(2,1)S(1)} %get-tuple-element.43.refs_0_, bf16[512,640]{1,0:T(8,128)(2,1)S(1)} %get-tuple-element.44.refs_1_, bf16[512,640]{1,0:T(8,128)(2,1)S(1)} %get-tuple-element.45.refs_2_), custom_call_target="tpu_custom_call" | custom-call | tf_op jit(solution)/shard_map/weight_terms/pallas_call | solution.py:269
  25.8 1.5 %collective-permute-start.7 = (bf16[4,80,640]{2,1,0:T(8,128)(2,1)S(1)}, bf16[4,80,640]{2,1,0:T(8,128)(2,1)S(1)}, u32[]{:S(2)}, u32[]{:S(2)}) collective-permute-start(bf16[4,80,640]{2,1,0:T(8,128)(2,1)S(1)} %get-tuple-element.46), channel_id=1, source_target_pairs={{0,2},{2,0},{1,3},{3,1},{4,6},{6,4},{5,7},{7,5},{8,10},{10,8},{9,1... | collective-permute-start | bytes 1228808 | tf_op jit(solution)/shard_map/ppermute | solution.py:23
  27.5 0.7 %weight_terms.3 = (f32[4,80,640]{2,1,0:T(8,128)S(1)}, bf16[4,80,640]{2,1,0:T(8,128)(2,1)S(1)}) custom-call(bf16[512,640]{1,0:T(8,128)(2,1)S(1)} %get-tuple-element.62.refs_0_, bf16[512,640]{1,0:T(8,128)(2,1)S(1)} %get-tuple-element.44.refs_1_), custom_call_target="tpu_custom_call" | custom-call | tf_op jit(solution)/shard_map/weight_terms/pallas_call | solution.py:269
  28.2 0.6 %collective-permute-start.14 = (bf16[4,80,640]{2,1,0:T(8,128)(2,1)S(1)}, bf16[4,80,640]{2,1,0:T(8,128)(2,1)S(1)}, u32[]{:S(2)}, u32[]{:S(2)}) collective-permute-start(bf16[4,80,640]{2,1,0:T(8,128)(2,1)S(1)} %get-tuple-element.64), channel_id=1, source_target_pairs={{0,2},{2,0},{1,3},{3,1},{4,6},{6,4},{5,7},{7,5},{8,10},{10,8},{9,1... | collective-permute-start | bytes 1228808 | tf_op jit(solution)/shard_map/ppermute | solution.py:23
  28.8 3.7 %collective-permute-start.8 = (bf16[64,640]{1,0:T(8,128)(2,1)S(1)}, bf16[64,640]{1,0:T(8,128)(2,1)S(1)}, u32[]{:S(2)}, u32[]{:S(2)}) collective-permute-start(bf16[64,640]{1,0:T(8,128)(2,1)S(1)} %get-tuple-element.47), channel_id=1, source_target_pairs={{0,4},{4,8},{8,12},{12,0},{1,5},{5,9},{9,13},{13,1},{2,6},{6,10},{... | collective-permute-start | bytes 245768 | tf_op jit(solution)/shard_map/ppermute | solution.py:23
  32.5 1.9 %collective-permute-start.9 = (bf16[64,640]{1,0:T(8,128)(2,1)S(1)}, bf16[64,640]{1,0:T(8,128)(2,1)S(1)}, u32[]{:S(2)}, u32[]{:S(2)}) collective-permute-start(bf16[64,640]{1,0:T(8,128)(2,1)S(1)} %get-tuple-element.50), channel_id=1, source_target_pairs={{0,8},{4,12},{8,0},{12,4},{1,9},{5,13},{9,1},{13,5},{2,10},{6,14},... | collective-permute-start | bytes 245768 | tf_op jit(solution)/shard_map/ppermute | solution.py:23
  34.5 0.4 collective-permute-start.10
  34.9 3.3 %collective-permute-done.7.refs_0_ = bf16[4,80,640]{2,1,0:T(8,128)(2,1)S(1)} collective-permute-done((bf16[4,80,640]{2,1,0:T(8,128)(2,1)S(1)}, bf16[4,80,640]{2,1,0:T(8,128)(2,1)S(1)}, u32[]{:S(2)}, u32[]{:S(2)}) %collective-permute-start.7) | collective-permute-done | bytes 409632 | tf_op jit(solution)/shard_map/ppermute | solution.py:23
  38.2 1.8 %collective-permute-done.9.refs_2_ = bf16[64,640]{1,0:T(8,128)(2,1)S(1)} collective-permute-done((bf16[64,640]{1,0:T(8,128)(2,1)S(1)}, bf16[64,640]{1,0:T(8,128)(2,1)S(1)}, u32[]{:S(2)}, u32[]{:S(2)}) %collective-permute-start.9) | collective-permute-done | bytes 81952 | tf_op jit(solution)/shard_map/ppermute | solution.py:23
  40.4 2.0 %collective-permute-start.11 = (bf16[80,640]{1,0:T(8,128)(2,1)S(1)}, bf16[80,640]{1,0:T(8,128)(2,1)S(1)}, u32[]{:S(2)}, u32[]{:S(2)}) collective-permute-start(bf16[80,640]{1,0:T(8,128)(2,1)S(1)} %get-tuple-element.58), channel_id=1, source_target_pairs={{0,4},{4,8},{8,12},{12,0},{1,5},{5,9},{9,13},{13,1},{2,6},{6,10},{... | collective-permute-start | bytes 307208 | tf_op jit(solution)/shard_map/ppermute | solution.py:23
  42.4 1.6 %collective-permute-start.12 = (bf16[80,640]{1,0:T(8,128)(2,1)S(1)}, bf16[80,640]{1,0:T(8,128)(2,1)S(1)}, u32[]{:S(2)}, u32[]{:S(2)}) collective-permute-start(bf16[80,640]{1,0:T(8,128)(2,1)S(1)} %get-tuple-element.59), channel_id=1, source_target_pairs={{0,8},{4,12},{8,0},{12,4},{1,9},{5,13},{9,1},{13,5},{2,10},{6,14},... | collective-permute-start | bytes 307208 | tf_op jit(solution)/shard_map/ppermute | solution.py:23
  44.0 0.9 %collective-permute-start.13 = (bf16[80,640]{1,0:T(8,128)(2,1)S(1)}, bf16[80,640]{1,0:T(8,128)(2,1)S(1)}, u32[]{:S(2)}, u32[]{:S(2)}) collective-permute-start(bf16[80,640]{1,0:T(8,128)(2,1)S(1)} %get-tuple-element.60), channel_id=1, source_target_pairs={{0,12},{4,0},{8,4},{12,8},{1,13},{5,1},{9,5},{13,9},{2,14},{6,2},{... | collective-permute-start | bytes 307208 | tf_op jit(solution)/shard_map/ppermute | solution.py:23
  44.8 1.4 %collective-permute-done.14.refs_0_ = bf16[4,80,640]{2,1,0:T(8,128)(2,1)S(1)} collective-permute-done((bf16[4,80,640]{2,1,0:T(8,128)(2,1)S(1)}, bf16[4,80,640]{2,1,0:T(8,128)(2,1)S(1)}, u32[]{:S(2)}, u32[]{:S(2)}) %collective-permute-start.14) | collective-permute-done | bytes 409632 | tf_op jit(solution)/shard_map/ppermute | solution.py:23
  46.4 3.8 %collective-permute-start.15 = (bf16[80,640]{1,0:T(8,128)(2,1)S(1)}, bf16[80,640]{1,0:T(8,128)(2,1)S(1)}, u32[]{:S(2)}, u32[]{:S(2)}) collective-permute-start(bf16[80,640]{1,0:T(8,128)(2,1)S(1)} %get-tuple-element.66), channel_id=1, source_target_pairs={{0,4},{4,8},{8,12},{12,0},{1,5},{5,9},{9,13},{13,1},{2,6},{6,10},{... | collective-permute-start | bytes 307208 | tf_op jit(solution)/shard_map/ppermute | solution.py:23
  50.2 1.9 %collective-permute-start.16 = (bf16[80,640]{1,0:T(8,128)(2,1)S(1)}, bf16[80,640]{1,0:T(8,128)(2,1)S(1)}, u32[]{:S(2)}, u32[]{:S(2)}) collective-permute-start(bf16[80,640]{1,0:T(8,128)(2,1)S(1)} %get-tuple-element.67), channel_id=1, source_target_pairs={{0,8},{4,12},{8,0},{12,4},{1,9},{5,13},{9,1},{13,5},{2,10},{6,14},... | collective-permute-start | bytes 307208 | tf_op jit(solution)/shard_map/ppermute | solution.py:23
  52.0 0.6 collective-permute-start.17
  52.8 1.1 %place.1 = bf16[8,64,320]{2,1,0:T(8,128)(2,1)} custom-call(bf16[64,640]{1,0:T(8,128)(2,1)S(1)} %get-tuple-element.42.refs_0_, bf16[64,640]{1,0:T(8,128)(2,1)S(1)} %collective-permute-done.8.refs_1_, bf16[64,640]{1,0:T(8,128)(2,1)S(1)} %collective-permute-done.9.refs_2_, bf16[64,640]{1,0:T(8,128)(2,1)S(1)} %collective-permute-done.10.refs_3_, ...), custom_call_target="tpu_custom_call" | custom-call | tf_op jit(solution)/shard_map/place/pallas_call | solution.py:387
  53.9 1.3 %collective-permute-done.15.refs_5_ = bf16[80,640]{1,0:T(8,128)(2,1)S(1)} collective-permute-done((bf16[80,640]{1,0:T(8,128)(2,1)S(1)}, bf16[80,640]{1,0:T(8,128)(2,1)S(1)}, u32[]{:S(2)}, u32[]{:S(2)}) %collective-permute-start.15) | collective-permute-done | bytes 102432 | tf_op jit(solution)/shard_map/ppermute | solution.py:23
  55.2 4.7 %collective-permute-done.16.refs_6_ = bf16[80,640]{1,0:T(8,128)(2,1)S(1)} collective-permute-done((bf16[80,640]{1,0:T(8,128)(2,1)S(1)}, bf16[80,640]{1,0:T(8,128)(2,1)S(1)}, u32[]{:S(2)}, u32[]{:S(2)}) %collective-permute-start.16) | collective-permute-done | bytes 102432 | tf_op jit(solution)/shard_map/ppermute | solution.py:23
  59.9 0.9 %finish.1 = (f32[3,80,320]{2,1,0:T(8,128)}, f32[80,320]{1,0:T(8,128)}) custom-call(f32[80,640]{1,0:T(8,128)S(1)} %get-tuple-element.57.refs_0_, bf16[80,640]{1,0:T(8,128)(2,1)S(1)} %collective-permute-done.11.refs_1_, bf16[80,640]{1,0:T(8,128)(2,1)S(1)} %collective-permute-done.12.refs_2_, bf16[80,640]{1,0:T(8,128)(2,1)S(1)} %collective-permute-done.13.refs_3_, ...), custom_call_target="tpu_custom_call" | custom-call | tf_op jit(solution)/shard_map/finish/pallas_call | solution.py:348
  (39 shorter events, 1.7 us)
Async XLA Ops:
  0.6 18.3 %copy-start = (f32[8,63]{1,0:T(8,128)S(1)}, f32[8,63]{1,0:T(8,128)}, u32[]{:S(2)}) copy-start(f32[8,63]{1,0:T(8,128)} %param.9) | copy-start | bytes 6052
  1.8 7.8 %copy-start.3 = (bf16[8,64,640]{2,1,0:T(8,128)(2,1)S(1)}, bf16[8,64,640]{2,1,0:T(8,128)(2,1)}, u32[]{:S(2)}) copy-start(bf16[8,64,640]{2,1,0:T(8,128)(2,1)} %param.6) | copy-start | bytes 1966084
  1.9 8.7 %copy-start.1 = (bf16[640,3,320]{0,2,1:T(8,128)(2,1)S(1)}, bf16[640,3,320]{0,2,1:T(8,128)(2,1)}, u32[]{:S(2)}) copy-start(bf16[640,3,320]{0,2,1:T(8,128)(2,1)} %param.7) | copy-start | bytes 3686404
  2.0 10.2 %collective-permute-start = (bf16[128,640]{1,0:T(8,128)(2,1)S(1)}, bf16[128,640]{1,0:T(8,128)(2,1)S(1)}, u32[]{:S(2)}, u32[]{:S(2)}) collective-permute-start(bf16[128,640]{1,0:T(8,128)(2,1)S(1)} %bitcast.35), channel_id=1, source_target_pairs={{0,4},{4,8},{8,12},{12,0},{1,5},{5,9},{9,13},{13,1},{2,6},{6,10},{... | collective-permute-start | bytes 491528 | tf_op jit(solution)/shard_map/ppermute | solution.py:23
  5.1 13.3 %collective-permute-start.2 = (bf16[128,640]{1,0:T(8,128)(2,1)S(1)}, bf16[128,640]{1,0:T(8,128)(2,1)S(1)}, u32[]{:S(2)}, u32[]{:S(2)}) collective-permute-start(bf16[128,640]{1,0:T(8,128)(2,1)S(1)} %bitcast.34), channel_id=1, source_target_pairs={{0,8},{4,12},{8,0},{12,4},{1,9},{5,13},{9,1},{13,5},{2,10},{6,14},... | collective-permute-start | bytes 491528 | tf_op jit(solution)/shard_map/ppermute | solution.py:23
  7.8 10.6 %collective-permute-start.4 = (bf16[128,640]{1,0:T(8,128)(2,1)S(1)}, bf16[128,640]{1,0:T(8,128)(2,1)S(1)}, u32[]{:S(2)}, u32[]{:S(2)}) collective-permute-start(bf16[128,640]{1,0:T(8,128)(2,1)S(1)} %bitcast.33), channel_id=1, source_target_pairs={{0,12},{4,0},{8,4},{12,8},{1,13},{5,1},{9,5},{13,9},{2,14},{6,2},{... | collective-permute-start | bytes 491528 | tf_op jit(solution)/shard_map/ppermute | solution.py:23
  11.3 8.8 %copy-start.2 = (bf16[320,640]{1,0:T(8,128)(2,1)S(1)}, bf16[320,640]{1,0:T(8,128)(2,1)}, u32[]{:S(2)}) copy-start(bf16[320,640]{1,0:T(8,128)(2,1)} %refs_11_.1) | copy-start | bytes 1228804
  12.2 7.7 %collective-permute-start.1 = (bf16[128,640]{1,0:T(8,128)(2,1)S(1)}, bf16[128,640]{1,0:T(8,128)(2,1)S(1)}, u32[]{:S(2)}, u32[]{:S(2)}) collective-permute-start(bf16[128,640]{1,0:T(8,128)(2,1)S(1)} %collective-permute-done.refs_2_), channel_id=1, source_target_pairs={{0,1},{1,0},{2,3},{3,2},{4,5},{5,4},{6,7},{7,6},{8,9},{9,8},{10,11... | collective-permute-start | bytes 491528 | tf_op jit(solution)/shard_map/ppermute | solution.py:23
  18.4 1.5 %collective-permute-start.3 = (bf16[128,640]{1,0:T(8,128)(2,1)S(1)}, bf16[128,640]{1,0:T(8,128)(2,1)S(1)}, u32[]{:S(2)}, u32[]{:S(2)}) collective-permute-start(bf16[128,640]{1,0:T(8,128)(2,1)S(1)} %collective-permute-done.2.refs_4_), channel_id=1, source_target_pairs={{0,1},{1,0},{2,3},{3,2},{4,5},{5,4},{6,7},{7,6},{8,9},{9,8},{10,11... | collective-permute-start | bytes 491528 | tf_op jit(solution)/shard_map/ppermute | solution.py:23
  18.4 1.6 %collective-permute-start.5 = (bf16[128,640]{1,0:T(8,128)(2,1)S(1)}, bf16[128,640]{1,0:T(8,128)(2,1)S(1)}, u32[]{:S(2)}, u32[]{:S(2)}) collective-permute-start(bf16[128,640]{1,0:T(8,128)(2,1)S(1)} %collective-permute-done.4.refs_6_), channel_id=1, source_target_pairs={{0,1},{1,0},{2,3},{3,2},{4,5},{5,4},{6,7},{7,6},{8,9},{9,8},{10,11... | collective-permute-start | bytes 491528 | tf_op jit(solution)/shard_map/ppermute | solution.py:23
  24.6 2.8 %collective-permute-start.6 = (bf16[4,128,320]{2,1,0:T(8,128)(2,1)S(1)}, bf16[4,128,320]{2,1,0:T(8,128)(2,1)S(1)}, u32[]{:S(2)}, u32[]{:S(2)}) collective-permute-start(bf16[4,128,320]{2,1,0:T(8,128)(2,1)S(1)} %get-tuple-element.41), channel_id=1, source_target_pairs={{0,1},{1,0},{2,3},{3,2},{4,5},{5,4},{6,7},{7,6},{8,9},{9,8},{10,11... | collective-permute-start | bytes 983048 | tf_op jit(solution)/shard_map/ppermute | solution.py:23
  25.8 12.4 %collective-permute-start.7 = (bf16[4,80,640]{2,1,0:T(8,128)(2,1)S(1)}, bf16[4,80,640]{2,1,0:T(8,128)(2,1)S(1)}, u32[]{:S(2)}, u32[]{:S(2)}) collective-permute-start(bf16[4,80,640]{2,1,0:T(8,128)(2,1)S(1)} %get-tuple-element.46), channel_id=1, source_target_pairs={{0,2},{2,0},{1,3},{3,1},{4,6},{6,4},{5,7},{7,5},{8,10},{10,8},{9,1... | collective-permute-start | bytes 1228808 | tf_op jit(solution)/shard_map/ppermute | solution.py:23
  28.2 18.0 %collective-permute-start.14 = (bf16[4,80,640]{2,1,0:T(8,128)(2,1)S(1)}, bf16[4,80,640]{2,1,0:T(8,128)(2,1)S(1)}, u32[]{:S(2)}, u32[]{:S(2)}) collective-permute-start(bf16[4,80,640]{2,1,0:T(8,128)(2,1)S(1)} %get-tuple-element.64), channel_id=1, source_target_pairs={{0,2},{2,0},{1,3},{3,1},{4,6},{6,4},{5,7},{7,5},{8,10},{10,8},{9,1... | collective-permute-start | bytes 1228808 | tf_op jit(solution)/shard_map/ppermute | solution.py:23
  28.8 9.4 %collective-permute-start.8 = (bf16[64,640]{1,0:T(8,128)(2,1)S(1)}, bf16[64,640]{1,0:T(8,128)(2,1)S(1)}, u32[]{:S(2)}, u32[]{:S(2)}) collective-permute-start(bf16[64,640]{1,0:T(8,128)(2,1)S(1)} %get-tuple-element.47), channel_id=1, source_target_pairs={{0,4},{4,8},{8,12},{12,0},{1,5},{5,9},{9,13},{13,1},{2,6},{6,10},{... | collective-permute-start | bytes 245768 | tf_op jit(solution)/shard_map/ppermute | solution.py:23
  32.5 7.5 %collective-permute-start.9 = (bf16[64,640]{1,0:T(8,128)(2,1)S(1)}, bf16[64,640]{1,0:T(8,128)(2,1)S(1)}, u32[]{:S(2)}, u32[]{:S(2)}) collective-permute-start(bf16[64,640]{1,0:T(8,128)(2,1)S(1)} %get-tuple-element.50), channel_id=1, source_target_pairs={{0,8},{4,12},{8,0},{12,4},{1,9},{5,13},{9,1},{13,5},{2,10},{6,14},... | collective-permute-start | bytes 245768 | tf_op jit(solution)/shard_map/ppermute | solution.py:23
  34.5 5.9 %collective-permute-start.10 = (bf16[64,640]{1,0:T(8,128)(2,1)S(1)}, bf16[64,640]{1,0:T(8,128)(2,1)S(1)}, u32[]{:S(2)}, u32[]{:S(2)}) collective-permute-start(bf16[64,640]{1,0:T(8,128)(2,1)S(1)} %get-tuple-element.53), channel_id=1, source_target_pairs={{0,12},{4,0},{8,4},{12,8},{1,13},{5,1},{9,5},{13,9},{2,14},{6,2},{... | collective-permute-start | bytes 245768 | tf_op jit(solution)/shard_map/ppermute | solution.py:23
  40.4 11.6 %collective-permute-start.11 = (bf16[80,640]{1,0:T(8,128)(2,1)S(1)}, bf16[80,640]{1,0:T(8,128)(2,1)S(1)}, u32[]{:S(2)}, u32[]{:S(2)}) collective-permute-start(bf16[80,640]{1,0:T(8,128)(2,1)S(1)} %get-tuple-element.58), channel_id=1, source_target_pairs={{0,4},{4,8},{8,12},{12,0},{1,5},{5,9},{9,13},{13,1},{2,6},{6,10},{... | collective-permute-start | bytes 307208 | tf_op jit(solution)/shard_map/ppermute | solution.py:23
  42.4 11.5 %collective-permute-start.12 = (bf16[80,640]{1,0:T(8,128)(2,1)S(1)}, bf16[80,640]{1,0:T(8,128)(2,1)S(1)}, u32[]{:S(2)}, u32[]{:S(2)}) collective-permute-start(bf16[80,640]{1,0:T(8,128)(2,1)S(1)} %get-tuple-element.59), channel_id=1, source_target_pairs={{0,8},{4,12},{8,0},{12,4},{1,9},{5,13},{9,1},{13,5},{2,10},{6,14},... | collective-permute-start | bytes 307208 | tf_op jit(solution)/shard_map/ppermute | solution.py:23
  44.0 9.9 %collective-permute-start.13 = (bf16[80,640]{1,0:T(8,128)(2,1)S(1)}, bf16[80,640]{1,0:T(8,128)(2,1)S(1)}, u32[]{:S(2)}, u32[]{:S(2)}) collective-permute-start(bf16[80,640]{1,0:T(8,128)(2,1)S(1)} %get-tuple-element.60), channel_id=1, source_target_pairs={{0,12},{4,0},{8,4},{12,8},{1,13},{5,1},{9,5},{13,9},{2,14},{6,2},{... | collective-permute-start | bytes 307208 | tf_op jit(solution)/shard_map/ppermute | solution.py:23
  46.4 8.9 %collective-permute-start.15 = (bf16[80,640]{1,0:T(8,128)(2,1)S(1)}, bf16[80,640]{1,0:T(8,128)(2,1)S(1)}, u32[]{:S(2)}, u32[]{:S(2)}) collective-permute-start(bf16[80,640]{1,0:T(8,128)(2,1)S(1)} %get-tuple-element.66), channel_id=1, source_target_pairs={{0,4},{4,8},{8,12},{12,0},{1,5},{5,9},{9,13},{13,1},{2,6},{6,10},{... | collective-permute-start | bytes 307208 | tf_op jit(solution)/shard_map/ppermute | solution.py:23
  50.2 9.8 %collective-permute-start.16 = (bf16[80,640]{1,0:T(8,128)(2,1)S(1)}, bf16[80,640]{1,0:T(8,128)(2,1)S(1)}, u32[]{:S(2)}, u32[]{:S(2)}) collective-permute-start(bf16[80,640]{1,0:T(8,128)(2,1)S(1)} %get-tuple-element.67), channel_id=1, source_target_pairs={{0,8},{4,12},{8,0},{12,4},{1,9},{5,13},{9,1},{13,5},{2,10},{6,14},... | collective-permute-start | bytes 307208 | tf_op jit(solution)/shard_map/ppermute | solution.py:23
  52.0 7.9 %collective-permute-start.17 = (bf16[80,640]{1,0:T(8,128)(2,1)S(1)}, bf16[80,640]{1,0:T(8,128)(2,1)S(1)}, u32[]{:S(2)}, u32[]{:S(2)}) collective-permute-start(bf16[80,640]{1,0:T(8,128)(2,1)S(1)} %get-tuple-element.68), channel_id=1, source_target_pairs={{0,12},{4,0},{8,4},{12,8},{1,13},{5,1},{9,5},{13,9},{2,14},{6,2},{... | collective-permute-start | bytes 307208 | tf_op jit(solution)/shard_map/ppermute | solution.py:23
